TPU v7x, 512 devices: a whole 4x4x16 slice. The times are simulated.
512 devices in a mesh: leaf: 8 (over x, core), row: 8 (over y, z_hi), col: 8 (over z_lo).
Axes of the slice: x: 4, y: 4, z: 16 (z_hi: 2, z_lo: 8; z = z_hi * 8 + z_lo), core: 2. Of those that a mesh axis runs over, the one named last changes fastest.
Arguments:
- child_front: float32 [8, 4096, 4096], P('leaf', 'row', 'col'), as said below
- parent_front: bfloat16 [8192, 32768], P('row', ('leaf', 'col')), as said below
- block_map: int32 [8, 30], replicated, may hold values from 0 to 63, as said below
Outputs:
- child_panel_t: float32 [8, 256, 4096], P('leaf', 'col', 'row')
- parent_panel_t: float32 [1024, 8192], P(('leaf', 'col'), 'row')
- parent_update: float32 [8192, 32768], P('row', ('leaf', 'col'))
Inputs may be any that keep to these rules, and one draw needn't show every extreme that they name: `child_front`: every child front is symmetric positive definite. `parent_front`: every parent front (each block of 8192 columns) is symmetric positive definite. `block_map`: in each row the entries are distinct. Of the contribution blocks that one device of a child's grid holds in its rows, at most 1 go to parent blocks whose rows one index of row holds; of those it holds in its columns, at most 1 go to parent blocks whose columns are held by one index of col, counting both leaves of the pair together; of all contribution blocks of one child, at most 4 go to parent blocks whose rows one index of row holds. All three bounds are reached.
All inputs are finite; a program needn't handle non-finite values.
Results may differ from a plain program's by a relative error of at most 0.0003.
Values sent between devices are 32-bit elements; how exact they have to be, the bound alone decides.
No kernel may reach another device: no remote copies, remote signals or barrier semaphores. Data moves between devices by JAX's collectives and lax.ppermute only.
A program may use at most 64 MiB of HBM per device.

v0:
```python
import jax
import jax.numpy as jnp
from jax import lax
from jax.sharding import PartitionSpec as P

BLK = 128


def from_partner(value, axis, bit):
    mask = 2**bit
    pairs = [(source, source ^ mask) for source in range(lax.axis_size(axis))]
    return lax.ppermute(value, axis, pairs)


def from_root(value, axis, source):
    kept = jnp.where(lax.axis_index(axis) == source, value, 0).astype(value.dtype)
    return lax.psum(kept, axis)


def pair_swap(values):
    return from_partner(values, "leaf", 0)


def one_hot(values, size):
    return (values[:, None] == jnp.arange(size)[None, :]).astype(jnp.float32)


def factor_panel(front_block, panel_width, row_start, col_start, paired):
    precise_setting = lax.Precision.HIGHEST
    panel_slab = from_root(front_block[:, :panel_width], "col", 0)
    if paired:
        partner = pair_swap(panel_slab)
        panel_slab = jnp.where(lax.axis_index("leaf") % 2 == 0, panel_slab, partner)
    block_cols = front_block.shape[1]
    joined = jnp.concatenate((front_block[:panel_width], panel_slab[:panel_width]), axis=1)
    joined = from_root(joined, "row", 0)
    top_block = joined[:, :block_cols]
    diagonal_block = joined[:, block_cols:]
    lower_factor = jnp.linalg.cholesky(diagonal_block)
    identity = jnp.eye(panel_width, dtype=jnp.float32)
    inverse_factor = jax.scipy.linalg.solve_triangular(lower_factor, identity, lower=True)
    rows_factor = jnp.dot(panel_slab, inverse_factor.T, precision=precise_setting)
    cols_factor = jnp.dot(inverse_factor, top_block, precision=precise_setting)
    update = jnp.dot(rows_factor, cols_factor, precision=precise_setting)
    row_ids = row_start + jnp.arange(front_block.shape[0])
    col_ids = col_start + jnp.arange(block_cols)
    keep_mask = (row_ids[:, None] >= panel_width) & (col_ids[None, :] >= panel_width)
    schur_part = jnp.where(keep_mask, front_block - update, jnp.float32(0.0))
    return (rows_factor, schur_part)


def shards(child_front, parent_front, block_map):
    leaf_id = lax.axis_index("leaf")
    row_id = lax.axis_index("row")
    col_id = lax.axis_index("col")
    row_count = lax.axis_size("row")
    col_count = lax.axis_size("col")
    precise_setting = lax.Precision.HIGHEST
    child_block = child_front[0]
    child_rows, child_cols = child_block.shape
    panel_width = child_cols // 2
    rows_factor, contribution = factor_panel(
        child_block, panel_width, row_id * child_rows, col_id * child_cols, False
    )
    out_width = panel_width // col_count
    child_out = lax.dynamic_slice_in_dim(rows_factor, col_id * out_width, out_width, 1).T[None]
    parent_rows, parent_cols = parent_front.shape
    parent_order = parent_rows * row_count
    row_span = parent_rows // BLK
    col_span = parent_cols // BLK
    row_blocks = child_rows // BLK
    col_blocks = child_cols // BLK
    cap_rows = max(1, row_blocks // row_count)
    cap_cols = max(1, col_blocks // col_count)
    own_map = lax.dynamic_index_in_dim(block_map, leaf_id, 0, keepdims=False)
    block_count = own_map.shape[0]
    block_ids = jnp.arange(block_count)
    global_ids = panel_width + block_ids * BLK
    src_row = global_ids // child_rows
    src_col = global_ids // child_cols
    dst_row = own_map // row_span
    owner_col = own_map // col_span
    dst_col = owner_col % col_count
    dst_half = owner_col // col_count
    earlier = block_ids[None, :] < block_ids[:, None]
    rank_row = jnp.sum(
        earlier & (src_row[None, :] == src_row[:, None]) & (dst_row[None, :] == dst_row[:, None]),
        axis=1,
    )
    rank_col = jnp.sum(
        earlier & (src_col[None, :] == src_col[:, None]) & (dst_col[None, :] == dst_col[:, None]),
        axis=1,
    )
    local_rows = (global_ids - row_id * child_rows) // BLK
    local_cols = (global_ids - col_id * child_cols) // BLK
    row_pick = jnp.einsum(
        "k,kd,ka,kx->dax",
        (src_row == row_id).astype(jnp.float32),
        one_hot(dst_row, row_count),
        one_hot(rank_row, cap_rows),
        one_hot(local_rows, row_blocks),
        precision=precise_setting,
    )
    col_pick = jnp.einsum(
        "k,ke,kj,ky->ejy",
        (src_col == col_id).astype(jnp.float32),
        one_hot(dst_col, col_count),
        one_hot(rank_col, cap_cols),
        one_hot(local_cols, col_blocks),
        precision=precise_setting,
    )
    place_cols = jnp.einsum(
        "k,kh,ky,kc,kj->hycj",
        (dst_col == col_id).astype(jnp.float32),
        one_hot(dst_half, 2),
        one_hot(own_map % col_span, col_span),
        one_hot(src_col, col_count),
        one_hot(rank_col, cap_cols),
        precision=precise_setting,
    )
    strip_view = contribution.reshape(row_blocks, BLK, child_cols)
    strips = jnp.einsum("dax,xiw->daiw", row_pick, strip_view, precision=precise_setting)
    received_blocks = lax.all_to_all(
        strips.reshape(row_count, cap_rows * BLK, child_cols),
        "row",
        split_axis=0,
        concat_axis=0,
        tiled=True,
    )
    received_blocks = received_blocks.reshape(row_count, cap_rows, BLK, child_cols)
    on_this_row = (dst_row == row_id).astype(jnp.float32)
    rank_dest = jnp.sum(earlier & (dst_row[None, :] == dst_row[:, None]), axis=1)
    cap_incoming = -(-block_count // row_count)
    dense_selection = jnp.einsum(
        "c,cn,cw,cp->nwp",
        on_this_row,
        one_hot(rank_dest, cap_incoming),
        one_hot(src_row, row_count),
        one_hot(rank_row, cap_rows),
        precision=precise_setting,
    )
    squeezed_result = jnp.einsum(
        "byx,yxhq->bhq", dense_selection, received_blocks, precision=precise_setting
    )
    squeezed_result = squeezed_result.reshape(cap_incoming, BLK, col_blocks, BLK)
    sending = jnp.einsum("miyb,ejy->emijb", squeezed_result, col_pick, precision=precise_setting)
    landed = lax.all_to_all(
        sending.reshape(col_count, cap_incoming * BLK, cap_cols * BLK),
        "col",
        split_axis=0,
        concat_axis=0,
        tiled=True,
    )
    landed = landed.reshape(col_count, cap_incoming, BLK, cap_cols, BLK)
    place_rows = jnp.einsum(
        "k,kx,km->xm",
        on_this_row,
        one_hot(own_map % row_span, row_span),
        one_hot(rank_dest, cap_incoming),
        precision=precise_setting,
    )
    placed_rows = jnp.einsum("xm,cmijb->xcijb", place_rows, landed, precision=precise_setting)
    halves = jnp.einsum(
        "xcijb,hycj->hxiyb", placed_rows, place_cols, precision=precise_setting
    ).reshape(2, parent_rows, parent_cols)
    own_half = leaf_id % 2
    own_part = lax.dynamic_index_in_dim(halves, own_half, 0, keepdims=False)
    other_part = lax.dynamic_index_in_dim(halves, 1 - own_half, 0, keepdims=False)
    assembled = parent_front.astype(jnp.float32) + own_part + pair_swap(other_part)
    parent_width = parent_cols // 2
    col_start = own_half * (parent_order // 2) + col_id * parent_cols
    parent_factor, parent_schur = factor_panel(
        assembled, parent_width, row_id * parent_rows, col_start, True
    )
    share_width = parent_width // (2 * col_count)
    share_start = (own_half * col_count + col_id) * share_width
    parent_out = lax.dynamic_slice_in_dim(parent_factor, share_start, share_width, 1).T
    return (child_out, parent_out, parent_schur)


def solution(mesh):
    placed = (P("leaf", "row", "col"), P("row", ("leaf", "col")), P())
    return jax.shard_map(
        shards,
        mesh=mesh,
        in_specs=placed,
        out_specs=(P("leaf", "col", "row"), P(("leaf", "col"), "row"), P("row", ("leaf", "col"))),
        check_vma=False,
    )
```

profile of v0, /device:TPU:6, one launch (start us, length us, event | category | flops | bytes accessed | tf_op | source)
XLA Modules:
  0.0 1079.2 jit_solution(1554957028383324433)
XLA Ops:
  7.2 1.6 copy.64
  10.5 128.7 %all-reduce.6.cloned.1.call-done = f32[512,256]{0,1:T(8,128)} async-done(((f32[512,256]{0,1:T(8,128)}), f32[512,256]{0,1:T(8,128)}) %all-reduce.6.cloned.1.call-update) | async-done | bytes 524304 | tf_op jit(solution)/shard_map/psum | solution.py:17
  141.8 207.1 %all-reduce.8.cloned.1.call-done = f32[256,768]{0,1:T(8,128)} async-done(((f32[256,768]{0,1:T(8,128)}), f32[256,768]{0,1:T(8,128)}) %all-reduce.8.cloned.1.call-update) | async-done | bytes 786448 | tf_op jit(solution)/shard_map/psum | solution.py:17
  349.9 1.0 fusion.23
  350.9 11.7 %cholesky.130 = f32[128,128]{1,0:T(8,128)S(1)} custom-call(f32[128,128]{1,0:T(8,128)S(1)} %cholesky.194), custom_call_target="Cholesky" | custom-call | tf_op jit(solution)/shard_map/jit(cholesky)/cholesky | solution.py:39
  362.7 9.8 custom-call.13
  373.0 11.7 %cholesky.147 = f32[128,128]{1,0:T(8,128)S(1)} custom-call(f32[128,128]{1,0:T(8,128)S(1)} %convolution_subtract_fusion.4), custom_call_target="Cholesky" | custom-call | tf_op jit(solution)/shard_map/jit(cholesky)/cholesky | solution.py:39
  386.8 4.2 while.4
  387.6 1.4 bitcast_dynamic-update-slice_fusion.4
  389.6 1.4 bitcast_dynamic-update-slice_fusion.4
  391.0 19.7 %custom-call.14 = f32[2,128,128]{1,2,0:T(8,128)S(1)} custom-call(f32[2,128,128]{2,1,0:T(8,128)S(1)} %get-tuple-element.19), custom_call_target="InvertDiagBlocksLowerTriangular" | custom-call | tf_op jit(solution)/shard_map/jit(_solve_triangular)/triangular_solve | solution.py:41
  413.1 1.2 fusion.15
  415.2 2.3 fusion.82
  417.5 2.5 copy.70
  420.0 8.9 all-to-all-start
  429.5 79.5 %all-to-all-done = f32[8,128,512]{2,1,0:T(8,128)S(1)} async-done(((f32[8,128,512]{2,1,0:T(8,128)}), f32[8,128,512]{2,1,0:T(8,128)S(1)}, u32[]{:S(2)}, u32[]{:S(2)}) %all-to-all-start) | async-done | bytes 2097184 | tf_op jit(solution)/shard_map/all_to_all | solution.py:123
  509.0 2.8 fusion.12
  512.1 2.8 fusion.16
  515.0 1.7 copy.74
  516.7 13.0 %all-to-all-start.1 = ((f32[8,512,128]{2,1,0:T(8,128)}), f32[8,512,128]{2,1,0:T(8,128)S(1)}, u32[]{:S(2)}, u32[]{:S(2)}) async-start(f32[8,512,128]{2,1,0:T(8,128)} %copy.74), calls=%async_computation.1 | async-start | bytes 4194304 | tf_op jit(solution)/shard_map/all_to_all | solution.py:147
  530.4 95.4 %all-to-all-done.1 = f32[8,512,128]{2,1,0:T(8,128)S(1)} async-done(((f32[8,512,128]{2,1,0:T(8,128)}), f32[8,512,128]{2,1,0:T(8,128)S(1)}, u32[]{:S(2)}, u32[]{:S(2)}) %all-to-all-start.1) | async-done | bytes 2097184 | tf_op jit(solution)/shard_map/all_to_all | solution.py:147
  625.7 5.9 fusion.9
  631.7 8.4 fusion.3
  640.0 5.5 reshape.323
  645.5 4.0 constant_dynamic-slice_fusion.3
  649.5 2.9 copy.88
  652.4 2.1 collective-permute-start
  654.6 1.5 copy.67
  656.1 1.8 copy.87
  658.8 2.8 fusion.8
  661.6 1.2 slice_select_fusion
  662.9 127.0 %all-reduce.10.cloned.1.call-done = f32[1024,256]{0,1:T(8,128)} async-done(((f32[1024,256]{0,1:T(8,128)}), f32[1024,256]{0,1:T(8,128)}) %all-reduce.10.cloned.1.call-update) | async-done | bytes 1048592 | tf_op jit(solution)/shard_map/psum | solution.py:17
  789.9 1.9 collective-permute-start.1
  791.8 2.8 collective-permute-done.1
  794.6 1.4 broadcast_select_fusion
  797.1 1.5 dynamic-slice_bitcast_fusion.1
  798.6 204.2 %all-reduce.12.cloned.1.call-done = f32[256,768]{0,1:T(8,128)} async-done(((f32[256,768]{0,1:T(8,128)}), f32[256,768]{0,1:T(8,128)}) %all-reduce.12.cloned.1.call-update) | async-done | bytes 786448 | tf_op jit(solution)/shard_map/psum | solution.py:17
  1003.9 1.0 fusion.22
  1004.9 11.7 %cholesky.164 = f32[128,128]{1,0:T(8,128)S(1)} custom-call(f32[128,128]{1,0:T(8,128)S(1)} %cholesky.197), custom_call_target="Cholesky" | custom-call | tf_op jit(solution)/shard_map/jit(cholesky)/cholesky | solution.py:39
  1016.7 9.8 custom-call.15
  1027.0 11.7 %cholesky.181 = f32[128,128]{1,0:T(8,128)S(1)} custom-call(f32[128,128]{1,0:T(8,128)S(1)} %convolution_subtract_fusion.3), custom_call_target="Cholesky" | custom-call | tf_op jit(solution)/shard_map/jit(cholesky)/cholesky | solution.py:39
  1041.2 4.0 while.5
  1042.1 1.3 bitcast_dynamic-update-slice_fusion.5
  1043.9 1.3 bitcast_dynamic-update-slice_fusion.5
  1045.2 19.7 %custom-call.16 = f32[2,128,128]{1,2,0:T(8,128)S(1)} custom-call(f32[2,128,128]{2,1,0:T(8,128)S(1)} %get-tuple-element.20), custom_call_target="InvertDiagBlocksLowerTriangular" | custom-call | tf_op jit(solution)/shard_map/jit(_solve_triangular)/triangular_solve | solution.py:41
  1065.8 1.1 fusion.25
  1068.2 2.2 subtract_select_fusion
  1070.4 1.8 copy.81
  (95 shorter events, 20.9 us)
Async XLA Ops:
  7.2 132.1 %all-reduce.6.cloned.1.call-start = ((), (), s32[]{:S(2)}) async-start(), calls=%async_computation.2 | async-start | bytes 1048576 | tf_op jit(solution)/shard_map/psum | solution.py:17
  9.6 339.2 %all-reduce.8.cloned.1.call-start = ((), (), s32[]{:S(2)}) async-start(), calls=%async_computation.3 | async-start | bytes 1572864 | tf_op jit(solution)/shard_map/psum | solution.py:17
  350.9 60.7 %copy-start.5 = (f32[512,256]{0,1:T(8,128)S(1)}, f32[512,256]{0,1:T(8,128)}, u32[]{:S(2)}) copy-start(f32[512,256]{0,1:T(8,128)} %all-reduce.6.cloned.1.call-done) | copy-start | bytes 1572868
  373.0 39.2 %copy-start.4 = (f32[256,768]{0,1:T(8,128)S(1)}, f32[256,768]{0,1:T(8,128)}, u32[]{:S(2)}) copy-start(f32[256,768]{0,1:T(8,128)} %all-reduce.8.cloned.1.call-done) | copy-start | bytes 2359300
  412.2 0.8 copy-start.2
  420.0 88.9 %all-to-all-start = ((f32[8,128,512]{2,1,0:T(8,128)}), f32[8,128,512]{2,1,0:T(8,128)S(1)}, u32[]{:S(2)}, u32[]{:S(2)}) async-start(f32[8,128,512]{2,1,0:T(8,128)} %copy.70), calls=%async_computation | async-start | bytes 4194304 | tf_op jit(solution)/shard_map/all_to_all | solution.py:123
  516.7 109.0 %all-to-all-start.1 = ((f32[8,512,128]{2,1,0:T(8,128)}), f32[8,512,128]{2,1,0:T(8,128)S(1)}, u32[]{:S(2)}, u32[]{:S(2)}) async-start(f32[8,512,128]{2,1,0:T(8,128)} %copy.74), calls=%async_computation.1 | async-start | bytes 4194304 | tf_op jit(solution)/shard_map/all_to_all | solution.py:147
  529.7 260.1 %all-reduce.10.cloned.1.call-start = ((), (), s32[]{:S(2)}) async-start(), calls=%async_computation.4 | async-start | bytes 2097152 | tf_op jit(solution)/shard_map/psum | solution.py:17
  652.4 6.4 collective-permute-start
  661.6 130.2 %copy-start = (f32[1024,512]{0,1:T(8,128)}, f32[1024,512]{0,1:T(8,128)S(1)}, u32[]{:S(2)}) copy-start(f32[1024,512]{0,1:T(8,128)S(1)} %fusion.8) | copy-start | bytes 6291460
  662.8 340.0 %all-reduce.12.cloned.1.call-start = ((), (), s32[]{:S(2)}) async-start(), calls=%async_computation.5 | async-start | bytes 1572864 | tf_op jit(solution)/shard_map/psum | solution.py:17
  789.9 4.8 collective-permute-start.1
  794.6 1.5 slice-start
  1041.2 26.3 %copy-start.3 = (f32[256,768]{0,1:T(8,128)S(1)}, f32[256,768]{0,1:T(8,128)}, u32[]{:S(2)}) copy-start(f32[256,768]{0,1:T(8,128)} %all-reduce.12.cloned.1.call-done) | copy-start | bytes 2359300
  1065.5 2.7 copy-start.1
Sparse Core Ops, SparseCore 0:
  11.5 127.7 all-reduce.5
  143.1 205.7 all-reduce.7
  662.9 126.8 all-reduce.9
  797.2 205.5 all-reduce.11
where the time goes:
time: 1090 us; the launch traced here: 1080 us
  waiting for transfers between devices  846 us (78%)
  other arithmetic  119 us (11%)
  local copies, waits for them, and re-layouts  37.9 us (3%)
  matrix products  32.4 us (3%)
  starting transfers between devices  26.2 us (2%)
  between operations  17.3 us (2%)
    psum x4, waiting for transfers between devices, from_root(): return lax.psum(kept, axis)  667 us
    all_to_all x1, waiting for transfers between devices, shards(): lax.all_to_all(sending.reshape(col_count, cap_incoming * BLK, cap_cols *...  95.4 us
    all_to_all x1, waiting for transfers between devices, shards(): lax.all_to_all(strips.reshape(row_count, cap_rows * BLK, child_cols), 'ro...  79.5 us
    another operation x13, other arithmetic, factor_panel(): lower_factor = jnp.linalg.cholesky(diagonal_block)  68.5 us
    another operation x5, other arithmetic, factor_panel(): jax.scipy.linalg.solve_triangular(lower_factor, identity, lower=True)  39.4 us
  transfers between devices with their start and end apart: 8, of which 8 were waited for; matrix products, arithmetic and copies ran while one was open for 1% of the time, Pallas kernels for 0%

commit v1 on v0

v1 whole, which is shorter than its diff:
```python
import functools

import jax
import jax.numpy as jnp
from jax import lax
from jax.experimental import pallas as pl
from jax.experimental.pallas import tpu as pltpu
from jax.sharding import PartitionSpec as P

BLK = 128
STEP = 32
HIGHEST = lax.Precision.HIGHEST


def send(value, axes, pairs):
    return lax.ppermute(value, axes, pairs)


def tree(value, axis, rounds):
    index = lax.axis_index(axis)
    for pairs in rounds:
        got = send(value, axis, pairs)
        is_target = functools.reduce(jnp.logical_or, [index == t for _, t in pairs])
        value = jnp.where(is_target, got, value)
    return value


HALVING = ([(0, 4)], [(0, 2), (4, 6)], [(0, 1), (2, 3), (4, 5), (6, 7)])


def inverse_factor_kernel(a_ref, out_ref, x_ref):
    order = a_ref.shape[0]
    x_ref[...] = a_ref[...]
    for start in range(0, order, STEP):
        stop = start + STEP
        rows = x_ref[start:stop, :]
        block = x_ref[start:stop, start:stop]
        sub = lax.broadcasted_iota(jnp.int32, (STEP, STEP), 0)
        lane = lax.broadcasted_iota(jnp.int32, (STEP, STEP), 1)
        eye = (sub == lane).astype(jnp.float32)
        work = jnp.concatenate([block, eye], axis=1)
        down = lax.broadcasted_iota(jnp.int32, (STEP, 1), 0)
        for k in range(STEP):
            row = work[k : k + 1, :]
            scaled = row / work[k : k + 1, k : k + 1]
            col = jnp.where(down > k, work[:, k : k + 1], 0.0)
            work = work - col * scaled
        pivots = jnp.sum(work[:, :STEP] * eye, axis=1, keepdims=True)
        inverse = work[:, STEP:] * lax.rsqrt(pivots)
        panel = jnp.dot(inverse, rows, precision=HIGHEST, preferred_element_type=jnp.float32)
        place = lax.broadcasted_iota(jnp.int32, (STEP, order), 1)
        pieces = [inverse]
        if start:
            pieces.insert(0, panel[:, :start])
        if stop < order:
            pieces.append(panel[:, stop:])
        panel = jnp.concatenate(pieces, axis=1)
        x_ref[start:stop, :] = panel
        if stop < order:
            upper = panel[:, stop:]
            change = lax.dot_general(
                upper, panel, (((0,), (0,)), ((), ())),
                precision=HIGHEST, preferred_element_type=jnp.float32,
            )
            old = x_ref[stop:, :]
            at = lax.broadcasted_iota(jnp.int32, old.shape, 1)
            old = jnp.where((at >= start) & (at < stop), 0.0, old)
            x_ref[stop:, :] = old - change
    full = x_ref[...]
    sub = lax.broadcasted_iota(jnp.int32, full.shape, 0)
    lane = lax.broadcasted_iota(jnp.int32, full.shape, 1)
    out_ref[...] = jnp.where(lane <= sub, full, 0.0)


def inverse_factor(block):
    return pl.pallas_call(
        inverse_factor_kernel,
        out_shape=jax.ShapeDtypeStruct(block.shape, jnp.float32),
        scratch_shapes=[pltpu.VMEM(block.shape, jnp.float32)],
        name="inverse_factor",
    )(block)


def smem():
    return pl.BlockSpec(memory_space=pltpu.SMEM)


def vmem():
    return pl.BlockSpec(memory_space=pltpu.VMEM)


def strips_kernel(sizes, ids_ref, map_ref, part_ref, out_ref):
    row_span, first, row_blocks = sizes
    row = ids_ref[1]
    for a in range(row_blocks):
        block = row * row_blocks + a - first

        @pl.when(block >= 0)
        def _():
            target = map_ref[jnp.maximum(block, 0)] // row_span
            out_ref[target] = part_ref[a * BLK : (a + 1) * BLK, :]


def tiles_kernel(sizes, ids_ref, map_ref, got_ref, out_ref):
    row_span, col_span, first, row_blocks, col_blocks, cols, count = sizes
    row, col = ids_ref[1], ids_ref[2]

    def body(k, rank):
        here = map_ref[k] // row_span == row

        @pl.when(here)
        def _():
            source = (k + first) // row_blocks
            slot = jnp.minimum(rank, out_ref.shape[1] - 1)
            for y in range(col_blocks):
                block = col * col_blocks + y - first

                @pl.when(block >= 0)
                def _():
                    target = (map_ref[jnp.maximum(block, 0)] // col_span) % cols
                    out_ref[target, slot] = got_ref[source, :, y * BLK : (y + 1) * BLK]

        return rank + here.astype(jnp.int32)

    lax.fori_loop(0, count, body, jnp.int32(0))


def place_kernel(sizes, ids_ref, map_ref, landed_ref, parent_ref, out_ref, other_ref):
    row_span, col_span, first, col_blocks, cols, count = sizes
    half, row, col = ids_ref[0], ids_ref[1], ids_ref[2]
    out_ref[...] = parent_ref[...].astype(jnp.float32)
    other_ref[...] = jnp.zeros_like(other_ref)

    def row_body(k, rank):
        here = map_ref[k] // row_span == row

        @pl.when(here)
        def _():
            slot = jnp.minimum(rank, landed_ref.shape[1] - 1)
            at_row = pl.multiple_of((map_ref[k] % row_span) * BLK, BLK)

            def col_body(j, carry):
                owner = map_ref[j] // col_span
                source = (j + first) // col_blocks
                at = map_ref[j] % col_span

                @pl.when((owner % cols == col) & (owner // cols == half))
                def _():
                    spot = (pl.ds(at_row, BLK), pl.ds(pl.multiple_of(at * BLK, BLK), BLK))
                    out_ref[spot] = out_ref[spot] + landed_ref[source, slot]

                @pl.when((owner % cols == col) & (owner // cols != half))
                def _():
                    other_ref[slot, at] = landed_ref[source, slot]

                return carry

            lax.fori_loop(0, count, col_body, jnp.int32(0))

        return rank + here.astype(jnp.int32)

    lax.fori_loop(0, count, row_body, jnp.int32(0))


def merge_kernel(sizes, ids_ref, map_ref, other_ref, base_ref, out_ref):
    row_span, col_span, count = sizes
    row = ids_ref[1]
    out_ref[...] = base_ref[...]

    def row_body(k, rank):
        here = map_ref[k] // row_span == row

        @pl.when(here)
        def _():
            slot = jnp.minimum(rank, other_ref.shape[0] - 1)
            at_row = pl.multiple_of((map_ref[k] % row_span) * BLK, BLK)
            for at in range(col_span):
                spot = (pl.ds(at_row, BLK), slice(at * BLK, (at + 1) * BLK))
                out_ref[spot] = out_ref[spot] + other_ref[slot, at]

        return rank + here.astype(jnp.int32)

    lax.fori_loop(0, count, row_body, jnp.int32(0))


def shards(child_front, parent_front, block_map):
    leaf_id = lax.axis_index("leaf")
    row_id = lax.axis_index("row")
    col_id = lax.axis_index("col")
    row_count = lax.axis_size("row")
    col_count = lax.axis_size("col")
    leaf_count = lax.axis_size("leaf")
    half_id = leaf_id % 2
    ids = jnp.stack([half_id, row_id, col_id]).astype(jnp.int32)
    own_map = lax.dynamic_index_in_dim(block_map, leaf_id, 0, keepdims=False)
    partner_map = lax.dynamic_index_in_dim(block_map, leaf_id ^ 1, 0, keepdims=False)
    count = own_map.shape[0]

    child_block = child_front[0]
    child_rows, child_cols = child_block.shape
    width = child_cols // 2
    parent_rows, parent_cols = parent_front.shape
    row_span, col_span = parent_rows // BLK, parent_cols // BLK
    row_blocks, col_blocks = child_rows // BLK, child_cols // BLK
    first = width // BLK
    cap = -(-count // row_count)
    swap = [(i, i ^ 1) for i in range(leaf_count)]

    diagonal = child_block[:width, :width]
    spread = [send(diagonal, ("row", "col"), [(0, r * col_count)]) for r in range(1, row_count)]
    diagonal = jnp.where(row_id == 0, diagonal, functools.reduce(jnp.add, spread))
    diagonal = tree(diagonal, "col", HALVING)
    slab = tree(child_block[:, :width], "col", HALVING)
    top = tree(child_block[:width], "row", HALVING)
    inverse = inverse_factor(diagonal)
    rows_factor = lax.dot_general(slab, inverse, (((1,), (1,)), ((), ())), precision=HIGHEST)
    cols_factor = jnp.dot(inverse, top, precision=HIGHEST)
    contribution = child_block - jnp.dot(rows_factor, cols_factor, precision=HIGHEST)
    out_width = width // col_count
    child_out = lax.dynamic_slice_in_dim(rows_factor, col_id * out_width, out_width, 1).T[None]

    strips = pl.pallas_call(
        functools.partial(strips_kernel, (row_span, first, row_blocks)),
        out_shape=jax.ShapeDtypeStruct((row_count, BLK, child_cols), jnp.float32),
        in_specs=[smem(), smem(), vmem()],
        out_specs=vmem(),
        name="strips",
    )(ids, own_map, contribution)
    got = lax.all_to_all(strips, "row", 0, 0, tiled=True)
    tiles = pl.pallas_call(
        functools.partial(
            tiles_kernel, (row_span, col_span, first, row_blocks, col_blocks, col_count, count)
        ),
        out_shape=jax.ShapeDtypeStruct((col_count, cap, BLK, BLK), jnp.float32),
        in_specs=[smem(), smem(), vmem()],
        out_specs=vmem(),
        name="tiles",
    )(ids, own_map, got)
    landed = lax.all_to_all(
        tiles.reshape(col_count, cap * BLK, BLK), "col", 0, 0, tiled=True
    ).reshape(tiles.shape)
    assembled, other = pl.pallas_call(
        functools.partial(place_kernel, (row_span, col_span, first, col_blocks, col_count, count)),
        out_shape=(
            jax.ShapeDtypeStruct(parent_front.shape, jnp.float32),
            jax.ShapeDtypeStruct((cap, col_span, BLK, BLK), jnp.float32),
        ),
        in_specs=[smem(), smem(), vmem(), vmem()],
        out_specs=(vmem(), vmem()),
        name="place",
    )(ids, own_map, landed, parent_front)
    other = send(other.reshape(cap * col_span * BLK, BLK), "leaf", swap).reshape(other.shape)
    assembled = pl.pallas_call(
        functools.partial(merge_kernel, (row_span, col_span, count)),
        out_shape=jax.ShapeDtypeStruct(parent_front.shape, jnp.float32),
        in_specs=[smem(), smem(), vmem(), vmem()],
        out_specs=vmem(),
        name="merge",
    )(ids, partner_map, other, assembled)

    parent_order = parent_rows * row_count
    parent_width = parent_cols // 2
    diagonal = assembled[:parent_width, :parent_width]
    even = range(0, leaf_count, 2)
    grid = row_count * col_count
    spread = [
        send(diagonal, ("leaf", "row", "col"), [(l * grid, l * grid + r * col_count) for l in even])
        for r in range(1, row_count)
    ]
    diagonal = jnp.where(row_id == 0, diagonal, functools.reduce(jnp.add, spread))
    across = [(l, l + 1) for l in even]
    diagonal = jnp.where(half_id == 0, diagonal, send(diagonal, "leaf", across))
    diagonal = tree(diagonal, "col", HALVING)
    slab = assembled[:, :parent_width]
    for pairs in HALVING:
        moves = [(l * col_count + s, l * col_count + t) for l in even for s, t in pairs]
        moved = send(slab, ("leaf", "col"), moves)
        is_target = functools.reduce(jnp.logical_or, [col_id == t for _, t in pairs])
        slab = jnp.where(is_target, moved, slab)
    slab = jnp.where(half_id == 0, slab, send(slab, "leaf", across))
    top = tree(assembled[:parent_width], "row", HALVING)
    inverse = inverse_factor(diagonal)
    rows_factor = lax.dot_general(slab, inverse, (((1,), (1,)), ((), ())), precision=HIGHEST)
    cols_factor = jnp.dot(inverse, top, precision=HIGHEST)
    update = jnp.dot(rows_factor, cols_factor, precision=HIGHEST)
    row_ids = row_id * parent_rows + jnp.arange(parent_rows)
    col_ids = half_id * (parent_order // 2) + col_id * parent_cols + jnp.arange(parent_cols)
    keep = (row_ids[:, None] >= parent_width) & (col_ids[None, :] >= parent_width)
    parent_schur = jnp.where(keep, assembled - update, jnp.float32(0.0))
    share = parent_width // (2 * col_count)
    start = (half_id * col_count + col_id) * share
    parent_out = lax.dynamic_slice_in_dim(rows_factor, start, share, 1).T
    return (child_out, parent_out, parent_schur)


def solution(mesh):
    placed = (P("leaf", "row", "col"), P("row", ("leaf", "col")), P())
    return jax.shard_map(
        shards,
        mesh=mesh,
        in_specs=placed,
        out_specs=(P("leaf", "col", "row"), P(("leaf", "col"), "row"), P("row", ("leaf", "col"))),
        check_vma=False,
    )
```

time: 1090 us -> 530 us (0.49)
  the two profiles are of different devices: /device:TPU:6 before, /device:TPU:224 now
where the time goes in v1:
time: 530 us; the launch traced here: 529 us
  blocking collectives  221 us (42%)
  waiting for transfers between devices  146 us (28%)
  Pallas kernels  75.8 us (14%)
  starting transfers between devices  49 us (9%)
  matrix products  12.8 us (2%)
  local copies, waits for them, and re-layouts  11.7 us (2%)
  other arithmetic  11 us (2%)
    all_to_all x1, blocking collectives, shards(): lax.all_to_all(tiles.reshape(col_count, cap * BLK, BLK), 'col', 0, 0, til...  166 us
    ppermute x35, waiting for transfers between devices, send(): return lax.ppermute(value, axes, pairs)  146 us
    pallas_call x2, Pallas kernels, inverse_factor(): pl.pallas_call(inverse_factor_kernel, out_shape=jax.ShapeDtypeStruct(bloc...  56.8 us
    all_to_all x1, blocking collectives, shards(): got = lax.all_to_all(strips, 'row', 0, 0, tiled=True)  54.8 us
    ppermute x35, starting transfers between devices, send(): return lax.ppermute(value, axes, pairs)  49 us
  transfers between devices with their start and end apart: 35, of which 8 were waited for; matrix products, arithmetic and copies ran while one was open for 4% of the time, Pallas kernels for 11%

profile of v1, /device:TPU:224, one launch (start us, length us, event | category | flops | bytes accessed | tf_op | source)
XLA Modules:
  0.0 528.8 jit_solution(4424426457099749691)
XLA Ops:
  0.6 1.8 slice.29
  5.1 1.4 collective-permute-start.5
  7.2 1.4 collective-permute-start.4
  13.9 5.9 %collective-permute-start.13 = (f32[256,512]{1,0:T(8,128)}, f32[256,512]{1,0:T(8,128)}, u32[]{:S(2)}, u32[]{:S(2)}) collective-permute-start(f32[256,512]{1,0:T(8,128)} %slice_bitcast_fusion), channel_id=1, source_target_pairs={{0,32},{1,33},{2,34},{3,35},{4,36},{5,37},{6,38},{7,39},{64,96},{6... | collective-permute-start | bytes 1572872 | tf_op jit(solution)/shard_map/ppermute | solution.py:16
  19.9 1.4 collective-permute-start.11
  22.0 8.5 %collective-permute-done.13 = f32[256,512]{1,0:T(8,128)} collective-permute-done((f32[256,512]{1,0:T(8,128)}, f32[256,512]{1,0:T(8,128)}, u32[]{:S(2)}, u32[]{:S(2)}) %collective-permute-start.13) | collective-permute-done | bytes 524320 | tf_op jit(solution)/shard_map/ppermute | solution.py:16
  30.6 2.1 collective-permute-start.14
  36.7 5.8 %collective-permute-done.14 = f32[256,512]{1,0:T(8,128)} collective-permute-done((f32[256,512]{1,0:T(8,128)S(1)}, f32[256,512]{1,0:T(8,128)}, u32[]{:S(2)}, u32[]{:S(2)}) %collective-permute-start.14) | collective-permute-done | bytes 524320 | tf_op jit(solution)/shard_map/ppermute | solution.py:16
  42.6 1.3 collective-permute-start.15
  44.6 29.8 %collective-permute-done.12 = f32[256,256]{1,0:T(8,128)} collective-permute-done((f32[256,256]{1,0:T(8,128)S(1)}, f32[256,256]{1,0:T(8,128)}, u32[]{:S(2)}, u32[]{:S(2)}) %collective-permute-start.12) | collective-permute-done | bytes 262176 | tf_op jit(solution)/shard_map/ppermute | solution.py:16
  74.3 1.7 broadcast_select_fusion.15.a_ref
  76.0 28.4 %inverse_factor.2 = f32[256,256]{1,0:T(8,128)} custom-call(f32[256,256]{1,0:T(8,128)} %broadcast_select_fusion.15.a_ref), custom_call_target="tpu_custom_call" | custom-call | tf_op jit(solution)/shard_map/inverse_factor/pallas_call | solution.py:76
  104.4 12.5 %collective-permute-done.2 = f32[512,256]{1,0:T(8,128)S(1)} collective-permute-done((f32[512,256]{1,0:T(8,128)S(1)}, f32[512,256]{1,0:T(8,128)S(1)}, u32[]{:S(2)}, u32[]{:S(2)}) %collective-permute-start.2) | collective-permute-done | bytes 524320 | tf_op jit(solution)/shard_map/ppermute | solution.py:16
  116.9 1.6 fusion.6
  118.5 1.8 fusion.4
  120.3 2.0 convolution_subtract_fusion.part_ref
  122.3 2.6 strips.1
  125.0 54.8 %all_to_all.10.got_ref = f32[8,128,512]{2,1,0:T(8,128)} all-to-all(f32[8,128,512]{2,1,0:T(8,128)} %strips.1), channel_id=1, replica_groups=mesh['leaf'=8,'row'=8,'col'=8] {'row'}, dimensions={0} | all-to-all | bytes 4194304 | tf_op jit(solution)/shard_map/all_to_all | solution.py:229
  179.8 3.9 tiles.1
  183.7 166.4 %all_to_all.11 = f32[8,512,128]{2,1,0:T(8,128)} all-to-all(f32[8,512,128]{2,1,0:T(8,128)} %bitcast.35), channel_id=1, replica_groups=mesh['leaf'=8,'row'=8,'col'=8] {'col'}, dimensions={0} | all-to-all | bytes 4194304 | tf_op jit(solution)/shard_map/all_to_all | solution.py:239
  350.1 8.4 %place.1 = (f32[1024,512]{1,0:T(8,128)}, f32[4,4,128,128]{3,2,1,0:T(8,128)}) custom-call(s32[3]{0:T(128)} %pad_add_fusion.ids_ref, s32[30]{0:T(128)} %get-tuple-element.7.map_ref, f32[8,4,128,128]{3,2,1,0:T(8,128)} %bitcast.36, bf16[1024,512]{1,0:T(8,128)(2,1)} %parent_ref.1), custom_call_target="tpu_custom_call" | custom-call | tf_op jit(solution)/shard_map/place/pallas_call | solution.py:242
  358.5 1.9 collective-permute-start.16
  360.4 2.8 collective-permute-done.16
  364.2 4.2 merge.1
  368.4 1.4 slice.30
  370.8 1.7 collective-permute-start.18
  373.8 1.4 collective-permute-start.26
  375.2 1.4 collective-permute-start.25
  376.6 1.4 collective-permute-start.24
  378.0 1.4 collective-permute-start.23
  379.3 1.5 collective-permute-start.21
  380.8 1.4 collective-permute-start.22
  383.0 2.7 collective-permute-start.32
  385.7 1.5 add_select_fusion
  387.2 2.0 collective-permute-start.28
  393.1 3.8 collective-permute-done.32
  397.0 1.3 collective-permute-start.33
  399.7 33.8 %collective-permute-done.19 = f32[1024,256]{1,0:T(8,128)} collective-permute-done((f32[1024,256]{1,0:T(8,128)}, f32[1024,256]{1,0:T(8,128)}, u32[]{:S(2)}, u32[]{:S(2)}) %collective-permute-start.19) | collective-permute-done | bytes 1048608 | tf_op jit(solution)/shard_map/ppermute | solution.py:16
  433.5 1.4 broadcast_select_fusion.2
  434.9 2.3 collective-permute-start.20
  438.1 2.1 collective-permute-start.34
  440.1 1.5 dynamic-slice_bitcast_fusion.1
  441.6 49.1 %collective-permute-done.31 = f32[256,256]{1,0:T(8,128)} collective-permute-done((f32[256,256]{1,0:T(8,128)S(1)}, f32[256,256]{1,0:T(8,128)}, u32[]{:S(2)}, u32[]{:S(2)}) %collective-permute-start.31) | collective-permute-done | bytes 262176 | tf_op jit(solution)/shard_map/ppermute | solution.py:16
  490.7 1.7 broadcast_select_fusion.14.a_ref
  492.4 28.4 %inverse_factor.3 = f32[256,256]{1,0:T(8,128)} custom-call(f32[256,256]{1,0:T(8,128)} %broadcast_select_fusion.14.a_ref), custom_call_target="tpu_custom_call" | custom-call | tf_op jit(solution)/shard_map/inverse_factor/pallas_call | solution.py:76
  520.8 1.7 fusion.2
  522.5 2.1 fusion
  525.3 3.6 subtract_select_fusion
  (76 shorter events, 25.2 us)
Async XLA Ops:
  0.6 12.5 %copy-start.1 = (f32[1,512,512]{2,1,0:T(8,128)S(1)}, f32[1,512,512]{2,1,0:T(8,128)}, u32[]{:S(2)}) copy-start(f32[1,512,512]{2,1,0:T(8,128)} %param.3) | copy-start | bytes 3145732
  2.4 4.1 collective-permute-start.9
  3.1 4.1 collective-permute-start.8
  3.8 5.9 %collective-permute-start.7 = (f32[256,256]{1,0:T(8,128)}, f32[256,256]{1,0:T(8,128)S(1)}, u32[]{:S(2)}, u32[]{:S(2)}) collective-permute-start(f32[256,256]{1,0:T(8,128)} %slice.29), channel_id=1, source_target_pairs={{0,40},{64,104},{128,168},{192,232},{256,296},{320,360},{384,424},... | collective-permute-start | bytes 786440 | tf_op jit(solution)/shard_map/ppermute | solution.py:16
  4.4 5.9 %collective-permute-start.6 = (f32[256,256]{1,0:T(8,128)}, f32[256,256]{1,0:T(8,128)S(1)}, u32[]{:S(2)}, u32[]{:S(2)}) collective-permute-start(f32[256,256]{1,0:T(8,128)} %slice.29), channel_id=1, source_target_pairs={{0,32},{64,96},{128,160},{192,224},{256,288},{320,352},{384,416},{... | collective-permute-start | bytes 786440 | tf_op jit(solution)/shard_map/ppermute | solution.py:16
  5.1 5.3 collective-permute-start.5
  6.5 3.9 collective-permute-start.3
  7.2 3.9 collective-permute-start.4
  9.7 11.6 %collective-permute-start = (f32[512,256]{1,0:T(8,128)S(1)}, f32[512,256]{1,0:T(8,128)S(1)}, u32[]{:S(2)}, u32[]{:S(2)}) collective-permute-start(f32[512,256]{1,0:T(8,128)S(1)} %slice.28), channel_id=1, source_target_pairs={{0,4},{8,12},{16,20},{24,28},{32,36},{40,44},{48,52},{56,60},{64,6... | collective-permute-start | bytes 1572872 | tf_op jit(solution)/shard_map/ppermute | solution.py:16
  10.4 0.7 copy-start.4
  12.4 7.4 %collective-permute-start.10 = (f32[256,256]{1,0:T(8,128)S(1)}, f32[256,256]{1,0:T(8,128)S(1)}, u32[]{:S(2)}, u32[]{:S(2)}) collective-permute-start(f32[256,256]{1,0:T(8,128)S(1)} %add_select_fusion.1), channel_id=1, source_target_pairs={{0,4},{8,12},{16,20},{24,28},{32,36},{40,44},{48,52},{56,60},{64,6... | collective-permute-start | bytes 786440 | tf_op jit(solution)/shard_map/ppermute | solution.py:16
  13.9 16.6 %collective-permute-start.13 = (f32[256,512]{1,0:T(8,128)}, f32[256,512]{1,0:T(8,128)}, u32[]{:S(2)}, u32[]{:S(2)}) collective-permute-start(f32[256,512]{1,0:T(8,128)} %slice_bitcast_fusion), channel_id=1, source_target_pairs={{0,32},{1,33},{2,34},{3,35},{4,36},{5,37},{6,38},{7,39},{64,96},{6... | collective-permute-start | bytes 1572872 | tf_op jit(solution)/shard_map/ppermute | solution.py:16
  19.9 14.1 %collective-permute-start.11 = (f32[256,256]{1,0:T(8,128)S(1)}, f32[256,256]{1,0:T(8,128)}, u32[]{:S(2)}, u32[]{:S(2)}) collective-permute-start(f32[256,256]{1,0:T(8,128)S(1)} %broadcast_select_fusion.11), channel_id=1, source_target_pairs={{0,2},{4,6},{8,10},{12,14},{16,18},{20,22},{24,26},{28,30},{32,34}... | collective-permute-start | bytes 786440 | tf_op jit(solution)/shard_map/ppermute | solution.py:16
  21.3 14.0 %collective-permute-start.1 = (f32[512,256]{1,0:T(8,128)S(1)}, f32[512,256]{1,0:T(8,128)S(1)}, u32[]{:S(2)}, u32[]{:S(2)}) collective-permute-start(f32[512,256]{1,0:T(8,128)S(1)} %broadcast_select_fusion.7), channel_id=1, source_target_pairs={{0,2},{4,6},{8,10},{12,14},{16,18},{20,22},{24,26},{28,30},{32,34}... | collective-permute-start | bytes 1572872 | tf_op jit(solution)/shard_map/ppermute | solution.py:16
  30.6 11.9 %collective-permute-start.14 = (f32[256,512]{1,0:T(8,128)S(1)}, f32[256,512]{1,0:T(8,128)}, u32[]{:S(2)}, u32[]{:S(2)}) collective-permute-start(f32[256,512]{1,0:T(8,128)S(1)} %broadcast_select_fusion.4), channel_id=1, source_target_pairs={{0,16},{32,48},{1,17},{33,49},{2,18},{34,50},{3,19},{35,51},{4,20}... | collective-permute-start | bytes 1572872 | tf_op jit(solution)/shard_map/ppermute | solution.py:16
  34.0 40.3 %collective-permute-start.12 = (f32[256,256]{1,0:T(8,128)S(1)}, f32[256,256]{1,0:T(8,128)}, u32[]{:S(2)}, u32[]{:S(2)}) collective-permute-start(f32[256,256]{1,0:T(8,128)S(1)} %broadcast_select_fusion.13), channel_id=1, source_target_pairs={{0,1},{2,3},{4,5},{6,7},{8,9},{10,11},{12,13},{14,15},{16,17},{18,... | collective-permute-start | bytes 786440 | tf_op jit(solution)/shard_map/ppermute | solution.py:16
  35.4 81.5 %collective-permute-start.2 = (f32[512,256]{1,0:T(8,128)S(1)}, f32[512,256]{1,0:T(8,128)S(1)}, u32[]{:S(2)}, u32[]{:S(2)}) collective-permute-start(f32[512,256]{1,0:T(8,128)S(1)} %broadcast_select_fusion.8), channel_id=1, source_target_pairs={{0,1},{2,3},{4,5},{6,7},{8,9},{10,11},{12,13},{14,15},{16,17},{18,... | collective-permute-start | bytes 1572872 | tf_op jit(solution)/shard_map/ppermute | solution.py:16
  42.6 75.9 %collective-permute-start.15 = (f32[256,512]{1,0:T(8,128)S(1)}, f32[256,512]{1,0:T(8,128)S(1)}, u32[]{:S(2)}, u32[]{:S(2)}) collective-permute-start(f32[256,512]{1,0:T(8,128)S(1)} %broadcast_select_fusion.6), channel_id=1, source_target_pairs={{0,8},{16,24},{32,40},{48,56},{1,9},{17,25},{33,41},{49,57},{2,10}... | collective-permute-start | bytes 1572872 | tf_op jit(solution)/shard_map/ppermute | solution.py:16
  118.5 3.8 copy-start.2
  358.5 4.8 collective-permute-start.16
  363.2 1.0 copy-start.3
  368.4 2.2 copy-start
  369.8 0.7 collective-permute-start.17
  370.8 18.4 %collective-permute-start.18 = (f32[1024,256]{1,0:T(8,128)S(1)}, f32[1024,256]{1,0:T(8,128)}, u32[]{:S(2)}, u32[]{:S(2)}) collective-permute-start(f32[1024,256]{1,0:T(8,128)S(1)} %broadcast_select_fusion), channel_id=1, source_target_pairs={{0,2},{4,6},{128,130},{132,134},{256,258},{260,262},{384,386},{388... | collective-permute-start | bytes 3145736 | tf_op jit(solution)/shard_map/ppermute | solution.py:16
  373.2 4.8 collective-permute-start.27
  373.8 5.5 %collective-permute-start.26 = (f32[256,256]{1,0:T(8,128)}, f32[256,256]{1,0:T(8,128)}, u32[]{:S(2)}, u32[]{:S(2)}) collective-permute-start(f32[256,256]{1,0:T(8,128)} %slice.31), channel_id=1, source_target_pairs={{0,48},{128,176},{256,304},{384,432}} | collective-permute-start | bytes 786440 | tf_op jit(solution)/shard_map/ppermute | solution.py:16
  375.2 5.6 %collective-permute-start.25 = (f32[256,256]{1,0:T(8,128)}, f32[256,256]{1,0:T(8,128)}, u32[]{:S(2)}, u32[]{:S(2)}) collective-permute-start(f32[256,256]{1,0:T(8,128)} %slice.31), channel_id=1, source_target_pairs={{0,40},{128,168},{256,296},{384,424}} | collective-permute-start | bytes 786440 | tf_op jit(solution)/shard_map/ppermute | solution.py:16
  376.6 6.5 %collective-permute-start.24 = (f32[256,256]{1,0:T(8,128)}, f32[256,256]{1,0:T(8,128)}, u32[]{:S(2)}, u32[]{:S(2)}) collective-permute-start(f32[256,256]{1,0:T(8,128)} %slice.31), channel_id=1, source_target_pairs={{0,32},{128,160},{256,288},{384,416}} | collective-permute-start | bytes 786440 | tf_op jit(solution)/shard_map/ppermute | solution.py:16
  378.0 7.8 %collective-permute-start.23 = (f32[256,256]{1,0:T(8,128)}, f32[256,256]{1,0:T(8,128)}, u32[]{:S(2)}, u32[]{:S(2)}) collective-permute-start(f32[256,256]{1,0:T(8,128)} %slice.31), channel_id=1, source_target_pairs={{0,24},{128,152},{256,280},{384,408}} | collective-permute-start | bytes 786440 | tf_op jit(solution)/shard_map/ppermute | solution.py:16
  379.3 6.4 %collective-permute-start.21 = (f32[256,256]{1,0:T(8,128)}, f32[256,256]{1,0:T(8,128)}, u32[]{:S(2)}, u32[]{:S(2)}) collective-permute-start(f32[256,256]{1,0:T(8,128)} %slice.31), channel_id=1, source_target_pairs={{0,8},{128,136},{256,264},{384,392}} | collective-permute-start | bytes 786440 | tf_op jit(solution)/shard_map/ppermute | solution.py:16
  380.8 4.9 collective-permute-start.22
  383.0 13.9 %collective-permute-start.32 = (f32[256,512]{1,0:T(8,128)}, f32[256,512]{1,0:T(8,128)}, u32[]{:S(2)}, u32[]{:S(2)}) collective-permute-start(f32[256,512]{1,0:T(8,128)} %slice.32), channel_id=1, source_target_pairs={{0,32},{1,33},{2,34},{3,35},{4,36},{5,37},{6,38},{7,39},{64,96},{6... | collective-permute-start | bytes 1572872 | tf_op jit(solution)/shard_map/ppermute | solution.py:16
  387.2 4.4 collective-permute-start.28
  390.4 43.2 %collective-permute-start.19 = (f32[1024,256]{1,0:T(8,128)}, f32[1024,256]{1,0:T(8,128)}, u32[]{:S(2)}, u32[]{:S(2)}) collective-permute-start(f32[1024,256]{1,0:T(8,128)} %broadcast_select_fusion.1), channel_id=1, source_target_pairs={{0,1},{2,3},{4,5},{6,7},{128,129},{130,131},{132,133},{134,135},{2... | collective-permute-start | bytes 3145736 | tf_op jit(solution)/shard_map/ppermute | solution.py:16
  391.7 0.7 collective-permute-start.29
  392.4 5.9 %collective-permute-start.30 = (f32[256,256]{1,0:T(8,128)S(1)}, f32[256,256]{1,0:T(8,128)S(1)}, u32[]{:S(2)}, u32[]{:S(2)}) collective-permute-start(f32[256,256]{1,0:T(8,128)S(1)} %broadcast_select_fusion.10), channel_id=1, source_target_pairs={{0,2},{4,6},{8,10},{12,14},{16,18},{20,22},{24,26},{28,30},{32,34}... | collective-permute-start | bytes 786440 | tf_op jit(solution)/shard_map/ppermute | solution.py:16
  397.0 40.2 %collective-permute-start.33 = (f32[256,512]{1,0:T(8,128)S(1)}, f32[256,512]{1,0:T(8,128)S(1)}, u32[]{:S(2)}, u32[]{:S(2)}) collective-permute-start(f32[256,512]{1,0:T(8,128)S(1)} %broadcast_select_fusion.3), channel_id=1, source_target_pairs={{0,16},{32,48},{1,17},{33,49},{2,18},{34,50},{3,19},{35,51},{4,20}... | collective-permute-start | bytes 1572872 | tf_op jit(solution)/shard_map/ppermute | solution.py:16
  398.4 92.3 %collective-permute-start.31 = (f32[256,256]{1,0:T(8,128)S(1)}, f32[256,256]{1,0:T(8,128)}, u32[]{:S(2)}, u32[]{:S(2)}) collective-permute-start(f32[256,256]{1,0:T(8,128)S(1)} %broadcast_select_fusion.12), channel_id=1, source_target_pairs={{0,1},{2,3},{4,5},{6,7},{8,9},{10,11},{12,13},{14,15},{16,17},{18,... | collective-permute-start | bytes 786440 | tf_op jit(solution)/shard_map/ppermute | solution.py:16
  434.9 87.6 %collective-permute-start.20 = (f32[1024,256]{1,0:T(8,128)S(1)}, f32[1024,256]{1,0:T(8,128)}, u32[]{:S(2)}, u32[]{:S(2)}) collective-permute-start(f32[1024,256]{1,0:T(8,128)S(1)} %broadcast_select_fusion.2), channel_id=1, source_target_pairs={{0,64},{128,192},{256,320},{384,448},{1,65},{129,193},{257,321},{3... | collective-permute-start | bytes 3145736 | tf_op jit(solution)/shard_map/ppermute | solution.py:16
  438.1 82.7 %collective-permute-start.34 = (f32[256,512]{1,0:T(8,128)}, f32[256,512]{1,0:T(8,128)}, u32[]{:S(2)}, u32[]{:S(2)}) collective-permute-start(f32[256,512]{1,0:T(8,128)} %broadcast_select_fusion.5), channel_id=1, source_target_pairs={{0,8},{16,24},{32,40},{48,56},{1,9},{17,25},{33,41},{49,57},{2,10}... | collective-permute-start | bytes 1572872 | tf_op jit(solution)/shard_map/ppermute | solution.py:16

commit v2 on v1

v2 whole, which is shorter than its diff:
```python
import functools

import jax
import jax.numpy as jnp
from jax import lax
from jax.experimental import pallas as pl
from jax.experimental.pallas import tpu as pltpu
from jax.sharding import PartitionSpec as P

BLK = 128
STEP = 64
GROUP = 8
HIGHEST = lax.Precision.HIGHEST


def send(value, axes, pairs):
    return lax.ppermute(value, axes, pairs)


def tree(value, axis, rounds):
    index = lax.axis_index(axis)
    for pairs in rounds:
        got = send(value, axis, pairs)
        is_target = functools.reduce(jnp.logical_or, [index == t for _, t in pairs])
        value = jnp.where(is_target, got, value)
    return value


HALVING = ([(0, 4)], [(0, 2), (4, 6)], [(0, 1), (2, 3), (4, 5), (6, 7)])


def reciprocal(x):
    guess = pltpu.reciprocal(x, approx=True)
    guess = guess * (2.0 - x * guess)
    return guess * (2.0 - x * guess)


def inverse_factor_kernel(a_ref, out_ref, x_ref):
    order = a_ref.shape[0]
    f32 = jnp.float32
    value = a_ref[...]
    full_sub = lax.broadcasted_iota(jnp.int32, value.shape, 0)
    full_lane = lax.broadcasted_iota(jnp.int32, value.shape, 1)
    diagonal = jnp.where(full_sub == full_lane, value, 0.0)
    scale_col = lax.rsqrt(jnp.sum(diagonal, axis=1, keepdims=True))
    scale_row = lax.rsqrt(jnp.sum(diagonal, axis=0, keepdims=True))
    x_ref[...] = (value * scale_col) * scale_row
    wide = (STEP, 2 * STEP)
    sub = lax.broadcasted_iota(jnp.int32, wide, 0)
    lane = lax.broadcasted_iota(jnp.int32, wide, 1)
    eye = (sub[:, :STEP] == lane[:, :STEP]).astype(f32)
    for start in range(0, order, STEP):
        stop = start + STEP
        rows = x_ref[start:stop, :]
        work = jnp.concatenate([x_ref[start:stop, start:stop], eye], axis=1)
        for base in range(0, STEP, GROUP):
            cols = [
                jnp.broadcast_to(work[:, base + j : base + j + 1], wide) for j in range(GROUP)
            ]
            for j in range(0, GROUP, 2):
                k = base + j
                c0, c1 = cols[j], cols[j + 1]
                p00, p01, p11 = c0[k : k + 1], c1[k : k + 1], c1[k + 1 : k + 2]
                over = reciprocal(p00 * p11 - p01 * p01)
                a00, a01, a11 = p00 * over, p01 * over, p11 * over
                below = sub > k + 1
                f0 = jnp.where(below, c0 * a11 - c1 * a01, 0.0)
                f1 = jnp.where(below, c1 * a00 - c0 * a01, 0.0)
                for i in range(j + 2, GROUP):
                    cols[i] = cols[i] - f0 * cols[i][k : k + 1] - f1 * cols[i][k + 1 : k + 2]
                work = work - f0 * work[k : k + 1] - f1 * work[k + 1 : k + 2]
        pivots = jnp.sum(jnp.where(sub == lane, work, 0.0), axis=1, keepdims=True)
        left = jnp.sum(jnp.where(sub == lane + 1, work, 0.0), axis=1, keepdims=True)
        above = pltpu.roll(jnp.broadcast_to(pivots, wide), 1, 0)
        work = work - jnp.where(sub % 2 == 1, left / above, 0.0) * pltpu.roll(work, 1, 0)
        pivots = jnp.sum(jnp.where(sub == lane, work, 0.0), axis=1, keepdims=True)
        inverse = work[:, STEP:] * lax.rsqrt(pivots)
        panel = jnp.dot(inverse, rows, precision=HIGHEST, preferred_element_type=f32)
        pieces = [inverse]
        if start:
            pieces.insert(0, panel[:, :start])
        if stop < order:
            pieces.append(panel[:, stop:])
        panel = jnp.concatenate(pieces, axis=1)
        x_ref[start:stop, :] = panel
        if stop < order:
            change = lax.dot_general(
                panel[:, stop:], panel, (((0,), (0,)), ((), ())),
                precision=HIGHEST, preferred_element_type=f32,
            )
            old = x_ref[stop:, :]
            at = lax.broadcasted_iota(jnp.int32, old.shape, 1)
            x_ref[stop:, :] = jnp.where((at >= start) & (at < stop), 0.0, old) - change
    out_ref[...] = jnp.where(full_lane <= full_sub, x_ref[...] * scale_row, 0.0)


def inverse_factor(block):
    return pl.pallas_call(
        inverse_factor_kernel,
        out_shape=jax.ShapeDtypeStruct(block.shape, jnp.float32),
        scratch_shapes=[pltpu.VMEM(block.shape, jnp.float32)],
        name="inverse_factor",
    )(block)


def smem():
    return pl.BlockSpec(memory_space=pltpu.SMEM)


def vmem():
    return pl.BlockSpec(memory_space=pltpu.VMEM)


def row_tables(map_ref, row, row_span, count, rank_ref, at_ref):
    for m in range(at_ref.shape[0]):
        at_ref[m] = -1

    def body(k, rank):
        here = map_ref[k] // row_span == row
        rank_ref[k] = jnp.where(here, rank, -1)

        @pl.when(here)
        def _():
            at_ref[jnp.minimum(rank, at_ref.shape[0] - 1)] = map_ref[k] % row_span

        return rank + here.astype(jnp.int32)

    lax.fori_loop(0, count, body, jnp.int32(0))


def strips_kernel(sizes, ids_ref, map_ref, part_ref, *refs):
    row_span, first, row_blocks, rows = sizes
    outs, slots_ref = refs[:rows], refs[rows]
    row = ids_ref[1]
    for a in range(row_blocks):
        block = row * row_blocks + a - first

        @pl.when(block >= 0)
        def _():
            target = map_ref[jnp.maximum(block, 0)] // row_span
            slots_ref[(target - row + rows) % rows] = part_ref[a * BLK : (a + 1) * BLK, :]

    for s in range(rows):
        outs[s][...] = slots_ref[s]


def tiles_kernel(sizes, ids_ref, map_ref, *refs):
    row_span, col_span, first, row_blocks, col_blocks, rows, cols, count = sizes
    gots, outs = refs[:rows], refs[rows : rows + cols]
    slots_ref, rank_ref, at_ref = refs[rows + cols :]
    row, col = ids_ref[1], ids_ref[2]
    row_tables(map_ref, row, row_span, count, rank_ref, at_ref)
    for s in range(rows):
        source = (row - s + rows) % rows

        def body(a, carry):
            block = source * row_blocks + a - first
            rank = jnp.where(block >= 0, rank_ref[jnp.maximum(block, 0)], -1)

            @pl.when(rank >= 0)
            def _():
                held = gots[s]
                slot = jnp.minimum(rank, slots_ref.shape[1] - 1)
                for y in range(col_blocks):
                    block = col * col_blocks + y - first

                    @pl.when(block >= 0)
                    def _():
                        target = (map_ref[jnp.maximum(block, 0)] // col_span) % cols
                        slots_ref[(target - col + cols) % cols, slot] = held[
                            :, y * BLK : (y + 1) * BLK
                        ]

            return carry

        lax.fori_loop(0, row_blocks, body, jnp.int32(0))
    for t in range(cols):
        outs[t][...] = slots_ref[t]


def other_kernel(sizes, ids_ref, map_ref, *refs):
    col_span, first, col_blocks, cols = sizes
    gots, out_ref = refs[:cols], refs[cols]
    half, col = ids_ref[0], ids_ref[2]
    out_ref[...] = jnp.zeros_like(out_ref)
    for t in range(cols):
        source = (col - t + cols) % cols

        def body(y, carry):
            block = source * col_blocks + y - first
            spot = map_ref[jnp.maximum(block, 0)]
            owner = spot // col_span

            @pl.when((block >= 0) & (owner % cols == col) & (owner // cols != half))
            def _():
                out_ref[spot % col_span] = gots[t][...]

            return carry

        lax.fori_loop(0, col_blocks, body, jnp.int32(0))


def assemble_kernel(sizes, ids_ref, map_ref, pair_map_ref, parent_ref, own_ref, pair_ref,
                    other_ref, *refs):
    row_span, col_span, first, col_blocks, cols, count = sizes
    gots, out_ref = refs[:cols], refs[cols]
    rank_ref, at_ref, pair_at_ref = refs[cols + 1 :]
    half, row, col = ids_ref[0], ids_ref[1], ids_ref[2]
    out_ref[...] = parent_ref[...].astype(jnp.float32)
    row_tables(pair_map_ref, row, row_span, count, rank_ref, pair_at_ref)
    row_tables(map_ref, row, row_span, count, rank_ref, at_ref)
    caps = at_ref.shape[0]
    for m in range(caps):
        for table, product in ((at_ref, own_ref), (pair_at_ref, pair_ref)):
            at = table[m]

            @pl.when(at >= 0)
            def _():
                spot = (pl.ds(pl.multiple_of(at * BLK, BLK), BLK), slice(None))
                out_ref[spot] = out_ref[spot] - product[m * BLK : (m + 1) * BLK, :]

        at = pair_at_ref[m]

        @pl.when(at >= 0)
        def _():
            for y in range(col_span):
                spot = (
                    pl.ds(pl.multiple_of(at * BLK, BLK), BLK), slice(y * BLK, (y + 1) * BLK)
                )
                out_ref[spot] = out_ref[spot] + other_ref[y, m]

    for t in range(cols):
        source = (col - t + cols) % cols

        def body(y, carry):
            block = source * col_blocks + y - first
            place = map_ref[jnp.maximum(block, 0)]
            owner = place // col_span

            @pl.when((block >= 0) & (owner % cols == col) & (owner // cols == half))
            def _():
                at_col = pl.ds(pl.multiple_of((place % col_span) * BLK, BLK), BLK)
                for m in range(caps):
                    at = at_ref[m]

                    @pl.when(at >= 0)
                    def _():
                        spot = (pl.ds(pl.multiple_of(at * BLK, BLK), BLK), at_col)
                        out_ref[spot] = out_ref[spot] + gots[t][m]

            return carry

        lax.fori_loop(0, col_blocks, body, jnp.int32(0))


def row_slots_kernel(sizes, ids_ref, map_ref, part_ref, out_ref):
    row_span, first, row_blocks = sizes
    row = ids_ref[1]
    for a in range(row_blocks):
        block = row * row_blocks + a - first

        @pl.when(block >= 0)
        def _():
            target = map_ref[jnp.maximum(block, 0)] // row_span
            out_ref[target] = part_ref[:, a * BLK : (a + 1) * BLK]


def col_slots_kernel(sizes, ids_ref, map_ref, part_ref, out_ref):
    col_span, first, col_blocks, cols = sizes
    col = ids_ref[2]
    for y in range(col_blocks):
        block = col * col_blocks + y - first

        @pl.when(block >= 0)
        def _():
            target = (map_ref[jnp.maximum(block, 0)] // col_span) % cols
            out_ref[target] = part_ref[:, y * BLK : (y + 1) * BLK]


def row_pick_kernel(sizes, ids_ref, map_ref, got_ref, out_ref, rank_ref, at_ref):
    row_span, first, row_blocks, count = sizes
    row_tables(map_ref, ids_ref[1], row_span, count, rank_ref, at_ref)
    out_ref[...] = jnp.zeros_like(out_ref)

    def body(k, carry):
        rank = rank_ref[k]

        @pl.when(rank >= 0)
        def _():
            out_ref[jnp.minimum(rank, out_ref.shape[0] - 1)] = got_ref[(k + first) // row_blocks]

        return carry

    lax.fori_loop(0, count, body, jnp.int32(0))


def col_pick_kernel(sizes, ids_ref, map_ref, got_ref, own_ref, other_ref):
    col_span, first, col_blocks, cols, count = sizes
    half, col = ids_ref[0], ids_ref[2]
    own_ref[...] = jnp.zeros_like(own_ref)
    other_ref[...] = jnp.zeros_like(other_ref)

    def body(k, carry):
        owner = map_ref[k] // col_span
        for target, wanted in ((own_ref, half), (other_ref, 1 - half)):

            @pl.when((owner % cols == col) & (owner // cols == wanted))
            def _():
                target[map_ref[k] % col_span] = got_ref[(k + first) // col_blocks]

        return carry

    lax.fori_loop(0, count, body, jnp.int32(0))


def kernel_call(body, name, outs, n_smem, n_vmem, scratch=()):
    many = isinstance(outs, list)
    shapes = [jax.ShapeDtypeStruct(o, jnp.float32) for o in (outs if many else [outs])]
    specs = [vmem() for _ in shapes]
    return pl.pallas_call(
        body,
        out_shape=shapes if many else shapes[0],
        in_specs=[smem()] * n_smem + [vmem()] * n_vmem,
        out_specs=specs if many else specs[0],
        scratch_shapes=list(scratch),
        compiler_params=pltpu.CompilerParams(vmem_limit_bytes=40 * 2**20),
        name=name,
    )


def gather_doubling(value, axis, order):
    index = lax.axis_index(axis)
    size = lax.axis_size(axis)
    value = value[None]
    done = []
    for bit in order:
        got = send(value, axis, [(i, i ^ (1 << bit)) for i in range(size)])
        upper = (index >> bit) & 1
        low = jnp.where(upper == 0, value, got)
        high = jnp.where(upper == 0, got, value)
        value = jnp.concatenate([low, high], axis=0)
        done.insert(0, bit)
    bits = len(order)
    shape = value.shape[1:]
    value = value.reshape((2,) * bits + shape)
    perm = [done.index(b) for b in range(bits - 1, -1, -1)]
    value = jnp.transpose(value, perm + list(range(bits, bits + len(shape))))
    return value.reshape((size,) + shape)


def shards(child_front, parent_front, block_map):
    leaf_id = lax.axis_index("leaf")
    row_id = lax.axis_index("row")
    col_id = lax.axis_index("col")
    row_count = lax.axis_size("row")
    col_count = lax.axis_size("col")
    leaf_count = lax.axis_size("leaf")
    half_id = leaf_id % 2
    ids = jnp.stack([half_id, row_id, col_id]).astype(jnp.int32)
    own_map = lax.dynamic_index_in_dim(block_map, leaf_id, 0, keepdims=False)
    partner_map = lax.dynamic_index_in_dim(block_map, leaf_id ^ 1, 0, keepdims=False)
    count = own_map.shape[0]

    child_block = child_front[0]
    child_rows, child_cols = child_block.shape
    width = child_cols // 2
    parent_rows, parent_cols = parent_front.shape
    row_span, col_span = parent_rows // BLK, parent_cols // BLK
    row_blocks, col_blocks = child_rows // BLK, child_cols // BLK
    first = width // BLK
    cap = -(-count // row_count)
    swap = [(i, i ^ 1) for i in range(leaf_count)]

    strips = kernel_call(
        functools.partial(strips_kernel, (row_span, first, row_blocks, row_count)),
        "strips", [(BLK, child_cols)] * row_count, 2, 1,
        [pltpu.VMEM((row_count, BLK, child_cols), jnp.float32)],
    )(ids, own_map, child_block)

    diagonal = child_block[:width, :width]
    spread = [send(diagonal, ("row", "col"), [(0, r * col_count)]) for r in range(1, row_count)]
    diagonal = jnp.where(row_id == 0, diagonal, functools.reduce(jnp.add, spread))
    diagonal = tree(diagonal, "col", HALVING)
    slab = tree(child_block[:, :width], "col", HALVING)
    top = tree(child_block[:width], "row", HALVING)

    got = [strips[0]] + [
        send(strips[s], "row", [(i, (i + s) % row_count) for i in range(row_count)])
        for s in range(1, row_count)
    ]
    tables = [pltpu.SMEM((count,), jnp.int32), pltpu.SMEM((cap,), jnp.int32)]
    tiles = kernel_call(
        functools.partial(
            tiles_kernel,
            (row_span, col_span, first, row_blocks, col_blocks, row_count, col_count, count),
        ),
        "tiles", [(cap, BLK, BLK)] * col_count, 2, row_count,
        [pltpu.VMEM((col_count, cap, BLK, BLK), jnp.float32)] + tables,
    )(ids, own_map, *got)
    landed = [tiles[0]] + [
        send(tiles[t], "col", [(i, (i + t) % col_count) for i in range(col_count)])
        for t in range(1, col_count)
    ]

    inverse = inverse_factor(diagonal)
    cols_factor = jnp.dot(inverse, top, precision=HIGHEST)
    out_width = width // col_count
    share = lax.dynamic_slice_in_dim(inverse, col_id * out_width, out_width, 0)
    child_out = lax.dot_general(share, slab, (((1,), (1,)), ((), ())), precision=HIGHEST)
    piece = (out_width, BLK)

    row_slots = kernel_call(
        functools.partial(row_slots_kernel, (row_span, first, row_blocks)),
        "row_slots", (row_count,) + piece, 2, 1,
    )(ids, own_map, child_out)
    row_got = lax.all_to_all(row_slots, "row", 0, 0, tiled=True)
    row_panel = kernel_call(
        functools.partial(row_pick_kernel, (row_span, first, row_blocks, count)),
        "row_pick", (cap,) + piece, 2, 1, tables,
    )(ids, own_map, row_got)
    row_panel = gather_doubling(row_panel, "col", (2, 1, 0))
    row_panel = jnp.transpose(row_panel, (0, 2, 1, 3)).reshape(width, cap * BLK)
    pair_row_panel = send(row_panel, "leaf", swap)

    col_share = lax.dynamic_slice_in_dim(cols_factor, row_id * out_width, out_width, 0)
    col_slots = kernel_call(
        functools.partial(col_slots_kernel, (col_span, first, col_blocks, col_count)),
        "col_slots", (col_count,) + piece, 2, 1,
    )(ids, own_map, col_share)
    col_got = lax.all_to_all(col_slots, "col", 0, 0, tiled=True)
    own_cols, other_cols = kernel_call(
        functools.partial(col_pick_kernel, (col_span, first, col_blocks, col_count, count)),
        "col_pick", [(col_span,) + piece] * 2, 2, 1,
    )(ids, own_map, col_got)
    col_panels = jnp.stack([own_cols, send(other_cols, "leaf", swap)])
    col_panels = gather_doubling(col_panels, "row", (0, 1, 2))
    col_panels = jnp.transpose(col_panels, (1, 0, 3, 2, 4)).reshape(2, width, col_span * BLK)

    def product(rows, cols):
        return lax.dot_general(rows, cols, (((0,), (0,)), ((), ())), precision=HIGHEST)

    own_product = product(row_panel, col_panels[0])
    pair_product = product(pair_row_panel, col_panels[1])

    other = kernel_call(
        functools.partial(other_kernel, (col_span, first, col_blocks, col_count)),
        "other", (col_span, cap, BLK, BLK), 2, col_count,
    )(ids, own_map, *landed)
    other = send(other, "leaf", swap)
    assembled = kernel_call(
        functools.partial(
            assemble_kernel, (row_span, col_span, first, col_blocks, col_count, count)
        ),
        "assemble", parent_front.shape, 3, 4 + col_count,
        tables + [pltpu.SMEM((cap,), jnp.int32)],
    )(ids, own_map, partner_map, parent_front, own_product, pair_product, other, *landed)

    parent_order = parent_rows * row_count
    parent_width = parent_cols // 2
    diagonal = assembled[:parent_width, :parent_width]
    even = range(0, leaf_count, 2)
    grid = row_count * col_count
    spread = [
        send(diagonal, ("leaf", "row", "col"), [(l * grid, l * grid + r * col_count) for l in even])
        for r in range(1, row_count)
    ]
    diagonal = jnp.where(row_id == 0, diagonal, functools.reduce(jnp.add, spread))
    across = [(l, l + 1) for l in even]
    diagonal = jnp.where(half_id == 0, diagonal, send(diagonal, "leaf", across))
    diagonal = tree(diagonal, "col", HALVING)
    slab = assembled[:, :parent_width]
    for pairs in HALVING:
        moves = [(l * col_count + s, l * col_count + t) for l in even for s, t in pairs]
        moved = send(slab, ("leaf", "col"), moves)
        is_target = functools.reduce(jnp.logical_or, [col_id == t for _, t in pairs])
        slab = jnp.where(is_target, moved, slab)
    slab = jnp.where(half_id == 0, slab, send(slab, "leaf", across))
    top = tree(assembled[:parent_width], "row", HALVING)
    inverse = inverse_factor(diagonal)
    rows_factor = lax.dot_general(slab, inverse, (((1,), (1,)), ((), ())), precision=HIGHEST)
    cols_factor = jnp.dot(inverse, top, precision=HIGHEST)
    update = jnp.dot(rows_factor, cols_factor, precision=HIGHEST)
    row_ids = row_id * parent_rows + jnp.arange(parent_rows)
    col_ids = half_id * (parent_order // 2) + col_id * parent_cols + jnp.arange(parent_cols)
    keep = (row_ids[:, None] >= parent_width) & (col_ids[None, :] >= parent_width)
    parent_schur = jnp.where(keep, assembled - update, jnp.float32(0.0))
    share = parent_width // (2 * col_count)
    start = (half_id * col_count + col_id) * share
    parent_out = lax.dynamic_slice_in_dim(rows_factor, start, share, 1).T
    return (child_out[None], parent_out, parent_schur)


def solution(mesh):
    placed = (P("leaf", "row", "col"), P("row", ("leaf", "col")), P())
    return jax.shard_map(
        shards,
        mesh=mesh,
        in_specs=placed,
        out_specs=(P("leaf", "col", "row"), P(("leaf", "col"), "row"), P("row", ("leaf", "col"))),
        check_vma=False,
    )
```

time: 530 us -> 687 us (1.30)
  the two profiles are of different devices: /device:TPU:224 before, /device:TPU:185 now
where the time goes in v2:
time: 687 us; the launch traced here: 685 us
  starting transfers between devices  377 us (55%)
  waiting for transfers between devices  226 us (33%)
  Pallas kernels  40.4 us (6%)
  other arithmetic  15.7 us (2%)
  matrix products  13 us (2%)
  local copies, waits for them, and re-layouts  9.76 us (1%)
    ppermute x57, starting transfers between devices, send(): return lax.ppermute(value, axes, pairs)  325 us
    ppermute x57, waiting for transfers between devices, send(): return lax.ppermute(value, axes, pairs)  226 us
    all_to_all x1, starting transfers between devices, shards(): col_got = lax.all_to_all(col_slots, 'col', 0, 0, tiled=True)  41.9 us
    pallas_call x2, Pallas kernels, inverse_factor(): pl.pallas_call(inverse_factor_kernel, out_shape=jax.ShapeDtypeStruct(bloc...  24.9 us
  transfers between devices with their start and end apart: 59, of which 11 were waited for; matrix products, arithmetic and copies ran while one was open for 4% of the time, Pallas kernels for 5%

profile of v2, /device:TPU:185, one launch (start us, length us, event | category | flops | bytes accessed | tf_op | source)
XLA Modules:
  0.0 684.7 jit_solution(10957854178916733662)
XLA Ops:
  0.6 1.8 slice.38
  20.8 18.9 %collective-permute-done.17 = f32[256,512]{1,0:T(8,128)S(1)} collective-permute-done((f32[256,512]{1,0:T(8,128)S(1)}, f32[256,512]{1,0:T(8,128)S(1)}, u32[]{:S(2)}, u32[]{:S(2)}) %collective-permute-start.17) | collective-permute-done | bytes 524320 | tf_op jit(solution)/shard_map/ppermute | solution.py:17
  41.2 18.1 %collective-permute-done.9 = f32[256,256]{1,0:T(8,128)} collective-permute-done((f32[256,256]{1,0:T(8,128)S(1)}, f32[256,256]{1,0:T(8,128)}, u32[]{:S(2)}, u32[]{:S(2)}) %collective-permute-start.9) | collective-permute-done | bytes 262176 | tf_op jit(solution)/shard_map/ppermute | solution.py:17
  59.3 1.7 broadcast_select_fusion.21.a_ref
  61.0 12.4 %inverse_factor.2 = f32[256,256]{1,0:T(8,128)} custom-call(f32[256,256]{1,0:T(8,128)} %broadcast_select_fusion.21.a_ref), custom_call_target="tpu_custom_call" | custom-call | tf_op jit(solution)/shard_map/inverse_factor/pallas_call | solution.py:98
  78.5 41.9 %all-to-all-start.1 = ((f32[8,32,128]{2,1,0:T(8,128)}), f32[8,32,128]{2,1,0:T(8,128)S(1)}, u32[]{:S(2)}, u32[]{:S(2)}) async-start(f32[8,32,128]{2,1,0:T(8,128)} %col_slots.1), calls=%async_computation.1 | async-start | bytes 262144 | tf_op jit(solution)/shard_map/all_to_all | solution.py:430
  121.9 27.4 %collective-permute-start.24 = (f32[128,512]{1,0:T(8,128)S(1)}, f32[128,512]{1,0:T(8,128)S(1)}, u32[]{:S(2)}, u32[]{:S(2)}) collective-permute-start(f32[128,512]{1,0:T(8,128)S(1)} %get-tuple-element.24), channel_id=1, source_target_pairs={{0,8},{8,16},{16,24},{24,32},{32,40},{40,48},{48,56},{56,0},{1,9},... | collective-permute-start | bytes 786440 | tf_op jit(solution)/shard_map/ppermute | solution.py:17
  149.3 19.0 %collective-permute-start.25 = (f32[128,512]{1,0:T(8,128)S(1)}, f32[128,512]{1,0:T(8,128)S(1)}, u32[]{:S(2)}, u32[]{:S(2)}) collective-permute-start(f32[128,512]{1,0:T(8,128)S(1)} %get-tuple-element.25), channel_id=1, source_target_pairs={{0,16},{8,24},{16,32},{24,40},{32,48},{40,56},{48,0},{56,8},{1,17}... | collective-permute-start | bytes 786440 | tf_op jit(solution)/shard_map/ppermute | solution.py:17
  168.3 1.6 fusion.12.part_ref
  171.2 10.2 %all-to-all-start = ((f32[8,32,128]{2,1,0:T(8,128)}), f32[8,32,128]{2,1,0:T(8,128)S(1)}, u32[]{:S(2)}, u32[]{:S(2)}) async-start(f32[8,32,128]{2,1,0:T(8,128)} %row_slots.1), calls=%async_computation | async-start | bytes 262144 | tf_op jit(solution)/shard_map/all_to_all | solution.py:416
  181.5 23.2 %collective-permute-start.26 = (f32[128,512]{1,0:T(8,128)}, f32[128,512]{1,0:T(8,128)S(1)}, u32[]{:S(2)}, u32[]{:S(2)}) collective-permute-start(f32[128,512]{1,0:T(8,128)} %get-tuple-element.26), channel_id=1, source_target_pairs={{0,24},{8,32},{16,40},{24,48},{32,56},{40,0},{48,8},{56,16},{1,25}... | collective-permute-start | bytes 786440 | tf_op jit(solution)/shard_map/ppermute | solution.py:17
  204.6 3.0 collective-permute-start.27
  207.6 19.1 %collective-permute-start.28 = (f32[128,512]{1,0:T(8,128)S(1)}, f32[128,512]{1,0:T(8,128)S(1)}, u32[]{:S(2)}, u32[]{:S(2)}) collective-permute-start(f32[128,512]{1,0:T(8,128)S(1)} %get-tuple-element.28), channel_id=1, source_target_pairs={{0,40},{8,48},{16,56},{24,0},{32,8},{40,16},{48,24},{56,32},{1,41}... | collective-permute-start | bytes 786440 | tf_op jit(solution)/shard_map/ppermute | solution.py:17
  226.7 19.0 %collective-permute-start.29 = (f32[128,512]{1,0:T(8,128)S(1)}, f32[128,512]{1,0:T(8,128)S(1)}, u32[]{:S(2)}, u32[]{:S(2)}) collective-permute-start(f32[128,512]{1,0:T(8,128)S(1)} %get-tuple-element.29), channel_id=1, source_target_pairs={{0,48},{8,56},{16,0},{24,8},{32,16},{40,24},{48,32},{56,40},{1,49}... | collective-permute-start | bytes 786440 | tf_op jit(solution)/shard_map/ppermute | solution.py:17
  245.7 19.0 %collective-permute-start.30 = (f32[128,512]{1,0:T(8,128)S(1)}, f32[128,512]{1,0:T(8,128)S(1)}, u32[]{:S(2)}, u32[]{:S(2)}) collective-permute-start(f32[128,512]{1,0:T(8,128)S(1)} %get-tuple-element.30), channel_id=1, source_target_pairs={{0,56},{8,0},{16,8},{24,16},{32,24},{40,32},{48,40},{56,48},{1,57}... | collective-permute-start | bytes 786440 | tf_op jit(solution)/shard_map/ppermute | solution.py:17
  266.3 2.5 collective-permute-start.19
  268.8 23.6 %collective-permute-done.30.refs_7_ = f32[128,512]{1,0:T(8,128)S(1)} collective-permute-done((f32[128,512]{1,0:T(8,128)S(1)}, f32[128,512]{1,0:T(8,128)S(1)}, u32[]{:S(2)}, u32[]{:S(2)}) %collective-permute-start.30) | collective-permute-done | bytes 262176 | tf_op jit(solution)/shard_map/ppermute | solution.py:17
  292.4 3.2 tiles.1
  297.8 2.7 collective-permute-start.31
  300.5 9.5 %collective-permute-start.32 = (f32[4,128,128]{2,1,0:T(8,128)}, f32[4,128,128]{2,1,0:T(8,128)S(1)}, u32[]{:S(2)}, u32[]{:S(2)}) collective-permute-start(f32[4,128,128]{2,1,0:T(8,128)} %get-tuple-element.33), channel_id=1, source_target_pairs={{0,2},{1,3},{2,4},{3,5},{4,6},{5,7},{6,0},{7,1},{8,10},{9,11},{10,... | collective-permute-start | bytes 786440 | tf_op jit(solution)/shard_map/ppermute | solution.py:17
  309.9 1.9 collective-permute-start.33
  311.9 15.9 %collective-permute-start.34 = (f32[4,128,128]{2,1,0:T(8,128)}, f32[4,128,128]{2,1,0:T(8,128)S(1)}, u32[]{:S(2)}, u32[]{:S(2)}) collective-permute-start(f32[4,128,128]{2,1,0:T(8,128)} %get-tuple-element.35), channel_id=1, source_target_pairs={{0,4},{1,5},{2,6},{3,7},{4,0},{5,1},{6,2},{7,3},{8,12},{9,13},{10,... | collective-permute-start | bytes 786440 | tf_op jit(solution)/shard_map/ppermute | solution.py:17
  329.4 1.9 collective-permute-start.13
  332.2 30.9 %collective-permute-done.13 = f32[1,4,32,128]{3,2,1,0:T(8,128)S(1)} collective-permute-done((f32[1,4,32,128]{3,2,1,0:T(8,128)S(1)}, f32[1,4,32,128]{3,2,1,0:T(8,128)S(1)}, u32[]{:S(2)}, u32[]{:S(2)}) %collective-permute-start.13) | collective-permute-done | bytes 65568 | tf_op jit(solution)/shard_map/ppermute | solution.py:17
  363.2 22.4 %collective-permute-start.20 = (f32[1,2,4,32,128]{4,3,2,1,0:T(8,128)S(1)}, f32[1,2,4,32,128]{4,3,2,1,0:T(8,128)S(1)}, u32[]{:S(2)}, u32[]{:S(2)}) collective-permute-start(f32[1,2,4,32,128]{4,3,2,1,0:T(8,128)S(1)} %maximum_bitcast_fusion.1), channel_id=1, source_target_pairs={{0,8},{8,0},{16,24},{24,16},{32,40},{40,32},{48,56},{56,48},{1,9},... | collective-permute-start | bytes 393224 | tf_op jit(solution)/shard_map/ppermute | solution.py:17
  385.6 16.4 %collective-permute-done.20 = f32[1,2,4,32,128]{4,3,2,1,0:T(8,128)S(1)} collective-permute-done((f32[1,2,4,32,128]{4,3,2,1,0:T(8,128)S(1)}, f32[1,2,4,32,128]{4,3,2,1,0:T(8,128)S(1)}, u32[]{:S(2)}, u32[]{:S(2)}) %collective-permute-start.20) | collective-permute-done | bytes 131104 | tf_op jit(solution)/shard_map/ppermute | solution.py:17
  402.0 1.9 collective-permute-start.14
  404.8 4.6 collective-permute-done.14
  409.4 18.6 %collective-permute-start.21 = (f32[2,2,4,32,128]{4,3,2,1,0:T(8,128)S(1)}, f32[2,2,4,32,128]{4,3,2,1,0:T(8,128)S(1)}, u32[]{:S(2)}, u32[]{:S(2)}) collective-permute-start(f32[2,2,4,32,128]{4,3,2,1,0:T(8,128)S(1)} %pad_maximum_fusion.3), channel_id=1, source_target_pairs={{0,16},{8,24},{16,0},{24,8},{32,48},{40,56},{48,32},{56,40},{1,17}... | collective-permute-start | bytes 786440 | tf_op jit(solution)/shard_map/ppermute | solution.py:17
  428.8 6.0 collective-permute-done.21
  434.9 20.0 %collective-permute-start.35 = (f32[4,128,128]{2,1,0:T(8,128)S(1)}, f32[4,128,128]{2,1,0:T(8,128)S(1)}, u32[]{:S(2)}, u32[]{:S(2)}) collective-permute-start(f32[4,128,128]{2,1,0:T(8,128)S(1)} %copy-done.14), channel_id=1, source_target_pairs={{0,5},{1,6},{2,7},{3,0},{4,1},{5,2},{6,3},{7,4},{8,13},{9,14},{10,... | collective-permute-start | bytes 786440 | tf_op jit(solution)/shard_map/ppermute | solution.py:17
  454.9 19.0 %collective-permute-start.36 = (f32[4,128,128]{2,1,0:T(8,128)S(1)}, f32[4,128,128]{2,1,0:T(8,128)S(1)}, u32[]{:S(2)}, u32[]{:S(2)}) collective-permute-start(f32[4,128,128]{2,1,0:T(8,128)S(1)} %copy-done.12), channel_id=1, source_target_pairs={{0,6},{1,7},{2,0},{3,1},{4,2},{5,3},{6,4},{7,5},{8,14},{9,15},{10,... | collective-permute-start | bytes 786440 | tf_op jit(solution)/shard_map/ppermute | solution.py:17
  474.0 19.0 %collective-permute-start.37 = (f32[4,128,128]{2,1,0:T(8,128)S(1)}, f32[4,128,128]{2,1,0:T(8,128)S(1)}, u32[]{:S(2)}, u32[]{:S(2)}) collective-permute-start(f32[4,128,128]{2,1,0:T(8,128)S(1)} %copy-done.10), channel_id=1, source_target_pairs={{0,7},{1,0},{2,1},{3,2},{4,3},{5,4},{6,5},{7,6},{8,15},{9,8},{10,9... | collective-permute-start | bytes 786440 | tf_op jit(solution)/shard_map/ppermute | solution.py:17
  493.0 1.9 collective-permute-start.15
  495.8 2.9 collective-permute-start.22
  498.8 2.1 collective-permute-done.37.refs_7_
  502.5 19.0 %collective-permute-start.38 = (f32[4,4,128,128]{3,2,1,0:T(8,128)S(1)}, f32[4,4,128,128]{3,2,1,0:T(8,128)S(1)}, u32[]{:S(2)}, u32[]{:S(2)}) collective-permute-start(f32[4,4,128,128]{3,2,1,0:T(8,128)S(1)} %other.1), channel_id=1, source_target_pairs={{0,64},{64,0},{128,192},{192,128},{256,320},{320,256},{384,448},{4... | collective-permute-start | bytes 3145736 | tf_op jit(solution)/shard_map/ppermute | solution.py:17
  523.1 2.3 collective-permute-start.23
  529.7 3.4 assemble.1
  545.4 2.3 collective-permute-done.50
  554.1 17.9 %collective-permute-done.55 = f32[256,512]{1,0:T(8,128)S(1)} collective-permute-done((f32[256,512]{1,0:T(8,128)S(1)}, f32[256,512]{1,0:T(8,128)S(1)}, u32[]{:S(2)}, u32[]{:S(2)}) %collective-permute-start.55) | collective-permute-done | bytes 524320 | tf_op jit(solution)/shard_map/ppermute | solution.py:17
  572.9 2.1 collective-permute-start.56
  576.6 85.5 %collective-permute-done.53 = f32[256,256]{1,0:T(8,128)} collective-permute-done((f32[256,256]{1,0:T(8,128)S(1)}, f32[256,256]{1,0:T(8,128)}, u32[]{:S(2)}, u32[]{:S(2)}) %collective-permute-start.53) | collective-permute-done | bytes 262176 | tf_op jit(solution)/shard_map/ppermute | solution.py:17
  662.1 1.7 broadcast_select_fusion.20.a_ref
  663.8 12.5 %inverse_factor.3 = f32[256,256]{1,0:T(8,128)} custom-call(f32[256,256]{1,0:T(8,128)} %broadcast_select_fusion.20.a_ref), custom_call_target="tpu_custom_call" | custom-call | tf_op jit(solution)/shard_map/inverse_factor/pallas_call | solution.py:98
  676.3 1.7 fusion.8
  678.1 2.4 fusion
  681.1 3.6 subtract_select_fusion
  (178 shorter events, 65.1 us)
Async XLA Ops:
  2.4 4.8 collective-permute-start
  3.1 5.5 collective-permute-start.1
  3.8 7.3 %collective-permute-start.2 = (f32[256,256]{1,0:T(8,128)}, f32[256,256]{1,0:T(8,128)S(1)}, u32[]{:S(2)}, u32[]{:S(2)}) collective-permute-start(f32[256,256]{1,0:T(8,128)} %slice.38), channel_id=1, source_target_pairs={{0,24},{64,88},{128,152},{192,216},{256,280},{320,344},{384,408},{... | collective-permute-start | bytes 786440 | tf_op jit(solution)/shard_map/ppermute | solution.py:17
  4.4 9.2 %collective-permute-start.3 = (f32[256,256]{1,0:T(8,128)}, f32[256,256]{1,0:T(8,128)}, u32[]{:S(2)}, u32[]{:S(2)}) collective-permute-start(f32[256,256]{1,0:T(8,128)} %slice.38), channel_id=1, source_target_pairs={{0,32},{64,96},{128,160},{192,224},{256,288},{320,352},{384,416},{... | collective-permute-start | bytes 786440 | tf_op jit(solution)/shard_map/ppermute | solution.py:17
  5.8 8.5 %collective-permute-start.4 = (f32[256,256]{1,0:T(8,128)}, f32[256,256]{1,0:T(8,128)}, u32[]{:S(2)}, u32[]{:S(2)}) collective-permute-start(f32[256,256]{1,0:T(8,128)} %slice.38), channel_id=1, source_target_pairs={{0,40},{64,104},{128,168},{192,232},{256,296},{320,360},{384,424},... | collective-permute-start | bytes 786440 | tf_op jit(solution)/shard_map/ppermute | solution.py:17
  7.2 7.2 %collective-permute-start.5 = (f32[256,256]{1,0:T(8,128)}, f32[256,256]{1,0:T(8,128)}, u32[]{:S(2)}, u32[]{:S(2)}) collective-permute-start(f32[256,256]{1,0:T(8,128)} %slice.38), channel_id=1, source_target_pairs={{0,48},{64,112},{128,176},{192,240},{256,304},{320,368},{384,432},... | collective-permute-start | bytes 786440 | tf_op jit(solution)/shard_map/ppermute | solution.py:17
  8.6 5.8 collective-permute-start.6
  11.0 5.5 collective-permute-start.16
  13.6 5.0 collective-permute-start.10
  16.6 23.1 %collective-permute-start.17 = (f32[256,512]{1,0:T(8,128)S(1)}, f32[256,512]{1,0:T(8,128)S(1)}, u32[]{:S(2)}, u32[]{:S(2)}) collective-permute-start(f32[256,512]{1,0:T(8,128)S(1)} %broadcast_select_fusion.4), channel_id=1, source_target_pairs={{0,16},{32,48},{1,17},{33,49},{2,18},{34,50},{3,19},{35,51},{4,20}... | collective-permute-start | bytes 1572872 | tf_op jit(solution)/shard_map/ppermute | solution.py:17
  18.7 54.7 %collective-permute-start.11 = (f32[512,256]{1,0:T(8,128)S(1)}, f32[512,256]{1,0:T(8,128)S(1)}, u32[]{:S(2)}, u32[]{:S(2)}) collective-permute-start(f32[512,256]{1,0:T(8,128)S(1)} %broadcast_select_fusion.9), channel_id=1, source_target_pairs={{0,2},{4,6},{8,10},{12,14},{16,18},{20,22},{24,26},{28,30},{32,34}... | collective-permute-start | bytes 1572872 | tf_op jit(solution)/shard_map/ppermute | solution.py:17
  19.5 39.8 %collective-permute-start.9 = (f32[256,256]{1,0:T(8,128)S(1)}, f32[256,256]{1,0:T(8,128)}, u32[]{:S(2)}, u32[]{:S(2)}) collective-permute-start(f32[256,256]{1,0:T(8,128)S(1)} %broadcast_select_fusion.19), channel_id=1, source_target_pairs={{0,1},{2,3},{4,5},{6,7},{8,9},{10,11},{12,13},{14,15},{16,17},{18,... | collective-permute-start | bytes 786440 | tf_op jit(solution)/shard_map/ppermute | solution.py:17
  39.8 35.8 %collective-permute-start.18 = (f32[256,512]{1,0:T(8,128)S(1)}, f32[256,512]{1,0:T(8,128)S(1)}, u32[]{:S(2)}, u32[]{:S(2)}) collective-permute-start(f32[256,512]{1,0:T(8,128)S(1)} %broadcast_select_fusion.6), channel_id=1, source_target_pairs={{0,8},{16,24},{32,40},{48,56},{1,9},{17,25},{33,41},{49,57},{2,10}... | collective-permute-start | bytes 1572872 | tf_op jit(solution)/shard_map/ppermute | solution.py:17
  74.3 94.0 %collective-permute-start.12 = (f32[512,256]{1,0:T(8,128)}, f32[512,256]{1,0:T(8,128)}, u32[]{:S(2)}, u32[]{:S(2)}) collective-permute-start(f32[512,256]{1,0:T(8,128)} %broadcast_select_fusion.10), channel_id=1, source_target_pairs={{0,1},{2,3},{4,5},{6,7},{8,9},{10,11},{12,13},{14,15},{16,17},{18,... | collective-permute-start | bytes 1572872 | tf_op jit(solution)/shard_map/ppermute | solution.py:17
  78.5 92.7 %all-to-all-start.1 = ((f32[8,32,128]{2,1,0:T(8,128)}), f32[8,32,128]{2,1,0:T(8,128)S(1)}, u32[]{:S(2)}, u32[]{:S(2)}) async-start(f32[8,32,128]{2,1,0:T(8,128)} %col_slots.1), calls=%async_computation.1 | async-start | bytes 262144 | tf_op jit(solution)/shard_map/all_to_all | solution.py:430
  121.9 104.8 %collective-permute-start.24 = (f32[128,512]{1,0:T(8,128)S(1)}, f32[128,512]{1,0:T(8,128)S(1)}, u32[]{:S(2)}, u32[]{:S(2)}) collective-permute-start(f32[128,512]{1,0:T(8,128)S(1)} %get-tuple-element.24), channel_id=1, source_target_pairs={{0,8},{8,16},{16,24},{24,32},{32,40},{40,48},{48,56},{56,0},{1,9},... | collective-permute-start | bytes 786440 | tf_op jit(solution)/shard_map/ppermute | solution.py:17
  149.3 96.4 %collective-permute-start.25 = (f32[128,512]{1,0:T(8,128)S(1)}, f32[128,512]{1,0:T(8,128)S(1)}, u32[]{:S(2)}, u32[]{:S(2)}) collective-permute-start(f32[128,512]{1,0:T(8,128)S(1)} %get-tuple-element.25), channel_id=1, source_target_pairs={{0,16},{8,24},{16,32},{24,40},{32,48},{40,56},{48,0},{56,8},{1,17}... | collective-permute-start | bytes 786440 | tf_op jit(solution)/shard_map/ppermute | solution.py:17
  171.2 156.6 %all-to-all-start = ((f32[8,32,128]{2,1,0:T(8,128)}), f32[8,32,128]{2,1,0:T(8,128)S(1)}, u32[]{:S(2)}, u32[]{:S(2)}) async-start(f32[8,32,128]{2,1,0:T(8,128)} %row_slots.1), calls=%async_computation | async-start | bytes 262144 | tf_op jit(solution)/shard_map/all_to_all | solution.py:416
  181.5 84.8 %collective-permute-start.26 = (f32[128,512]{1,0:T(8,128)}, f32[128,512]{1,0:T(8,128)S(1)}, u32[]{:S(2)}, u32[]{:S(2)}) collective-permute-start(f32[128,512]{1,0:T(8,128)} %get-tuple-element.26), channel_id=1, source_target_pairs={{0,24},{8,32},{16,40},{24,48},{32,56},{40,0},{48,8},{56,16},{1,25}... | collective-permute-start | bytes 786440 | tf_op jit(solution)/shard_map/ppermute | solution.py:17
  204.6 64.1 %collective-permute-start.27 = (f32[128,512]{1,0:T(8,128)}, f32[128,512]{1,0:T(8,128)S(1)}, u32[]{:S(2)}, u32[]{:S(2)}) collective-permute-start(f32[128,512]{1,0:T(8,128)} %get-tuple-element.27), channel_id=1, source_target_pairs={{0,32},{8,40},{16,48},{24,56},{32,0},{40,8},{48,16},{56,24},{1,33}... | collective-permute-start | bytes 786440 | tf_op jit(solution)/shard_map/ppermute | solution.py:17
  207.6 61.2 %collective-permute-start.28 = (f32[128,512]{1,0:T(8,128)S(1)}, f32[128,512]{1,0:T(8,128)S(1)}, u32[]{:S(2)}, u32[]{:S(2)}) collective-permute-start(f32[128,512]{1,0:T(8,128)S(1)} %get-tuple-element.28), channel_id=1, source_target_pairs={{0,40},{8,48},{16,56},{24,0},{32,8},{40,16},{48,24},{56,32},{1,41}... | collective-permute-start | bytes 786440 | tf_op jit(solution)/shard_map/ppermute | solution.py:17
  226.7 42.1 %collective-permute-start.29 = (f32[128,512]{1,0:T(8,128)S(1)}, f32[128,512]{1,0:T(8,128)S(1)}, u32[]{:S(2)}, u32[]{:S(2)}) collective-permute-start(f32[128,512]{1,0:T(8,128)S(1)} %get-tuple-element.29), channel_id=1, source_target_pairs={{0,48},{8,56},{16,0},{24,8},{32,16},{40,24},{48,32},{56,40},{1,49}... | collective-permute-start | bytes 786440 | tf_op jit(solution)/shard_map/ppermute | solution.py:17
  245.7 46.7 %collective-permute-start.30 = (f32[128,512]{1,0:T(8,128)S(1)}, f32[128,512]{1,0:T(8,128)S(1)}, u32[]{:S(2)}, u32[]{:S(2)}) collective-permute-start(f32[128,512]{1,0:T(8,128)S(1)} %get-tuple-element.30), channel_id=1, source_target_pairs={{0,56},{8,0},{16,8},{24,16},{32,24},{40,32},{48,40},{56,48},{1,57}... | collective-permute-start | bytes 786440 | tf_op jit(solution)/shard_map/ppermute | solution.py:17
  266.3 63.2 %collective-permute-start.19 = (f32[4,32,128]{2,1,0:T(8,128)S(1)}, f32[4,32,128]{2,1,0:T(8,128)}, u32[]{:S(2)}, u32[]{:S(2)}) collective-permute-start(f32[4,32,128]{2,1,0:T(8,128)S(1)} %get-tuple-element.22), channel_id=1, source_target_pairs={{0,64},{64,0},{128,192},{192,128},{256,320},{320,256},{384,448},{4... | collective-permute-start | bytes 196616 | tf_op jit(solution)/shard_map/ppermute | solution.py:17
  297.8 157.1 %collective-permute-start.31 = (f32[4,128,128]{2,1,0:T(8,128)}, f32[4,128,128]{2,1,0:T(8,128)S(1)}, u32[]{:S(2)}, u32[]{:S(2)}) collective-permute-start(f32[4,128,128]{2,1,0:T(8,128)} %get-tuple-element.32), channel_id=1, source_target_pairs={{0,1},{1,2},{2,3},{3,4},{4,5},{5,6},{6,7},{7,0},{8,9},{9,10},{10,1... | collective-permute-start | bytes 786440 | tf_op jit(solution)/shard_map/ppermute | solution.py:17
  300.5 173.5 %collective-permute-start.32 = (f32[4,128,128]{2,1,0:T(8,128)}, f32[4,128,128]{2,1,0:T(8,128)S(1)}, u32[]{:S(2)}, u32[]{:S(2)}) collective-permute-start(f32[4,128,128]{2,1,0:T(8,128)} %get-tuple-element.33), channel_id=1, source_target_pairs={{0,2},{1,3},{2,4},{3,5},{4,6},{5,7},{6,0},{7,1},{8,10},{9,11},{10,... | collective-permute-start | bytes 786440 | tf_op jit(solution)/shard_map/ppermute | solution.py:17
  309.9 183.0 %collective-permute-start.33 = (f32[4,128,128]{2,1,0:T(8,128)}, f32[4,128,128]{2,1,0:T(8,128)S(1)}, u32[]{:S(2)}, u32[]{:S(2)}) collective-permute-start(f32[4,128,128]{2,1,0:T(8,128)} %get-tuple-element.34), channel_id=1, source_target_pairs={{0,3},{1,4},{2,5},{3,6},{4,7},{5,0},{6,1},{7,2},{8,11},{9,12},{10,... | collective-permute-start | bytes 786440 | tf_op jit(solution)/shard_map/ppermute | solution.py:17
  311.9 183.9 %collective-permute-start.34 = (f32[4,128,128]{2,1,0:T(8,128)}, f32[4,128,128]{2,1,0:T(8,128)S(1)}, u32[]{:S(2)}, u32[]{:S(2)}) collective-permute-start(f32[4,128,128]{2,1,0:T(8,128)} %get-tuple-element.35), channel_id=1, source_target_pairs={{0,4},{1,5},{2,6},{3,7},{4,0},{5,1},{6,2},{7,3},{8,12},{9,13},{10,... | collective-permute-start | bytes 786440 | tf_op jit(solution)/shard_map/ppermute | solution.py:17
  329.4 33.7 %collective-permute-start.13 = (f32[1,4,32,128]{3,2,1,0:T(8,128)S(1)}, f32[1,4,32,128]{3,2,1,0:T(8,128)S(1)}, u32[]{:S(2)}, u32[]{:S(2)}) collective-permute-start(f32[1,4,32,128]{3,2,1,0:T(8,128)S(1)} %bitcast.63), channel_id=1, source_target_pairs={{0,4},{1,5},{2,6},{3,7},{4,0},{5,1},{6,2},{7,3},{8,12},{9,13},{10,... | collective-permute-start | bytes 196616 | tf_op jit(solution)/shard_map/ppermute | solution.py:17
  363.2 38.8 %collective-permute-start.20 = (f32[1,2,4,32,128]{4,3,2,1,0:T(8,128)S(1)}, f32[1,2,4,32,128]{4,3,2,1,0:T(8,128)S(1)}, u32[]{:S(2)}, u32[]{:S(2)}) collective-permute-start(f32[1,2,4,32,128]{4,3,2,1,0:T(8,128)S(1)} %maximum_bitcast_fusion.1), channel_id=1, source_target_pairs={{0,8},{8,0},{16,24},{24,16},{32,40},{40,32},{48,56},{56,48},{1,9},... | collective-permute-start | bytes 393224 | tf_op jit(solution)/shard_map/ppermute | solution.py:17
  402.0 7.4 %collective-permute-start.14 = (f32[2,4,32,128]{3,2,1,0:T(8,128)S(1)}, f32[2,4,32,128]{3,2,1,0:T(8,128)S(1)}, u32[]{:S(2)}, u32[]{:S(2)}) collective-permute-start(f32[2,4,32,128]{3,2,1,0:T(8,128)S(1)} %pad_maximum_fusion.4), channel_id=1, source_target_pairs={{0,2},{1,3},{2,0},{3,1},{4,6},{5,7},{6,4},{7,5},{8,10},{9,11},{10,... | collective-permute-start | bytes 393224 | tf_op jit(solution)/shard_map/ppermute | solution.py:17
  409.4 25.5 %collective-permute-start.21 = (f32[2,2,4,32,128]{4,3,2,1,0:T(8,128)S(1)}, f32[2,2,4,32,128]{4,3,2,1,0:T(8,128)S(1)}, u32[]{:S(2)}, u32[]{:S(2)}) collective-permute-start(f32[2,2,4,32,128]{4,3,2,1,0:T(8,128)S(1)} %pad_maximum_fusion.3), channel_id=1, source_target_pairs={{0,16},{8,24},{16,0},{24,8},{32,48},{40,56},{48,32},{56,40},{1,17}... | collective-permute-start | bytes 786440 | tf_op jit(solution)/shard_map/ppermute | solution.py:17
  434.9 63.9 %collective-permute-start.35 = (f32[4,128,128]{2,1,0:T(8,128)S(1)}, f32[4,128,128]{2,1,0:T(8,128)S(1)}, u32[]{:S(2)}, u32[]{:S(2)}) collective-permute-start(f32[4,128,128]{2,1,0:T(8,128)S(1)} %copy-done.14), channel_id=1, source_target_pairs={{0,5},{1,6},{2,7},{3,0},{4,1},{5,2},{6,3},{7,4},{8,13},{9,14},{10,... | collective-permute-start | bytes 786440 | tf_op jit(solution)/shard_map/ppermute | solution.py:17
  454.9 43.8 %collective-permute-start.36 = (f32[4,128,128]{2,1,0:T(8,128)S(1)}, f32[4,128,128]{2,1,0:T(8,128)S(1)}, u32[]{:S(2)}, u32[]{:S(2)}) collective-permute-start(f32[4,128,128]{2,1,0:T(8,128)S(1)} %copy-done.12), channel_id=1, source_target_pairs={{0,6},{1,7},{2,0},{3,1},{4,2},{5,3},{6,4},{7,5},{8,14},{9,15},{10,... | collective-permute-start | bytes 786440 | tf_op jit(solution)/shard_map/ppermute | solution.py:17
  474.0 26.9 %collective-permute-start.37 = (f32[4,128,128]{2,1,0:T(8,128)S(1)}, f32[4,128,128]{2,1,0:T(8,128)S(1)}, u32[]{:S(2)}, u32[]{:S(2)}) collective-permute-start(f32[4,128,128]{2,1,0:T(8,128)S(1)} %copy-done.10), channel_id=1, source_target_pairs={{0,7},{1,0},{2,1},{3,2},{4,3},{5,4},{6,5},{7,6},{8,15},{9,8},{10,9... | collective-permute-start | bytes 786440 | tf_op jit(solution)/shard_map/ppermute | solution.py:17
  493.0 28.5 %collective-permute-start.15 = (f32[4,4,32,128]{3,2,1,0:T(8,128)}, f32[4,4,32,128]{3,2,1,0:T(8,128)}, u32[]{:S(2)}, u32[]{:S(2)}) collective-permute-start(f32[4,4,32,128]{3,2,1,0:T(8,128)} %pad_maximum_fusion.2), channel_id=1, source_target_pairs={{0,1},{1,0},{2,3},{3,2},{4,5},{5,4},{6,7},{7,6},{8,9},{9,8},{10,11... | collective-permute-start | bytes 786440 | tf_op jit(solution)/shard_map/ppermute | solution.py:17
  495.8 29.7 %collective-permute-start.22 = (f32[4,2,4,32,128]{4,3,2,1,0:T(8,128)}, f32[4,2,4,32,128]{4,3,2,1,0:T(8,128)}, u32[]{:S(2)}, u32[]{:S(2)}) collective-permute-start(f32[4,2,4,32,128]{4,3,2,1,0:T(8,128)} %pad_maximum_fusion.1), channel_id=1, source_target_pairs={{0,32},{8,40},{16,48},{24,56},{32,0},{40,8},{48,16},{56,24},{1,33}... | collective-permute-start | bytes 1572872 | tf_op jit(solution)/shard_map/ppermute | solution.py:17
  502.5 27.1 %collective-permute-start.38 = (f32[4,4,128,128]{3,2,1,0:T(8,128)S(1)}, f32[4,4,128,128]{3,2,1,0:T(8,128)S(1)}, u32[]{:S(2)}, u32[]{:S(2)}) collective-permute-start(f32[4,4,128,128]{3,2,1,0:T(8,128)S(1)} %other.1), channel_id=1, source_target_pairs={{0,64},{64,0},{128,192},{192,128},{256,320},{320,256},{384,448},{4... | collective-permute-start | bytes 3145736 | tf_op jit(solution)/shard_map/ppermute | solution.py:17
  523.1 5.4 collective-permute-start.23
  534.2 5.7 collective-permute-start.40
  538.5 5.3 collective-permute-start.47
  540.8 8.5 %collective-permute-start.54 = (f32[256,512]{1,0:T(8,128)}, f32[256,512]{1,0:T(8,128)}, u32[]{:S(2)}, u32[]{:S(2)}) collective-permute-start(f32[256,512]{1,0:T(8,128)} %slice.44), channel_id=1, source_target_pairs={{0,32},{1,33},{2,34},{3,35},{4,36},{5,37},{6,38},{7,39},{64,96},{6... | collective-permute-start | bytes 1572872 | tf_op jit(solution)/shard_map/ppermute | solution.py:17
  542.3 9.2 %collective-permute-start.41 = (f32[1024,256]{1,0:T(8,128)S(1)}, f32[1024,256]{1,0:T(8,128)}, u32[]{:S(2)}, u32[]{:S(2)}) collective-permute-start(f32[1024,256]{1,0:T(8,128)S(1)} %broadcast_select_fusion.1), channel_id=1, source_target_pairs={{0,1},{2,3},{4,5},{6,7},{128,129},{130,131},{132,133},{134,135},{2... | collective-permute-start | bytes 3145736 | tf_op jit(solution)/shard_map/ppermute | solution.py:17
  549.4 22.6 %collective-permute-start.55 = (f32[256,512]{1,0:T(8,128)S(1)}, f32[256,512]{1,0:T(8,128)S(1)}, u32[]{:S(2)}, u32[]{:S(2)}) collective-permute-start(f32[256,512]{1,0:T(8,128)S(1)} %broadcast_select_fusion.3), channel_id=1, source_target_pairs={{0,16},{32,48},{1,17},{33,49},{2,18},{34,50},{3,19},{35,51},{4,20}... | collective-permute-start | bytes 1572872 | tf_op jit(solution)/shard_map/ppermute | solution.py:17
  550.7 24.2 %collective-permute-start.52 = (f32[256,256]{1,0:T(8,128)S(1)}, f32[256,256]{1,0:T(8,128)S(1)}, u32[]{:S(2)}, u32[]{:S(2)}) collective-permute-start(f32[256,256]{1,0:T(8,128)S(1)} %broadcast_select_fusion.16), channel_id=1, source_target_pairs={{0,2},{4,6},{8,10},{12,14},{16,18},{20,22},{24,26},{28,30},{32,34}... | collective-permute-start | bytes 786440 | tf_op jit(solution)/shard_map/ppermute | solution.py:17
  552.8 125.2 %collective-permute-start.42 = (f32[1024,256]{1,0:T(8,128)S(1)}, f32[1024,256]{1,0:T(8,128)}, u32[]{:S(2)}, u32[]{:S(2)}) collective-permute-start(f32[1024,256]{1,0:T(8,128)S(1)} %broadcast_select_fusion.2), channel_id=1, source_target_pairs={{0,64},{128,192},{256,320},{384,448},{1,65},{129,193},{257,321},{3... | collective-permute-start | bytes 3145736 | tf_op jit(solution)/shard_map/ppermute | solution.py:17
  572.9 103.4 %collective-permute-start.56 = (f32[256,512]{1,0:T(8,128)}, f32[256,512]{1,0:T(8,128)}, u32[]{:S(2)}, u32[]{:S(2)}) collective-permute-start(f32[256,512]{1,0:T(8,128)} %broadcast_select_fusion.5), channel_id=1, source_target_pairs={{0,8},{16,24},{32,40},{48,56},{1,9},{17,25},{33,41},{49,57},{2,10}... | collective-permute-start | bytes 1572872 | tf_op jit(solution)/shard_map/ppermute | solution.py:17
  575.0 87.1 %collective-permute-start.53 = (f32[256,256]{1,0:T(8,128)S(1)}, f32[256,256]{1,0:T(8,128)}, u32[]{:S(2)}, u32[]{:S(2)}) collective-permute-start(f32[256,256]{1,0:T(8,128)S(1)} %broadcast_select_fusion.18), channel_id=1, source_target_pairs={{0,1},{2,3},{4,5},{6,7},{8,9},{10,11},{12,13},{14,15},{16,17},{18,... | collective-permute-start | bytes 786440 | tf_op jit(solution)/shard_map/ppermute | solution.py:17
  (32 other events, 909.6 us)

commit v3 on v2

--- a/solution.py
+++ b/solution.py
@@ -15,15 +15,6 @@
 
 def send(value, axes, pairs):
     return lax.ppermute(value, axes, pairs)
-
-
-def tree(value, axis, rounds):
-    index = lax.axis_index(axis)
-    for pairs in rounds:
-        got = send(value, axis, pairs)
-        is_target = functools.reduce(jnp.logical_or, [index == t for _, t in pairs])
-        value = jnp.where(is_target, got, value)
-    return value
 
 
 HALVING = ([(0, 4)], [(0, 2), (4, 6)], [(0, 1), (2, 3), (4, 5), (6, 7)])
@@ -328,26 +319,6 @@
     )
 
 
-def gather_doubling(value, axis, order):
-    index = lax.axis_index(axis)
-    size = lax.axis_size(axis)
-    value = value[None]
-    done = []
-    for bit in order:
-        got = send(value, axis, [(i, i ^ (1 << bit)) for i in range(size)])
-        upper = (index >> bit) & 1
-        low = jnp.where(upper == 0, value, got)
-        high = jnp.where(upper == 0, got, value)
-        value = jnp.concatenate([low, high], axis=0)
-        done.insert(0, bit)
-    bits = len(order)
-    shape = value.shape[1:]
-    value = value.reshape((2,) * bits + shape)
-    perm = [done.index(b) for b in range(bits - 1, -1, -1)]
-    value = jnp.transpose(value, perm + list(range(bits, bits + len(shape))))
-    return value.reshape((size,) + shape)
-
-
 def shards(child_front, parent_front, block_map):
     leaf_id = lax.axis_index("leaf")
     row_id = lax.axis_index("row")
@@ -371,77 +342,133 @@
     cap = -(-count // row_count)
     swap = [(i, i ^ 1) for i in range(leaf_count)]
 
+    bulk = []
+
+    def step(operands, lag=1):
+        operands = list(operands)
+        if len(bulk) > lag:
+            tied = lax.optimization_barrier((operands, bulk[-1 - lag]))
+            operands, bulk[-1 - lag] = tied
+        else:
+            operands = lax.optimization_barrier(operands)
+        return operands
+
+    def only(cell, got, value, targets):
+        index = lax.axis_index(cell)
+        hit = functools.reduce(jnp.logical_or, [index == t for t in targets])
+        return jnp.where(hit, got, value)
+
     strips = kernel_call(
         functools.partial(strips_kernel, (row_span, first, row_blocks, row_count)),
         "strips", [(BLK, child_cols)] * row_count, 2, 1,
         [pltpu.VMEM((row_count, BLK, child_cols), jnp.float32)],
     )(ids, own_map, child_block)
-
-    diagonal = child_block[:width, :width]
-    spread = [send(diagonal, ("row", "col"), [(0, r * col_count)]) for r in range(1, row_count)]
-    diagonal = jnp.where(row_id == 0, diagonal, functools.reduce(jnp.add, spread))
-    diagonal = tree(diagonal, "col", HALVING)
-    slab = tree(child_block[:, :width], "col", HALVING)
-    top = tree(child_block[:width], "row", HALVING)
-
-    got = [strips[0]] + [
-        send(strips[s], "row", [(i, (i + s) % row_count) for i in range(row_count)])
-        for s in range(1, row_count)
-    ]
+    strips = list(strips)
+    row_pairs = [[(i, (i + s) % row_count) for i in range(row_count)] for s in range(row_count)]
+    col_pairs = [[(i, (i + t) % col_count) for i in range(col_count)] for t in range(col_count)]
+
+    def by_rows(pairs):
+        return [(r * col_count, q * col_count) for r, q in pairs]
+
+    diagonal, slab, top = child_block[:width, :width], child_block[:, :width], child_block[:width]
+    for number, pairs in enumerate(HALVING):
+        shift = number + 1
+        diagonal, slab, top, strips[shift] = step([diagonal, slab, top, strips[shift]])
+        bulk.append(send(strips[shift], "row", row_pairs[shift]))
+        targets = [t for _, t in pairs]
+        diagonal = only("row", send(diagonal, ("row", "col"), by_rows(pairs)), diagonal, targets)
+        slab = only("col", send(slab, "col", pairs), slab, targets)
+        top = only("row", send(top, "row", pairs), top, targets)
+    for number, pairs in enumerate(HALVING):
+        shift = number + 4
+        diagonal, slab, top, strips[shift] = step([diagonal, slab, top, strips[shift]])
+        bulk.append(send(strips[shift], "row", row_pairs[shift]))
+        diagonal = only("col", send(diagonal, "col", pairs), diagonal, [t for _, t in pairs])
+    diagonal, slab, top, strips[7] = step([diagonal, slab, top, strips[7]])
+    bulk.append(send(strips[7], "row", row_pairs[7]))
+    inverse = inverse_factor(diagonal)
+    cols_factor = jnp.dot(inverse, top, precision=HIGHEST)
+    out_width = width // col_count
+    share = lax.dynamic_slice_in_dim(inverse, col_id * out_width, out_width, 0)
+    child_out = lax.dot_general(share, slab, (((1,), (1,)), ((), ())), precision=HIGHEST)
+    piece = (out_width, BLK)
+    row_slots = kernel_call(
+        functools.partial(row_slots_kernel, (row_span, first, row_blocks)),
+        "row_slots", (row_count,) + piece, 2, 1,
+    )(ids, own_map, child_out)
+    col_share = lax.dynamic_slice_in_dim(cols_factor, row_id * out_width, out_width, 0)
+    col_slots = kernel_call(
+        functools.partial(col_slots_kernel, (col_span, first, col_blocks, col_count)),
+        "col_slots", (col_count,) + piece, 2, 1,
+    )(ids, own_map, col_share)
+    row_slots, col_slots, got = lax.optimization_barrier((row_slots, col_slots, bulk))
+    got = [strips[0]] + list(got)
+
     tables = [pltpu.SMEM((count,), jnp.int32), pltpu.SMEM((cap,), jnp.int32)]
-    tiles = kernel_call(
+    tiles = list(kernel_call(
         functools.partial(
             tiles_kernel,
             (row_span, col_span, first, row_blocks, col_blocks, row_count, col_count, count),
         ),
         "tiles", [(cap, BLK, BLK)] * col_count, 2, row_count,
         [pltpu.VMEM((col_count, cap, BLK, BLK), jnp.float32)] + tables,
-    )(ids, own_map, *got)
-    landed = [tiles[0]] + [
-        send(tiles[t], "col", [(i, (i + t) % col_count) for i in range(col_count)])
-        for t in range(1, col_count)
-    ]
-
-    inverse = inverse_factor(diagonal)
-    cols_factor = jnp.dot(inverse, top, precision=HIGHEST)
-    out_width = width // col_count
-    share = lax.dynamic_slice_in_dim(inverse, col_id * out_width, out_width, 0)
-    child_out = lax.dot_general(share, slab, (((1,), (1,)), ((), ())), precision=HIGHEST)
-    piece = (out_width, BLK)
-
-    row_slots = kernel_call(
-        functools.partial(row_slots_kernel, (row_span, first, row_blocks)),
-        "row_slots", (row_count,) + piece, 2, 1,
-    )(ids, own_map, child_out)
+    )(ids, own_map, *got))
+    bulk = []
+
+    tiles[1], tiles[2], row_slots, col_slots = lax.optimization_barrier(
+        (tiles[1], tiles[2], row_slots, col_slots)
+    )
+    bulk.append(send(tiles[1], "col", col_pairs[1]))
     row_got = lax.all_to_all(row_slots, "row", 0, 0, tiled=True)
+    tiles[2], col_slots, row_got = lax.optimization_barrier((tiles[2], col_slots, row_got))
+    bulk.append(send(tiles[2], "col", col_pairs[2]))
+    col_got = lax.all_to_all(col_slots, "col", 0, 0, tiled=True)
     row_panel = kernel_call(
         functools.partial(row_pick_kernel, (row_span, first, row_blocks, count)),
         "row_pick", (cap,) + piece, 2, 1, tables,
     )(ids, own_map, row_got)
-    row_panel = gather_doubling(row_panel, "col", (2, 1, 0))
-    row_panel = jnp.transpose(row_panel, (0, 2, 1, 3)).reshape(width, cap * BLK)
-    pair_row_panel = send(row_panel, "leaf", swap)
-
-    col_share = lax.dynamic_slice_in_dim(cols_factor, row_id * out_width, out_width, 0)
-    col_slots = kernel_call(
-        functools.partial(col_slots_kernel, (col_span, first, col_blocks, col_count)),
-        "col_slots", (col_count,) + piece, 2, 1,
-    )(ids, own_map, col_share)
-    col_got = lax.all_to_all(col_slots, "col", 0, 0, tiled=True)
     own_cols, other_cols = kernel_call(
         functools.partial(col_pick_kernel, (col_span, first, col_blocks, col_count, count)),
         "col_pick", [(col_span,) + piece] * 2, 2, 1,
     )(ids, own_map, col_got)
+
+    def doubled(value, axis, bit):
+        got = send(value, axis, [(i, i ^ (1 << bit)) for i in range(lax.axis_size(axis))])
+        upper = (lax.axis_index(axis) >> bit) & 1
+        low = jnp.where(upper == 0, value, got)
+        high = jnp.where(upper == 0, got, value)
+        return jnp.stack([low, high])
+
+    row_panel, other_cols, tiles[3] = step([row_panel, other_cols, tiles[3]])
+    bulk.append(send(tiles[3], "col", col_pairs[3]))
+    row_panel = doubled(row_panel, "col", 2)
     col_panels = jnp.stack([own_cols, send(other_cols, "leaf", swap)])
-    col_panels = gather_doubling(col_panels, "row", (0, 1, 2))
-    col_panels = jnp.transpose(col_panels, (1, 0, 3, 2, 4)).reshape(2, width, col_span * BLK)
+    row_panel, col_panels, tiles[4] = step([row_panel, col_panels, tiles[4]])
+    bulk.append(send(tiles[4], "col", col_pairs[4]))
+    row_panel = doubled(row_panel, "col", 1)
+    col_panels = doubled(col_panels, "row", 0)
+    row_panel, col_panels, tiles[5] = step([row_panel, col_panels, tiles[5]])
+    bulk.append(send(tiles[5], "col", col_pairs[5]))
+    row_panel = doubled(row_panel, "col", 0)
+    col_panels = doubled(col_panels, "row", 1)
+    row_panel, col_panels, tiles[6] = step([row_panel, col_panels, tiles[6]])
+    bulk.append(send(tiles[6], "col", col_pairs[6]))
+    row_panel = jnp.transpose(row_panel, (2, 1, 0, 4, 3, 5)).reshape(width, cap * BLK)
+    pair_row_panel = send(row_panel, "leaf", swap)
+    col_panels = doubled(col_panels, "row", 2)
+    row_panel, pair_row_panel, col_panels, tiles[7] = step(
+        [row_panel, pair_row_panel, col_panels, tiles[7]]
+    )
+    bulk.append(send(tiles[7], "col", col_pairs[7]))
+    col_panels = jnp.transpose(col_panels, (3, 0, 1, 2, 5, 4, 6))
+    col_panels = col_panels.reshape(2, width, col_span * BLK)
 
     def product(rows, cols):
         return lax.dot_general(rows, cols, (((0,), (0,)), ((), ())), precision=HIGHEST)
 
     own_product = product(row_panel, col_panels[0])
     pair_product = product(pair_row_panel, col_panels[1])
-
+    landed = [tiles[0]] + bulk
     other = kernel_call(
         functools.partial(other_kernel, (col_span, first, col_blocks, col_count)),
         "other", (col_span, cap, BLK, BLK), 2, col_count,
@@ -457,25 +484,45 @@
 
     parent_order = parent_rows * row_count
     parent_width = parent_cols // 2
-    diagonal = assembled[:parent_width, :parent_width]
     even = range(0, leaf_count, 2)
     grid = row_count * col_count
-    spread = [
-        send(diagonal, ("leaf", "row", "col"), [(l * grid, l * grid + r * col_count) for l in even])
-        for r in range(1, row_count)
-    ]
-    diagonal = jnp.where(row_id == 0, diagonal, functools.reduce(jnp.add, spread))
     across = [(l, l + 1) for l in even]
+    diagonal = assembled[:parent_width, :parent_width]
+    slab, top = assembled[:, :parent_width], assembled[:parent_width]
+    diagonal, slab, top = lax.optimization_barrier((diagonal, slab, top))
+
+    def spread_rows(value, pairs):
+        moves = [
+            (l * grid + r * col_count, l * grid + q * col_count) for l in even for r, q in pairs
+        ]
+        return send(value, ("leaf", "row", "col"), moves)
+
+    def spread_cols(value, pairs):
+        moves = [(l * col_count + r, l * col_count + q) for l in even for r, q in pairs]
+        return only("col", send(value, ("leaf", "col"), moves), value, [q for _, q in pairs])
+
+    def spread_top(value, pairs):
+        return only("row", send(value, "row", pairs), value, [q for _, q in pairs])
+
+    fan = [spread_rows(diagonal, [(0, q)]) for q in (2, 4, 6)]
+    diagonal = only("row", functools.reduce(jnp.add, fan), diagonal, (2, 4, 6))
+    slab = spread_cols(slab, HALVING[0])
+    (diagonal,) = lax.optimization_barrier([diagonal])
+    zhi = [(0, 1), (2, 3), (4, 5), (6, 7)]
+    diagonal = only("row", spread_rows(diagonal, zhi), diagonal, (1, 3, 5, 7))
+    top = spread_top(top, HALVING[0])
+    diagonal, slab, top = lax.optimization_barrier((diagonal, slab, top))
+    diagonal = spread_cols(diagonal, HALVING[0])
+    slab = spread_cols(slab, HALVING[1])
+    top = spread_top(top, HALVING[1])
+    diagonal, slab, top = lax.optimization_barrier((diagonal, slab, top))
+    diagonal = spread_cols(diagonal, HALVING[1])
+    slab = spread_cols(slab, HALVING[2])
+    top = spread_top(top, HALVING[2])
+    diagonal, slab = lax.optimization_barrier((diagonal, slab))
+    diagonal = spread_cols(diagonal, HALVING[2])
     diagonal = jnp.where(half_id == 0, diagonal, send(diagonal, "leaf", across))
-    diagonal = tree(diagonal, "col", HALVING)
-    slab = assembled[:, :parent_width]
-    for pairs in HALVING:
-        moves = [(l * col_count + s, l * col_count + t) for l in even for s, t in pairs]
-        moved = send(slab, ("leaf", "col"), moves)
-        is_target = functools.reduce(jnp.logical_or, [col_id == t for _, t in pairs])
-        slab = jnp.where(is_target, moved, slab)
     slab = jnp.where(half_id == 0, slab, send(slab, "leaf", across))
-    top = tree(assembled[:parent_width], "row", HALVING)
     inverse = inverse_factor(diagonal)
     rows_factor = lax.dot_general(slab, inverse, (((1,), (1,)), ((), ())), precision=HIGHEST)
     cols_factor = jnp.dot(inverse, top, precision=HIGHEST)

time: 687 us -> 627 us (0.913)
  the two profiles are of different devices: /device:TPU:185 before, /device:TPU:468 now
where the time goes in v3:
time: 627 us; the launch traced here: 625 us
  waiting for transfers between devices  281 us (45%)
  starting transfers between devices  241 us (38%)
  Pallas kernels  38 us (6%)
  other arithmetic  19 us (3%)
  blocking collectives  17.7 us (3%)
  matrix products  14.8 us (2%)
  local copies, waits for them, and re-layouts  11.3 us (2%)
    ppermute x50, waiting for transfers between devices, send(): return lax.ppermute(value, axes, pairs)  277 us
    ppermute x50, starting transfers between devices, send(): return lax.ppermute(value, axes, pairs)  231 us
    pallas_call x2, Pallas kernels, inverse_factor(): pl.pallas_call(inverse_factor_kernel, out_shape=jax.ShapeDtypeStruct(bloc...  24.9 us
    all_to_all x1, blocking collectives, shards(): row_got = lax.all_to_all(row_slots, 'row', 0, 0, tiled=True)  17.7 us
    select_n x22, other arithmetic, only(): return jnp.where(hit, got, value)  16.6 us
  transfers between devices with their start and end apart: 51, of which 18 were waited for; matrix products, arithmetic and copies ran while one was open for 4% of the time, Pallas kernels for 5%

profile of v3, /device:TPU:468, one launch (start us, length us, event | category | flops | bytes accessed | tf_op | source)
XLA Modules:
  0.0 625.0 jit_solution(1226049200230703240)
XLA Ops:
  12.0 2.1 broadcast_select_fusion.10
  18.2 6.0 collective-permute-start.6
  25.5 29.5 %collective-permute-done.4 = f32[512,256]{1,0:T(8,128)} collective-permute-done((f32[512,256]{1,0:T(8,128)}, f32[512,256]{1,0:T(8,128)}, u32[]{:S(2)}, u32[]{:S(2)}) %collective-permute-start.4) | collective-permute-done | bytes 524320 | tf_op jit(solution)/shard_map/ppermute | solution.py:17
  58.8 2.1 collective-permute-start.8
  60.9 6.3 %collective-permute-start.10 = (f32[128,512]{1,0:T(8,128)S(1)}, f32[128,512]{1,0:T(8,128)S(1)}, u32[]{:S(2)}, u32[]{:S(2)}) collective-permute-start(f32[128,512]{1,0:T(8,128)S(1)} %get-tuple-element.116), channel_id=1, source_target_pairs={{0,16},{8,24},{16,32},{24,40},{32,48},{40,56},{48,0},{56,8},{1,17}... | collective-permute-start | bytes 786440 | tf_op jit(solution)/shard_map/ppermute | solution.py:17
  67.2 60.1 %collective-permute-done.9 = f32[256,512]{1,0:T(8,128)} collective-permute-done((f32[256,512]{1,0:T(8,128)S(1)}, f32[256,512]{1,0:T(8,128)}, u32[]{:S(2)}, u32[]{:S(2)}) %collective-permute-start.9) | collective-permute-done | bytes 524320 | tf_op jit(solution)/shard_map/ppermute | solution.py:17
  132.1 15.2 %collective-permute-start.12 = (f32[128,512]{1,0:T(8,128)S(1)}, f32[128,512]{1,0:T(8,128)S(1)}, u32[]{:S(2)}, u32[]{:S(2)}) collective-permute-start(f32[128,512]{1,0:T(8,128)S(1)} %get-tuple-element.121), channel_id=1, source_target_pairs={{0,24},{8,32},{16,40},{24,48},{32,56},{40,0},{48,8},{56,16},{1,25}... | collective-permute-start | bytes 786440 | tf_op jit(solution)/shard_map/ppermute | solution.py:17
  147.3 5.9 collective-permute-done.12.refs_3_
  154.6 9.3 %collective-permute-start.14 = (f32[128,512]{1,0:T(8,128)S(1)}, f32[128,512]{1,0:T(8,128)S(1)}, u32[]{:S(2)}, u32[]{:S(2)}) collective-permute-start(f32[128,512]{1,0:T(8,128)S(1)} %get-tuple-element.126), channel_id=1, source_target_pairs={{0,32},{8,40},{16,48},{24,56},{32,0},{40,8},{48,16},{56,24},{1,33}... | collective-permute-start | bytes 786440 | tf_op jit(solution)/shard_map/ppermute | solution.py:17
  164.6 3.6 collective-permute-done.14.refs_4_
  168.2 2.8 collective-permute-start.15
  171.0 23.9 %collective-permute-start.16 = (f32[128,512]{1,0:T(8,128)S(1)}, f32[128,512]{1,0:T(8,128)S(1)}, u32[]{:S(2)}, u32[]{:S(2)}) collective-permute-start(f32[128,512]{1,0:T(8,128)S(1)} %get-tuple-element.131), channel_id=1, source_target_pairs={{0,40},{8,48},{16,56},{24,0},{32,8},{40,16},{48,24},{56,32},{1,41}... | collective-permute-start | bytes 786440 | tf_op jit(solution)/shard_map/ppermute | solution.py:17
  195.0 19.0 %collective-permute-start.17 = (f32[128,512]{1,0:T(8,128)S(1)}, f32[128,512]{1,0:T(8,128)S(1)}, u32[]{:S(2)}, u32[]{:S(2)}) collective-permute-start(f32[128,512]{1,0:T(8,128)S(1)} %get-tuple-element.141), channel_id=1, source_target_pairs={{0,48},{8,56},{16,0},{24,8},{32,16},{40,24},{48,32},{56,40},{1,49}... | collective-permute-start | bytes 786440 | tf_op jit(solution)/shard_map/ppermute | solution.py:17
  215.7 6.2 collective-permute-done.16.refs_5_
  221.9 12.4 %inverse_factor.2 = f32[256,256]{1,0:T(8,128)} custom-call(f32[256,256]{1,0:T(8,128)} %broadcast_select_fusion.21.a_ref), custom_call_target="tpu_custom_call" | custom-call | tf_op jit(solution)/shard_map/inverse_factor/pallas_call | solution.py:89
  234.4 17.0 %collective-permute-start.18 = (f32[128,512]{1,0:T(8,128)S(1)}, f32[128,512]{1,0:T(8,128)S(1)}, u32[]{:S(2)}, u32[]{:S(2)}) collective-permute-start(f32[128,512]{1,0:T(8,128)S(1)} %get-tuple-element.142), channel_id=1, source_target_pairs={{0,56},{8,0},{16,8},{24,16},{32,24},{40,32},{48,40},{56,48},{1,57}... | collective-permute-start | bytes 786440 | tf_op jit(solution)/shard_map/ppermute | solution.py:17
  256.4 22.6 %collective-permute-done.18.refs_7_ = f32[128,512]{1,0:T(8,128)S(1)} collective-permute-done((f32[128,512]{1,0:T(8,128)S(1)}, f32[128,512]{1,0:T(8,128)S(1)}, u32[]{:S(2)}, u32[]{:S(2)}) %collective-permute-start.18) | collective-permute-done | bytes 262176 | tf_op jit(solution)/shard_map/ppermute | solution.py:17
  279.1 2.2 tiles.1
  283.5 17.7 %all_to_all.10.got_ref = f32[8,32,128]{2,1,0:T(8,128)S(1)} all-to-all(f32[8,32,128]{2,1,0:T(8,128)S(1)} %row_slots.1), channel_id=1, replica_groups=mesh['leaf'=8,'row'=8,'col'=8] {'row'}, dimensions={0} | all-to-all | bytes 262144 | tf_op jit(solution)/shard_map/all_to_all | solution.py:422
  301.2 9.9 %all-to-all-start.1 = ((f32[8,32,128]{2,1,0:T(8,128)}), f32[8,32,128]{2,1,0:T(8,128)S(1)}, u32[]{:S(2)}, u32[]{:S(2)}) async-start(f32[8,32,128]{2,1,0:T(8,128)} %col_slots.1), calls=%async_computation.1 | async-start | bytes 262144 | tf_op jit(solution)/shard_map/all_to_all | solution.py:425
  311.1 3.4 collective-permute-start.19
  316.0 3.9 all-to-all-done.1.got_ref
  321.5 8.3 %collective-permute-start.20 = (f32[4,32,128]{2,1,0:T(8,128)S(1)}, f32[4,32,128]{2,1,0:T(8,128)S(1)}, u32[]{:S(2)}, u32[]{:S(2)}) collective-permute-start(f32[4,32,128]{2,1,0:T(8,128)S(1)} %row_pick.1), channel_id=1, source_target_pairs={{0,4},{1,5},{2,6},{3,7},{4,0},{5,1},{6,2},{7,3},{8,12},{9,13},{10,... | collective-permute-start | bytes 196616 | tf_op jit(solution)/shard_map/ppermute | solution.py:17
  329.9 3.7 collective-permute-start.22
  335.5 3.2 collective-permute-done.20
  338.8 4.5 collective-permute-done.22.refs_2_
  343.2 15.4 %collective-permute-start.24 = (f32[2,4,32,128]{3,2,1,0:T(8,128)S(1)}, f32[2,4,32,128]{3,2,1,0:T(8,128)S(1)}, u32[]{:S(2)}, u32[]{:S(2)}) collective-permute-start(f32[2,4,32,128]{3,2,1,0:T(8,128)S(1)} %pad_maximum_fusion.6), channel_id=1, source_target_pairs={{0,8},{8,0},{16,24},{24,16},{32,40},{40,32},{48,56},{56,48},{1,9},... | collective-permute-start | bytes 393224 | tf_op jit(solution)/shard_map/ppermute | solution.py:17
  358.6 13.3 %collective-permute-start.25 = (f32[4,128,128]{2,1,0:T(8,128)S(1)}, f32[4,128,128]{2,1,0:T(8,128)S(1)}, u32[]{:S(2)}, u32[]{:S(2)}) collective-permute-start(f32[4,128,128]{2,1,0:T(8,128)S(1)} %get-tuple-element.170), channel_id=1, source_target_pairs={{0,3},{1,4},{2,5},{3,6},{4,7},{5,0},{6,1},{7,2},{8,11},{9,12},{10,... | collective-permute-start | bytes 786440 | tf_op jit(solution)/shard_map/ppermute | solution.py:17
  371.9 10.2 %collective-permute-start.23 = (f32[2,4,32,128]{3,2,1,0:T(8,128)S(1)}, f32[2,4,32,128]{3,2,1,0:T(8,128)S(1)}, u32[]{:S(2)}, u32[]{:S(2)}) collective-permute-start(f32[2,4,32,128]{3,2,1,0:T(8,128)S(1)} %pad_maximum_fusion.5), channel_id=1, source_target_pairs={{0,2},{1,3},{2,0},{3,1},{4,6},{5,7},{6,4},{7,5},{8,10},{9,11},{10,... | collective-permute-start | bytes 393224 | tf_op jit(solution)/shard_map/ppermute | solution.py:17
  382.1 5.2 collective-permute-done.23
  387.4 4.3 collective-permute-start.27
  391.7 8.6 %collective-permute-start.26 = (f32[2,2,4,32,128]{4,3,2,1,0:T(8,128)S(1)}, f32[2,2,4,32,128]{4,3,2,1,0:T(8,128)S(1)}, u32[]{:S(2)}, u32[]{:S(2)}) collective-permute-start(f32[2,2,4,32,128]{4,3,2,1,0:T(8,128)S(1)} %get-tuple-element.171), channel_id=1, source_target_pairs={{0,1},{1,0},{2,3},{3,2},{4,5},{5,4},{6,7},{7,6},{8,9},{9,8},{10,11... | collective-permute-start | bytes 786440 | tf_op jit(solution)/shard_map/ppermute | solution.py:17
  400.4 10.0 %collective-permute-start.28 = (f32[4,128,128]{2,1,0:T(8,128)S(1)}, f32[4,128,128]{2,1,0:T(8,128)S(1)}, u32[]{:S(2)}, u32[]{:S(2)}) collective-permute-start(f32[4,128,128]{2,1,0:T(8,128)S(1)} %copy-done.10), channel_id=1, source_target_pairs={{0,4},{1,5},{2,6},{3,7},{4,0},{5,1},{6,2},{7,3},{8,12},{9,13},{10,... | collective-permute-start | bytes 786440 | tf_op jit(solution)/shard_map/ppermute | solution.py:17
  410.6 10.7 %collective-permute-done.28.refs_4_ = f32[4,128,128]{2,1,0:T(8,128)S(1)} collective-permute-done((f32[4,128,128]{2,1,0:T(8,128)S(1)}, f32[4,128,128]{2,1,0:T(8,128)S(1)}, u32[]{:S(2)}, u32[]{:S(2)}) %collective-permute-start.28) | collective-permute-done | bytes 262176 | tf_op jit(solution)/shard_map/ppermute | solution.py:17
  421.3 3.0 collective-permute-start.30
  429.5 7.9 %collective-permute-start.32 = (f32[4,128,128]{2,1,0:T(8,128)S(1)}, f32[4,128,128]{2,1,0:T(8,128)S(1)}, u32[]{:S(2)}, u32[]{:S(2)}) collective-permute-start(f32[4,128,128]{2,1,0:T(8,128)S(1)} %copy-done.6), channel_id=1, source_target_pairs={{0,6},{1,7},{2,0},{3,1},{4,2},{5,3},{6,4},{7,5},{8,14},{9,15},{10,... | collective-permute-start | bytes 786440 | tf_op jit(solution)/shard_map/ppermute | solution.py:17
  438.8 16.0 %collective-permute-done.31.refs_5_ = f32[4,128,128]{2,1,0:T(8,128)S(1)} collective-permute-done((f32[4,128,128]{2,1,0:T(8,128)S(1)}, f32[4,128,128]{2,1,0:T(8,128)S(1)}, u32[]{:S(2)}, u32[]{:S(2)}) %collective-permute-start.31) | collective-permute-done | bytes 262176 | tf_op jit(solution)/shard_map/ppermute | solution.py:17
  456.7 18.7 %collective-permute-done.33.refs_7_ = f32[4,128,128]{2,1,0:T(8,128)S(1)} collective-permute-done((f32[4,128,128]{2,1,0:T(8,128)S(1)}, f32[4,128,128]{2,1,0:T(8,128)S(1)}, u32[]{:S(2)}, u32[]{:S(2)}) %collective-permute-start.33) | collective-permute-done | bytes 262176 | tf_op jit(solution)/shard_map/ppermute | solution.py:17
  479.8 2.2 fusion.2.pair_ref
  481.9 2.1 fusion.5.own_ref
  484.0 3.4 assemble.1
  502.5 22.4 %collective-permute-done.42 = f32[1024,256]{1,0:T(8,128)S(1)} collective-permute-done((f32[1024,256]{1,0:T(8,128)S(1)}, f32[1024,256]{1,0:T(8,128)S(1)}, u32[]{:S(2)}, u32[]{:S(2)}) %collective-permute-start.42) | collective-permute-done | bytes 1048608 | tf_op jit(solution)/shard_map/ppermute | solution.py:17
  527.8 50.0 %collective-permute-done.44 = f32[256,256]{1,0:T(8,128)S(1)} collective-permute-done((f32[256,256]{1,0:T(8,128)S(1)}, f32[256,256]{1,0:T(8,128)S(1)}, u32[]{:S(2)}, u32[]{:S(2)}) %collective-permute-start.44) | collective-permute-done | bytes 262176 | tf_op jit(solution)/shard_map/ppermute | solution.py:17
  579.3 2.3 collective-permute-start.46
  586.6 12.4 %inverse_factor.3 = f32[256,256]{1,0:T(8,128)} custom-call(f32[256,256]{1,0:T(8,128)} %broadcast_select_fusion.11.a_ref), custom_call_target="tpu_custom_call" | custom-call | tf_op jit(solution)/shard_map/inverse_factor/pallas_call | solution.py:89
  599.0 17.8 %collective-permute-done.49 = f32[256,512]{1,0:T(8,128)} collective-permute-done((f32[256,512]{1,0:T(8,128)}, f32[256,512]{1,0:T(8,128)}, u32[]{:S(2)}, u32[]{:S(2)}) %collective-permute-start.49) | collective-permute-done | bytes 524320 | tf_op jit(solution)/shard_map/ppermute | solution.py:17
  618.5 2.1 fusion
  621.3 3.6 subtract_select_fusion
  (154 shorter events, 80.8 us)
Async XLA Ops:
  7.2 3.7 collective-permute-start.2
  8.7 2.1 collective-permute-start
  9.3 2.7 collective-permute-start.1
  14.1 10.2 %collective-permute-start.5 = (f32[256,512]{1,0:T(8,128)S(1)}, f32[256,512]{1,0:T(8,128)}, u32[]{:S(2)}, u32[]{:S(2)}) collective-permute-start(f32[256,512]{1,0:T(8,128)S(1)} %broadcast_select_fusion.9), channel_id=1, source_target_pairs={{0,16},{32,48},{1,17},{33,49},{2,18},{34,50},{3,19},{35,51},{4,20}... | collective-permute-start | bytes 1572872 | tf_op jit(solution)/shard_map/ppermute | solution.py:17
  15.5 8.7 %collective-permute-start.3 = (f32[256,256]{1,0:T(8,128)S(1)}, f32[256,256]{1,0:T(8,128)}, u32[]{:S(2)}, u32[]{:S(2)}) collective-permute-start(f32[256,256]{1,0:T(8,128)S(1)} %broadcast_select_fusion.12), channel_id=1, source_target_pairs={{0,16},{32,48},{64,80},{96,112},{128,144},{160,176},{192,208},{224... | collective-permute-start | bytes 786440 | tf_op jit(solution)/shard_map/ppermute | solution.py:17
  16.9 38.0 %collective-permute-start.4 = (f32[512,256]{1,0:T(8,128)}, f32[512,256]{1,0:T(8,128)}, u32[]{:S(2)}, u32[]{:S(2)}) collective-permute-start(f32[512,256]{1,0:T(8,128)} %broadcast_select_fusion.10), channel_id=1, source_target_pairs={{0,2},{4,6},{8,10},{12,14},{16,18},{20,22},{24,26},{28,30},{32,34}... | collective-permute-start | bytes 1572872 | tf_op jit(solution)/shard_map/ppermute | solution.py:17
  18.2 38.6 %collective-permute-start.6 = (f32[128,512]{1,0:T(8,128)S(1)}, f32[128,512]{1,0:T(8,128)S(1)}, u32[]{:S(2)}, u32[]{:S(2)}) collective-permute-start(f32[128,512]{1,0:T(8,128)S(1)} %get-tuple-element.111), channel_id=1, source_target_pairs={{0,8},{8,16},{16,24},{24,32},{32,40},{40,48},{48,56},{56,0},{1,9},... | collective-permute-start | bytes 786440 | tf_op jit(solution)/shard_map/ppermute | solution.py:17
  56.8 70.5 %collective-permute-start.9 = (f32[256,512]{1,0:T(8,128)S(1)}, f32[256,512]{1,0:T(8,128)}, u32[]{:S(2)}, u32[]{:S(2)}) collective-permute-start(f32[256,512]{1,0:T(8,128)S(1)} %broadcast_select_fusion.6), channel_id=1, source_target_pairs={{0,8},{16,24},{32,40},{48,56},{1,9},{17,25},{33,41},{49,57},{2,10}... | collective-permute-start | bytes 1572872 | tf_op jit(solution)/shard_map/ppermute | solution.py:17
  58.1 9.1 %collective-permute-start.7 = (f32[256,256]{1,0:T(8,128)S(1)}, f32[256,256]{1,0:T(8,128)S(1)}, u32[]{:S(2)}, u32[]{:S(2)}) collective-permute-start(f32[256,256]{1,0:T(8,128)S(1)} %broadcast_select_fusion.13), channel_id=1, source_target_pairs={{0,8},{16,24},{32,40},{48,56},{64,72},{80,88},{96,104},{112,120},{... | collective-permute-start | bytes 786440 | tf_op jit(solution)/shard_map/ppermute | solution.py:17
  58.8 70.5 %collective-permute-start.8 = (f32[512,256]{1,0:T(8,128)}, f32[512,256]{1,0:T(8,128)}, u32[]{:S(2)}, u32[]{:S(2)}) collective-permute-start(f32[512,256]{1,0:T(8,128)} %broadcast_select_fusion.7), channel_id=1, source_target_pairs={{0,1},{2,3},{4,5},{6,7},{8,9},{10,11},{12,13},{14,15},{16,17},{18,... | collective-permute-start | bytes 1572872 | tf_op jit(solution)/shard_map/ppermute | solution.py:17
  60.9 70.4 %collective-permute-start.10 = (f32[128,512]{1,0:T(8,128)S(1)}, f32[128,512]{1,0:T(8,128)S(1)}, u32[]{:S(2)}, u32[]{:S(2)}) collective-permute-start(f32[128,512]{1,0:T(8,128)S(1)} %get-tuple-element.116), channel_id=1, source_target_pairs={{0,16},{8,24},{16,32},{24,40},{32,48},{40,56},{48,0},{56,8},{1,17}... | collective-permute-start | bytes 786440 | tf_op jit(solution)/shard_map/ppermute | solution.py:17
  131.2 16.0 %collective-permute-start.11 = (f32[256,256]{1,0:T(8,128)S(1)}, f32[256,256]{1,0:T(8,128)S(1)}, u32[]{:S(2)}, u32[]{:S(2)}) collective-permute-start(f32[256,256]{1,0:T(8,128)S(1)} %broadcast_select_fusion.15), channel_id=1, source_target_pairs={{0,4},{8,12},{16,20},{24,28},{32,36},{40,44},{48,52},{56,60},{64,6... | collective-permute-start | bytes 786440 | tf_op jit(solution)/shard_map/ppermute | solution.py:17
  132.1 21.2 %collective-permute-start.12 = (f32[128,512]{1,0:T(8,128)S(1)}, f32[128,512]{1,0:T(8,128)S(1)}, u32[]{:S(2)}, u32[]{:S(2)}) collective-permute-start(f32[128,512]{1,0:T(8,128)S(1)} %get-tuple-element.121), channel_id=1, source_target_pairs={{0,24},{8,32},{16,40},{24,48},{32,56},{40,0},{48,8},{56,16},{1,25}... | collective-permute-start | bytes 786440 | tf_op jit(solution)/shard_map/ppermute | solution.py:17
  153.3 10.6 %collective-permute-start.13 = (f32[256,256]{1,0:T(8,128)S(1)}, f32[256,256]{1,0:T(8,128)S(1)}, u32[]{:S(2)}, u32[]{:S(2)}) collective-permute-start(f32[256,256]{1,0:T(8,128)S(1)} %broadcast_select_fusion.17), channel_id=1, source_target_pairs={{0,2},{4,6},{8,10},{12,14},{16,18},{20,22},{24,26},{28,30},{32,34}... | collective-permute-start | bytes 786440 | tf_op jit(solution)/shard_map/ppermute | solution.py:17
  154.6 13.6 %collective-permute-start.14 = (f32[128,512]{1,0:T(8,128)S(1)}, f32[128,512]{1,0:T(8,128)S(1)}, u32[]{:S(2)}, u32[]{:S(2)}) collective-permute-start(f32[128,512]{1,0:T(8,128)S(1)} %get-tuple-element.126), channel_id=1, source_target_pairs={{0,32},{8,40},{16,48},{24,56},{32,0},{40,8},{48,16},{56,24},{1,33}... | collective-permute-start | bytes 786440 | tf_op jit(solution)/shard_map/ppermute | solution.py:17
  168.2 45.8 %collective-permute-start.15 = (f32[256,256]{1,0:T(8,128)}, f32[256,256]{1,0:T(8,128)S(1)}, u32[]{:S(2)}, u32[]{:S(2)}) collective-permute-start(f32[256,256]{1,0:T(8,128)} %broadcast_select_fusion.19), channel_id=1, source_target_pairs={{0,1},{2,3},{4,5},{6,7},{8,9},{10,11},{12,13},{14,15},{16,17},{18,... | collective-permute-start | bytes 786440 | tf_op jit(solution)/shard_map/ppermute | solution.py:17
  171.0 50.9 %collective-permute-start.16 = (f32[128,512]{1,0:T(8,128)S(1)}, f32[128,512]{1,0:T(8,128)S(1)}, u32[]{:S(2)}, u32[]{:S(2)}) collective-permute-start(f32[128,512]{1,0:T(8,128)S(1)} %get-tuple-element.131), channel_id=1, source_target_pairs={{0,40},{8,48},{16,56},{24,0},{32,8},{40,16},{48,24},{56,32},{1,41}... | collective-permute-start | bytes 786440 | tf_op jit(solution)/shard_map/ppermute | solution.py:17
  195.0 61.5 %collective-permute-start.17 = (f32[128,512]{1,0:T(8,128)S(1)}, f32[128,512]{1,0:T(8,128)S(1)}, u32[]{:S(2)}, u32[]{:S(2)}) collective-permute-start(f32[128,512]{1,0:T(8,128)S(1)} %get-tuple-element.141), channel_id=1, source_target_pairs={{0,48},{8,56},{16,0},{24,8},{32,16},{40,24},{48,32},{56,40},{1,49}... | collective-permute-start | bytes 786440 | tf_op jit(solution)/shard_map/ppermute | solution.py:17
  234.4 44.7 %collective-permute-start.18 = (f32[128,512]{1,0:T(8,128)S(1)}, f32[128,512]{1,0:T(8,128)S(1)}, u32[]{:S(2)}, u32[]{:S(2)}) collective-permute-start(f32[128,512]{1,0:T(8,128)S(1)} %get-tuple-element.142), channel_id=1, source_target_pairs={{0,56},{8,0},{16,8},{24,16},{32,24},{40,32},{48,40},{56,48},{1,57}... | collective-permute-start | bytes 786440 | tf_op jit(solution)/shard_map/ppermute | solution.py:17
  301.2 18.8 %all-to-all-start.1 = ((f32[8,32,128]{2,1,0:T(8,128)}), f32[8,32,128]{2,1,0:T(8,128)S(1)}, u32[]{:S(2)}, u32[]{:S(2)}) async-start(f32[8,32,128]{2,1,0:T(8,128)} %col_slots.1), calls=%async_computation.1 | async-start | bytes 262144 | tf_op jit(solution)/shard_map/all_to_all | solution.py:425
  311.1 10.5 %collective-permute-start.19 = (f32[4,128,128]{2,1,0:T(8,128)}, f32[4,128,128]{2,1,0:T(8,128)S(1)}, u32[]{:S(2)}, u32[]{:S(2)}) collective-permute-start(f32[4,128,128]{2,1,0:T(8,128)} %copy-done.12), channel_id=1, source_target_pairs={{0,1},{1,2},{2,3},{3,4},{4,5},{5,6},{6,7},{7,0},{8,9},{9,10},{10,1... | collective-permute-start | bytes 786440 | tf_op jit(solution)/shard_map/ppermute | solution.py:17
  321.5 17.2 %collective-permute-start.20 = (f32[4,32,128]{2,1,0:T(8,128)S(1)}, f32[4,32,128]{2,1,0:T(8,128)S(1)}, u32[]{:S(2)}, u32[]{:S(2)}) collective-permute-start(f32[4,32,128]{2,1,0:T(8,128)S(1)} %row_pick.1), channel_id=1, source_target_pairs={{0,4},{1,5},{2,6},{3,7},{4,0},{5,1},{6,2},{7,3},{8,12},{9,13},{10,... | collective-permute-start | bytes 196616 | tf_op jit(solution)/shard_map/ppermute | solution.py:17
  329.9 13.4 %collective-permute-start.22 = (f32[4,128,128]{2,1,0:T(8,128)}, f32[4,128,128]{2,1,0:T(8,128)S(1)}, u32[]{:S(2)}, u32[]{:S(2)}) collective-permute-start(f32[4,128,128]{2,1,0:T(8,128)} %copy-done.11), channel_id=1, source_target_pairs={{0,2},{1,3},{2,4},{3,5},{4,6},{5,7},{6,0},{7,1},{8,10},{9,11},{10,... | collective-permute-start | bytes 786440 | tf_op jit(solution)/shard_map/ppermute | solution.py:17
  333.6 5.1 collective-permute-start.21
  343.2 38.8 %collective-permute-start.24 = (f32[2,4,32,128]{3,2,1,0:T(8,128)S(1)}, f32[2,4,32,128]{3,2,1,0:T(8,128)S(1)}, u32[]{:S(2)}, u32[]{:S(2)}) collective-permute-start(f32[2,4,32,128]{3,2,1,0:T(8,128)S(1)} %pad_maximum_fusion.6), channel_id=1, source_target_pairs={{0,8},{8,0},{16,24},{24,16},{32,40},{40,32},{48,56},{56,48},{1,9},... | collective-permute-start | bytes 393224 | tf_op jit(solution)/shard_map/ppermute | solution.py:17
  358.6 28.8 %collective-permute-start.25 = (f32[4,128,128]{2,1,0:T(8,128)S(1)}, f32[4,128,128]{2,1,0:T(8,128)S(1)}, u32[]{:S(2)}, u32[]{:S(2)}) collective-permute-start(f32[4,128,128]{2,1,0:T(8,128)S(1)} %get-tuple-element.170), channel_id=1, source_target_pairs={{0,3},{1,4},{2,5},{3,6},{4,7},{5,0},{6,1},{7,2},{8,11},{9,12},{10,... | collective-permute-start | bytes 786440 | tf_op jit(solution)/shard_map/ppermute | solution.py:17
  371.9 15.4 %collective-permute-start.23 = (f32[2,4,32,128]{3,2,1,0:T(8,128)S(1)}, f32[2,4,32,128]{3,2,1,0:T(8,128)S(1)}, u32[]{:S(2)}, u32[]{:S(2)}) collective-permute-start(f32[2,4,32,128]{3,2,1,0:T(8,128)S(1)} %pad_maximum_fusion.5), channel_id=1, source_target_pairs={{0,2},{1,3},{2,0},{3,1},{4,6},{5,7},{6,4},{7,5},{8,10},{9,11},{10,... | collective-permute-start | bytes 393224 | tf_op jit(solution)/shard_map/ppermute | solution.py:17
  387.4 23.0 %collective-permute-start.27 = (f32[2,2,4,32,128]{4,3,2,1,0:T(8,128)S(1)}, f32[2,2,4,32,128]{4,3,2,1,0:T(8,128)S(1)}, u32[]{:S(2)}, u32[]{:S(2)}) collective-permute-start(f32[2,2,4,32,128]{4,3,2,1,0:T(8,128)S(1)} %get-tuple-element.172), channel_id=1, source_target_pairs={{0,16},{8,24},{16,0},{24,8},{32,48},{40,56},{48,32},{56,40},{1,17}... | collective-permute-start | bytes 786440 | tf_op jit(solution)/shard_map/ppermute | solution.py:17
  391.7 18.7 %collective-permute-start.26 = (f32[2,2,4,32,128]{4,3,2,1,0:T(8,128)S(1)}, f32[2,2,4,32,128]{4,3,2,1,0:T(8,128)S(1)}, u32[]{:S(2)}, u32[]{:S(2)}) collective-permute-start(f32[2,2,4,32,128]{4,3,2,1,0:T(8,128)S(1)} %get-tuple-element.171), channel_id=1, source_target_pairs={{0,1},{1,0},{2,3},{3,2},{4,5},{5,4},{6,7},{7,6},{8,9},{9,8},{10,11... | collective-permute-start | bytes 786440 | tf_op jit(solution)/shard_map/ppermute | solution.py:17
  400.4 20.9 %collective-permute-start.28 = (f32[4,128,128]{2,1,0:T(8,128)S(1)}, f32[4,128,128]{2,1,0:T(8,128)S(1)}, u32[]{:S(2)}, u32[]{:S(2)}) collective-permute-start(f32[4,128,128]{2,1,0:T(8,128)S(1)} %copy-done.10), channel_id=1, source_target_pairs={{0,4},{1,5},{2,6},{3,7},{4,0},{5,1},{6,2},{7,3},{8,12},{9,13},{10,... | collective-permute-start | bytes 786440 | tf_op jit(solution)/shard_map/ppermute | solution.py:17
  421.3 16.1 %collective-permute-start.30 = (f32[2,2,2,4,32,128]{5,4,3,2,1,0:T(8,128)S(1)}, f32[2,2,2,4,32,128]{5,4,3,2,1,0:T(8,128)}, u32[]{:S(2)}, u32[]{:S(2)}) collective-permute-start(f32[2,2,2,4,32,128]{5,4,3,2,1,0:T(8,128)S(1)} %pad_maximum_fusion.2), channel_id=1, source_target_pairs={{0,32},{8,40},{16,48},{24,56},{32,0},{40,8},{48,16},{56,24},{1,33}... | collective-permute-start | bytes 1572872 | tf_op jit(solution)/shard_map/ppermute | solution.py:17
  425.5 29.2 %collective-permute-start.29 = (f32[256,512]{1,0:T(8,128)}, f32[256,512]{1,0:T(8,128)}, u32[]{:S(2)}, u32[]{:S(2)}) collective-permute-start(f32[256,512]{1,0:T(8,128)} %bitcast.64), channel_id=1, source_target_pairs={{0,64},{64,0},{128,192},{192,128},{256,320},{320,256},{384,448},{4... | collective-permute-start | bytes 1572872 | tf_op jit(solution)/shard_map/ppermute | solution.py:17
  427.5 27.3 %collective-permute-start.31 = (f32[4,128,128]{2,1,0:T(8,128)S(1)}, f32[4,128,128]{2,1,0:T(8,128)S(1)}, u32[]{:S(2)}, u32[]{:S(2)}) collective-permute-start(f32[4,128,128]{2,1,0:T(8,128)S(1)} %copy-done.8), channel_id=1, source_target_pairs={{0,5},{1,6},{2,7},{3,0},{4,1},{5,2},{6,3},{7,4},{8,13},{9,14},{10,... | collective-permute-start | bytes 786440 | tf_op jit(solution)/shard_map/ppermute | solution.py:17
  429.5 27.1 %collective-permute-start.32 = (f32[4,128,128]{2,1,0:T(8,128)S(1)}, f32[4,128,128]{2,1,0:T(8,128)S(1)}, u32[]{:S(2)}, u32[]{:S(2)}) collective-permute-start(f32[4,128,128]{2,1,0:T(8,128)S(1)} %copy-done.6), channel_id=1, source_target_pairs={{0,6},{1,7},{2,0},{3,1},{4,2},{5,3},{6,4},{7,5},{8,14},{9,15},{10,... | collective-permute-start | bytes 786440 | tf_op jit(solution)/shard_map/ppermute | solution.py:17
  454.8 20.6 %collective-permute-start.33 = (f32[4,128,128]{2,1,0:T(8,128)S(1)}, f32[4,128,128]{2,1,0:T(8,128)S(1)}, u32[]{:S(2)}, u32[]{:S(2)}) collective-permute-start(f32[4,128,128]{2,1,0:T(8,128)S(1)} %copy-done.4), channel_id=1, source_target_pairs={{0,7},{1,0},{2,1},{3,2},{4,3},{5,4},{6,5},{7,6},{8,15},{9,8},{10,9... | collective-permute-start | bytes 786440 | tf_op jit(solution)/shard_map/ppermute | solution.py:17
  477.0 7.0 %collective-permute-start.34 = (f32[4,4,128,128]{3,2,1,0:T(8,128)S(1)}, f32[4,4,128,128]{3,2,1,0:T(8,128)S(1)}, u32[]{:S(2)}, u32[]{:S(2)}) collective-permute-start(f32[4,4,128,128]{3,2,1,0:T(8,128)S(1)} %other.1), channel_id=1, source_target_pairs={{0,64},{64,0},{128,192},{192,128},{256,320},{320,256},{384,448},{4... | collective-permute-start | bytes 3145736 | tf_op jit(solution)/shard_map/ppermute | solution.py:17
  488.4 10.3 %collective-permute-start.39 = (f32[1024,256]{1,0:T(8,128)S(1)}, f32[1024,256]{1,0:T(8,128)}, u32[]{:S(2)}, u32[]{:S(2)}) collective-permute-start(f32[1024,256]{1,0:T(8,128)S(1)} %slice.43), channel_id=1, source_target_pairs={{0,4},{128,132},{256,260},{384,388},{8,12},{136,140},{264,268},{39... | collective-permute-start | bytes 3145736 | tf_op jit(solution)/shard_map/ppermute | solution.py:17
  490.1 7.5 %collective-permute-start.40 = (f32[256,512]{1,0:T(8,128)}, f32[256,512]{1,0:T(8,128)}, u32[]{:S(2)}, u32[]{:S(2)}) collective-permute-start(f32[256,512]{1,0:T(8,128)} %slice.44), channel_id=1, source_target_pairs={{0,32},{1,33},{2,34},{3,35},{4,36},{5,37},{6,38},{7,39},{64,96},{6... | collective-permute-start | bytes 1572872 | tf_op jit(solution)/shard_map/ppermute | solution.py:17
  491.5 4.1 collective-permute-start.35
  492.9 2.7 collective-permute-start.36
  496.8 1.8 collective-permute-start.38
  498.9 26.1 %collective-permute-start.42 = (f32[1024,256]{1,0:T(8,128)S(1)}, f32[1024,256]{1,0:T(8,128)S(1)}, u32[]{:S(2)}, u32[]{:S(2)}) collective-permute-start(f32[1024,256]{1,0:T(8,128)S(1)} %broadcast_select_fusion.2), channel_id=1, source_target_pairs={{0,2},{4,6},{128,130},{132,134},{256,258},{260,262},{384,386},{388... | collective-permute-start | bytes 3145736 | tf_op jit(solution)/shard_map/ppermute | solution.py:17
  525.1 52.7 %collective-permute-start.45 = (f32[1024,256]{1,0:T(8,128)S(1)}, f32[1024,256]{1,0:T(8,128)S(1)}, u32[]{:S(2)}, u32[]{:S(2)}) collective-permute-start(f32[1024,256]{1,0:T(8,128)S(1)} %broadcast_select_fusion.1), channel_id=1, source_target_pairs={{0,1},{2,3},{4,5},{6,7},{128,129},{130,131},{132,133},{134,135},{2... | collective-permute-start | bytes 3145736 | tf_op jit(solution)/shard_map/ppermute | solution.py:17
  526.5 51.3 %collective-permute-start.44 = (f32[256,256]{1,0:T(8,128)S(1)}, f32[256,256]{1,0:T(8,128)S(1)}, u32[]{:S(2)}, u32[]{:S(2)}) collective-permute-start(f32[256,256]{1,0:T(8,128)S(1)} %broadcast_select_fusion.16), channel_id=1, source_target_pairs={{0,2},{4,6},{128,130},{132,134},{256,258},{260,262},{384,386},{388... | collective-permute-start | bytes 786440 | tf_op jit(solution)/shard_map/ppermute | solution.py:17
  578.0 5.2 collective-permute-start.47
  579.3 39.2 %collective-permute-start.46 = (f32[1024,256]{1,0:T(8,128)S(1)}, f32[1024,256]{1,0:T(8,128)}, u32[]{:S(2)}, u32[]{:S(2)}) collective-permute-start(f32[1024,256]{1,0:T(8,128)S(1)} %broadcast_select_fusion), channel_id=1, source_target_pairs={{0,64},{128,192},{256,320},{384,448},{1,65},{129,193},{257,321},{3... | collective-permute-start | bytes 3145736 | tf_op jit(solution)/shard_map/ppermute | solution.py:17
  581.6 35.1 %collective-permute-start.49 = (f32[256,512]{1,0:T(8,128)}, f32[256,512]{1,0:T(8,128)}, u32[]{:S(2)}, u32[]{:S(2)}) collective-permute-start(f32[256,512]{1,0:T(8,128)} %broadcast_select_fusion.5), channel_id=1, source_target_pairs={{0,8},{16,24},{32,40},{48,56},{1,9},{17,25},{33,41},{49,57},{2,10}... | collective-permute-start | bytes 1572872 | tf_op jit(solution)/shard_map/ppermute | solution.py:17
  583.2 2.6 collective-permute-start.48
  (18 other events, 596.9 us)

commit v4 on v3

--- a/solution.py
+++ b/solution.py
@@ -119,9 +119,8 @@
     lax.fori_loop(0, count, body, jnp.int32(0))
 
 
-def strips_kernel(sizes, ids_ref, map_ref, part_ref, *refs):
-    row_span, first, row_blocks, rows = sizes
-    outs, slots_ref = refs[:rows], refs[rows]
+def strips_kernel(sizes, ids_ref, map_ref, part_ref, out_ref):
+    row_span, first, row_blocks = sizes
     row = ids_ref[1]
     for a in range(row_blocks):
         block = row * row_blocks + a - first
@@ -129,73 +128,54 @@
         @pl.when(block >= 0)
         def _():
             target = map_ref[jnp.maximum(block, 0)] // row_span
-            slots_ref[(target - row + rows) % rows] = part_ref[a * BLK : (a + 1) * BLK, :]
-
-    for s in range(rows):
-        outs[s][...] = slots_ref[s]
-
-
-def tiles_kernel(sizes, ids_ref, map_ref, *refs):
-    row_span, col_span, first, row_blocks, col_blocks, rows, cols, count = sizes
-    gots, outs = refs[:rows], refs[rows : rows + cols]
-    slots_ref, rank_ref, at_ref = refs[rows + cols :]
+            out_ref[target] = part_ref[a * BLK : (a + 1) * BLK, :]
+
+
+def tiles_kernel(sizes, ids_ref, map_ref, got_ref, out_ref, rank_ref, at_ref):
+    row_span, col_span, first, row_blocks, col_blocks, cols, count = sizes
     row, col = ids_ref[1], ids_ref[2]
     row_tables(map_ref, row, row_span, count, rank_ref, at_ref)
-    for s in range(rows):
-        source = (row - s + rows) % rows
-
-        def body(a, carry):
-            block = source * row_blocks + a - first
-            rank = jnp.where(block >= 0, rank_ref[jnp.maximum(block, 0)], -1)
-
-            @pl.when(rank >= 0)
-            def _():
-                held = gots[s]
-                slot = jnp.minimum(rank, slots_ref.shape[1] - 1)
-                for y in range(col_blocks):
-                    block = col * col_blocks + y - first
-
-                    @pl.when(block >= 0)
-                    def _():
-                        target = (map_ref[jnp.maximum(block, 0)] // col_span) % cols
-                        slots_ref[(target - col + cols) % cols, slot] = held[
-                            :, y * BLK : (y + 1) * BLK
-                        ]
-
-            return carry
-
-        lax.fori_loop(0, row_blocks, body, jnp.int32(0))
-    for t in range(cols):
-        outs[t][...] = slots_ref[t]
-
-
-def other_kernel(sizes, ids_ref, map_ref, *refs):
-    col_span, first, col_blocks, cols = sizes
-    gots, out_ref = refs[:cols], refs[cols]
+
+    def body(k, carry):
+        rank = rank_ref[k]
+
+        @pl.when(rank >= 0)
+        def _():
+            source = (k + first) // row_blocks
+            slot = jnp.minimum(rank, out_ref.shape[1] - 1)
+            for y in range(col_blocks):
+                block = col * col_blocks + y - first
+
+                @pl.when(block >= 0)
+                def _():
+                    target = (map_ref[jnp.maximum(block, 0)] // col_span) % cols
+                    out_ref[target, slot] = got_ref[source, :, y * BLK : (y + 1) * BLK]
+
+        return carry
+
+    lax.fori_loop(0, count, body, jnp.int32(0))
+
+
+def other_kernel(sizes, ids_ref, map_ref, landed_ref, out_ref):
+    col_span, first, col_blocks, cols, count = sizes
     half, col = ids_ref[0], ids_ref[2]
     out_ref[...] = jnp.zeros_like(out_ref)
-    for t in range(cols):
-        source = (col - t + cols) % cols
-
-        def body(y, carry):
-            block = source * col_blocks + y - first
-            spot = map_ref[jnp.maximum(block, 0)]
-            owner = spot // col_span
-
-            @pl.when((block >= 0) & (owner % cols == col) & (owner // cols != half))
-            def _():
-                out_ref[spot % col_span] = gots[t][...]
-
-            return carry
-
-        lax.fori_loop(0, col_blocks, body, jnp.int32(0))
+
+    def body(k, carry):
+        owner = map_ref[k] // col_span
+
+        @pl.when((owner % cols == col) & (owner // cols != half))
+        def _():
+            out_ref[map_ref[k] % col_span] = landed_ref[(k + first) // col_blocks]
+
+        return carry
+
+    lax.fori_loop(0, count, body, jnp.int32(0))
 
 
 def assemble_kernel(sizes, ids_ref, map_ref, pair_map_ref, parent_ref, own_ref, pair_ref,
-                    other_ref, *refs):
+                    other_ref, landed_ref, out_ref, rank_ref, at_ref, pair_at_ref):
     row_span, col_span, first, col_blocks, cols, count = sizes
-    gots, out_ref = refs[:cols], refs[cols]
-    rank_ref, at_ref, pair_at_ref = refs[cols + 1 :]
     half, row, col = ids_ref[0], ids_ref[1], ids_ref[2]
     out_ref[...] = parent_ref[...].astype(jnp.float32)
     row_tables(pair_map_ref, row, row_span, count, rank_ref, pair_at_ref)
@@ -220,28 +200,23 @@
                 )
                 out_ref[spot] = out_ref[spot] + other_ref[y, m]
 
-    for t in range(cols):
-        source = (col - t + cols) % cols
-
-        def body(y, carry):
-            block = source * col_blocks + y - first
-            place = map_ref[jnp.maximum(block, 0)]
-            owner = place // col_span
-
-            @pl.when((block >= 0) & (owner % cols == col) & (owner // cols == half))
-            def _():
-                at_col = pl.ds(pl.multiple_of((place % col_span) * BLK, BLK), BLK)
-                for m in range(caps):
-                    at = at_ref[m]
-
-                    @pl.when(at >= 0)
-                    def _():
-                        spot = (pl.ds(pl.multiple_of(at * BLK, BLK), BLK), at_col)
-                        out_ref[spot] = out_ref[spot] + gots[t][m]
-
-            return carry
-
-        lax.fori_loop(0, col_blocks, body, jnp.int32(0))
+    def body(k, carry):
+        owner = map_ref[k] // col_span
+
+        @pl.when((owner % cols == col) & (owner // cols == half))
+        def _():
+            at_col = pl.ds(pl.multiple_of((map_ref[k] % col_span) * BLK, BLK), BLK)
+            for m in range(caps):
+                at = at_ref[m]
+
+                @pl.when(at >= 0)
+                def _():
+                    spot = (pl.ds(pl.multiple_of(at * BLK, BLK), BLK), at_col)
+                    out_ref[spot] = out_ref[spot] + landed_ref[(k + first) // col_blocks, m]
+
+        return carry
+
+    lax.fori_loop(0, count, body, jnp.int32(0))
 
 
 def row_slots_kernel(sizes, ids_ref, map_ref, part_ref, out_ref):
@@ -342,50 +317,30 @@
     cap = -(-count // row_count)
     swap = [(i, i ^ 1) for i in range(leaf_count)]
 
-    bulk = []
-
-    def step(operands, lag=1):
-        operands = list(operands)
-        if len(bulk) > lag:
-            tied = lax.optimization_barrier((operands, bulk[-1 - lag]))
-            operands, bulk[-1 - lag] = tied
-        else:
-            operands = lax.optimization_barrier(operands)
-        return operands
-
     def only(cell, got, value, targets):
         index = lax.axis_index(cell)
         hit = functools.reduce(jnp.logical_or, [index == t for t in targets])
         return jnp.where(hit, got, value)
 
     strips = kernel_call(
-        functools.partial(strips_kernel, (row_span, first, row_blocks, row_count)),
-        "strips", [(BLK, child_cols)] * row_count, 2, 1,
-        [pltpu.VMEM((row_count, BLK, child_cols), jnp.float32)],
+        functools.partial(strips_kernel, (row_span, first, row_blocks)),
+        "strips", (row_count, BLK, child_cols), 2, 1,
     )(ids, own_map, child_block)
-    strips = list(strips)
-    row_pairs = [[(i, (i + s) % row_count) for i in range(row_count)] for s in range(row_count)]
-    col_pairs = [[(i, (i + t) % col_count) for i in range(col_count)] for t in range(col_count)]
+    strips, child_block = lax.optimization_barrier((strips, child_block))
+    got = lax.all_to_all(strips, "row", 0, 0, tiled=True)
 
     def by_rows(pairs):
         return [(r * col_count, q * col_count) for r, q in pairs]
 
     diagonal, slab, top = child_block[:width, :width], child_block[:, :width], child_block[:width]
-    for number, pairs in enumerate(HALVING):
-        shift = number + 1
-        diagonal, slab, top, strips[shift] = step([diagonal, slab, top, strips[shift]])
-        bulk.append(send(strips[shift], "row", row_pairs[shift]))
+    for pairs in HALVING:
         targets = [t for _, t in pairs]
         diagonal = only("row", send(diagonal, ("row", "col"), by_rows(pairs)), diagonal, targets)
         slab = only("col", send(slab, "col", pairs), slab, targets)
         top = only("row", send(top, "row", pairs), top, targets)
-    for number, pairs in enumerate(HALVING):
-        shift = number + 4
-        diagonal, slab, top, strips[shift] = step([diagonal, slab, top, strips[shift]])
-        bulk.append(send(strips[shift], "row", row_pairs[shift]))
+        diagonal, slab, top = lax.optimization_barrier((diagonal, slab, top))
+    for pairs in HALVING:
         diagonal = only("col", send(diagonal, "col", pairs), diagonal, [t for _, t in pairs])
-    diagonal, slab, top, strips[7] = step([diagonal, slab, top, strips[7]])
-    bulk.append(send(strips[7], "row", row_pairs[7]))
     inverse = inverse_factor(diagonal)
     cols_factor = jnp.dot(inverse, top, precision=HIGHEST)
     out_width = width // col_count
@@ -401,27 +356,22 @@
         functools.partial(col_slots_kernel, (col_span, first, col_blocks, col_count)),
         "col_slots", (col_count,) + piece, 2, 1,
     )(ids, own_map, col_share)
-    row_slots, col_slots, got = lax.optimization_barrier((row_slots, col_slots, bulk))
-    got = [strips[0]] + list(got)
-
+    got, row_slots, col_slots = lax.optimization_barrier((got, row_slots, col_slots))
     tables = [pltpu.SMEM((count,), jnp.int32), pltpu.SMEM((cap,), jnp.int32)]
-    tiles = list(kernel_call(
+    tiles = kernel_call(
         functools.partial(
             tiles_kernel,
-            (row_span, col_span, first, row_blocks, col_blocks, row_count, col_count, count),
+            (row_span, col_span, first, row_blocks, col_blocks, col_count, count),
         ),
-        "tiles", [(cap, BLK, BLK)] * col_count, 2, row_count,
-        [pltpu.VMEM((col_count, cap, BLK, BLK), jnp.float32)] + tables,
-    )(ids, own_map, *got))
-    bulk = []
-
-    tiles[1], tiles[2], row_slots, col_slots = lax.optimization_barrier(
-        (tiles[1], tiles[2], row_slots, col_slots)
-    )
-    bulk.append(send(tiles[1], "col", col_pairs[1]))
+        "tiles", (col_count, cap, BLK, BLK), 2, 1, tables,
+    )(ids, own_map, got)
+    tiles, row_slots, col_slots = lax.optimization_barrier((tiles, row_slots, col_slots))
+    landed = lax.all_to_all(
+        tiles.reshape(col_count, cap * BLK, BLK), "col", 0, 0, tiled=True
+    ).reshape(tiles.shape)
+
     row_got = lax.all_to_all(row_slots, "row", 0, 0, tiled=True)
-    tiles[2], col_slots, row_got = lax.optimization_barrier((tiles[2], col_slots, row_got))
-    bulk.append(send(tiles[2], "col", col_pairs[2]))
+    col_slots, row_got = lax.optimization_barrier((col_slots, row_got))
     col_got = lax.all_to_all(col_slots, "col", 0, 0, tiled=True)
     row_panel = kernel_call(
         functools.partial(row_pick_kernel, (row_span, first, row_blocks, count)),
@@ -439,27 +389,18 @@
         high = jnp.where(upper == 0, got, value)
         return jnp.stack([low, high])
 
-    row_panel, other_cols, tiles[3] = step([row_panel, other_cols, tiles[3]])
-    bulk.append(send(tiles[3], "col", col_pairs[3]))
     row_panel = doubled(row_panel, "col", 2)
     col_panels = jnp.stack([own_cols, send(other_cols, "leaf", swap)])
-    row_panel, col_panels, tiles[4] = step([row_panel, col_panels, tiles[4]])
-    bulk.append(send(tiles[4], "col", col_pairs[4]))
+    row_panel, col_panels = lax.optimization_barrier((row_panel, col_panels))
     row_panel = doubled(row_panel, "col", 1)
     col_panels = doubled(col_panels, "row", 0)
-    row_panel, col_panels, tiles[5] = step([row_panel, col_panels, tiles[5]])
-    bulk.append(send(tiles[5], "col", col_pairs[5]))
+    row_panel, col_panels = lax.optimization_barrier((row_panel, col_panels))
     row_panel = doubled(row_panel, "col", 0)
     col_panels = doubled(col_panels, "row", 1)
-    row_panel, col_panels, tiles[6] = step([row_panel, col_panels, tiles[6]])
-    bulk.append(send(tiles[6], "col", col_pairs[6]))
+    row_panel, col_panels = lax.optimization_barrier((row_panel, col_panels))
     row_panel = jnp.transpose(row_panel, (2, 1, 0, 4, 3, 5)).reshape(width, cap * BLK)
     pair_row_panel = send(row_panel, "leaf", swap)
     col_panels = doubled(col_panels, "row", 2)
-    row_panel, pair_row_panel, col_panels, tiles[7] = step(
-        [row_panel, pair_row_panel, col_panels, tiles[7]]
-    )
-    bulk.append(send(tiles[7], "col", col_pairs[7]))
     col_panels = jnp.transpose(col_panels, (3, 0, 1, 2, 5, 4, 6))
     col_panels = col_panels.reshape(2, width, col_span * BLK)
 
@@ -468,19 +409,21 @@
 
     own_product = product(row_panel, col_panels[0])
     pair_product = product(pair_row_panel, col_panels[1])
-    landed = [tiles[0]] + bulk
+    landed, own_product, pair_product = lax.optimization_barrier(
+        (landed, own_product, pair_product)
+    )
     other = kernel_call(
-        functools.partial(other_kernel, (col_span, first, col_blocks, col_count)),
-        "other", (col_span, cap, BLK, BLK), 2, col_count,
-    )(ids, own_map, *landed)
+        functools.partial(other_kernel, (col_span, first, col_blocks, col_count, count)),
+        "other", (col_span, cap, BLK, BLK), 2, 1,
+    )(ids, own_map, landed)
     other = send(other, "leaf", swap)
     assembled = kernel_call(
         functools.partial(
             assemble_kernel, (row_span, col_span, first, col_blocks, col_count, count)
         ),
-        "assemble", parent_front.shape, 3, 4 + col_count,
+        "assemble", parent_front.shape, 3, 5,
         tables + [pltpu.SMEM((cap,), jnp.int32)],
-    )(ids, own_map, partner_map, parent_front, own_product, pair_product, other, *landed)
+    )(ids, own_map, partner_map, parent_front, own_product, pair_product, other, landed)
 
     parent_order = parent_rows * row_count
     parent_width = parent_cols // 2

time: 627 us -> 585 us (0.933)
  the two profiles are of different devices: /device:TPU:468 before, /device:TPU:6 now
where the time goes in v4:
time: 585 us; the launch traced here: 575 us
  waiting for transfers between devices  284 us (49%)
  starting transfers between devices  170 us (29%)
  blocking collectives  48 us (8%)
  Pallas kernels  36.4 us (6%)
  matrix products  13.5 us (2%)
  other arithmetic  12 us (2%)
  local copies, waits for them, and re-layouts  9.48 us (2%)
    ppermute x36, waiting for transfers between devices, send(): return lax.ppermute(value, axes, pairs)  284 us
    ppermute x36, starting transfers between devices, send(): return lax.ppermute(value, axes, pairs)  148 us
    all_to_all x1, blocking collectives, shards(): col_got = lax.all_to_all(col_slots, 'col', 0, 0, tiled=True)  27.7 us
    pallas_call x2, Pallas kernels, inverse_factor(): pl.pallas_call(inverse_factor_kernel, out_shape=jax.ShapeDtypeStruct(bloc...  24.9 us
    all_to_all x1, blocking collectives, shards(): row_got = lax.all_to_all(row_slots, 'row', 0, 0, tiled=True)  20.3 us
    all_to_all x1, starting transfers between devices, shards(): got = lax.all_to_all(strips, 'row', 0, 0, tiled=True)  17.9 us
  transfers between devices with their start and end apart: 38, of which 21 were waited for; matrix products, arithmetic and copies ran while one was open for 4% of the time, Pallas kernels for 5%

profile of v4, /device:TPU:6, one launch (start us, length us, event | category | flops | bytes accessed | tf_op | source)
XLA Modules:
  0.0 574.9 jit_solution(16498251701982076203)
XLA Ops:
  4.7 17.9 %all-to-all-start = ((f32[8,128,512]{2,1,0:T(8,128)}), f32[8,128,512]{2,1,0:T(8,128)S(1)}, u32[]{:S(2)}, u32[]{:S(2)}) async-start(f32[8,128,512]{2,1,0:T(8,128)} %copy-done.5), calls=%async_computation | async-start | bytes 4194304 | tf_op jit(solution)/shard_map/all_to_all | solution.py:330
  23.4 6.2 %collective-permute-start.2 = (f32[256,512]{1,0:T(8,128)}, f32[256,512]{1,0:T(8,128)}, u32[]{:S(2)}, u32[]{:S(2)}) collective-permute-start(f32[256,512]{1,0:T(8,128)} %slice.28), channel_id=1, source_target_pairs={{0,32},{1,33},{2,34},{3,35},{4,36},{5,37},{6,38},{7,39},{64,96},{6... | collective-permute-start | bytes 1572872 | tf_op jit(solution)/shard_map/ppermute | solution.py:17
  32.5 4.5 collective-permute-start.1
  37.0 19.5 %collective-permute-done = f32[256,256]{1,0:T(8,128)} collective-permute-done((f32[256,256]{1,0:T(8,128)S(1)}, f32[256,256]{1,0:T(8,128)}, u32[]{:S(2)}, u32[]{:S(2)}) %collective-permute-start) | collective-permute-done | bytes 262176 | tf_op jit(solution)/shard_map/ppermute | solution.py:17
  57.5 54.7 %collective-permute-done.1 = f32[512,256]{1,0:T(8,128)} collective-permute-done((f32[512,256]{1,0:T(8,128)}, f32[512,256]{1,0:T(8,128)}, u32[]{:S(2)}, u32[]{:S(2)}) %collective-permute-start.1) | collective-permute-done | bytes 524320 | tf_op jit(solution)/shard_map/ppermute | solution.py:17
  113.1 3.0 collective-permute-start.5
  117.4 2.1 collective-permute-start.4
  119.6 12.3 %collective-permute-done.3 = f32[256,256]{1,0:T(8,128)S(1)} collective-permute-done((f32[256,256]{1,0:T(8,128)S(1)}, f32[256,256]{1,0:T(8,128)S(1)}, u32[]{:S(2)}, u32[]{:S(2)}) %collective-permute-start.3) | collective-permute-done | bytes 262176 | tf_op jit(solution)/shard_map/ppermute | solution.py:17
  134.1 7.0 %collective-permute-done.4 = f32[512,256]{1,0:T(8,128)} collective-permute-done((f32[512,256]{1,0:T(8,128)}, f32[512,256]{1,0:T(8,128)}, u32[]{:S(2)}, u32[]{:S(2)}) %collective-permute-start.4) | collective-permute-done | bytes 524320 | tf_op jit(solution)/shard_map/ppermute | solution.py:17
  142.2 5.1 collective-permute-start.8
  149.3 2.1 collective-permute-start.7
  151.4 13.1 %collective-permute-done.6 = f32[256,256]{1,0:T(8,128)} collective-permute-done((f32[256,256]{1,0:T(8,128)S(1)}, f32[256,256]{1,0:T(8,128)}, u32[]{:S(2)}, u32[]{:S(2)}) %collective-permute-start.6) | collective-permute-done | bytes 262176 | tf_op jit(solution)/shard_map/ppermute | solution.py:17
  165.5 7.4 %collective-permute-done.7 = f32[512,256]{1,0:T(8,128)} collective-permute-done((f32[512,256]{1,0:T(8,128)S(1)}, f32[512,256]{1,0:T(8,128)}, u32[]{:S(2)}, u32[]{:S(2)}) %collective-permute-start.7) | collective-permute-done | bytes 524320 | tf_op jit(solution)/shard_map/ppermute | solution.py:17
  173.8 29.9 %collective-permute-start.9 = (f32[256,256]{1,0:T(8,128)S(1)}, f32[256,256]{1,0:T(8,128)S(1)}, u32[]{:S(2)}, u32[]{:S(2)}) collective-permute-start(f32[256,256]{1,0:T(8,128)S(1)} %broadcast_select_fusion.15), channel_id=1, source_target_pairs={{0,4},{8,12},{16,20},{24,28},{32,36},{40,44},{48,52},{56,60},{64,6... | collective-permute-start | bytes 786440 | tf_op jit(solution)/shard_map/ppermute | solution.py:17
  203.7 5.7 collective-permute-done.9
  210.8 5.2 collective-permute-done.10
  218.0 3.8 collective-permute-done.11
  222.5 12.4 %inverse_factor.2 = f32[256,256]{1,0:T(8,128)} custom-call(f32[256,256]{1,0:T(8,128)} %broadcast_select_fusion.21.a_ref), custom_call_target="tpu_custom_call" | custom-call | tf_op jit(solution)/shard_map/inverse_factor/pallas_call | solution.py:89
  242.3 20.3 %all_to_all.20.got_ref = f32[8,32,128]{2,1,0:T(8,128)S(1)} all-to-all(f32[8,32,128]{2,1,0:T(8,128)S(1)} %row_slots.1), channel_id=1, replica_groups=mesh['leaf'=8,'row'=8,'col'=8] {'row'}, dimensions={0} | all-to-all | bytes 262144 | tf_op jit(solution)/shard_map/all_to_all | solution.py:373
  262.6 27.7 %all_to_all.21.got_ref = f32[8,32,128]{2,1,0:T(8,128)S(1)} all-to-all(f32[8,32,128]{2,1,0:T(8,128)S(1)} %col_slots.1), channel_id=1, replica_groups=mesh['leaf'=8,'row'=8,'col'=8] {'col'}, dimensions={0} | all-to-all | bytes 262144 | tf_op jit(solution)/shard_map/all_to_all | solution.py:375
  290.3 3.6 all-to-all-start.1
  295.5 7.8 %collective-permute-start.12 = (f32[4,32,128]{2,1,0:T(8,128)S(1)}, f32[4,32,128]{2,1,0:T(8,128)S(1)}, u32[]{:S(2)}, u32[]{:S(2)}) collective-permute-start(f32[4,32,128]{2,1,0:T(8,128)S(1)} %row_pick.1), channel_id=1, source_target_pairs={{0,4},{1,5},{2,6},{3,7},{4,0},{5,1},{6,2},{7,3},{8,12},{9,13},{10,... | collective-permute-start | bytes 196616 | tf_op jit(solution)/shard_map/ppermute | solution.py:17
  303.3 88.6 %collective-permute-done.12 = f32[4,32,128]{2,1,0:T(8,128)S(1)} collective-permute-done((f32[4,32,128]{2,1,0:T(8,128)S(1)}, f32[4,32,128]{2,1,0:T(8,128)S(1)}, u32[]{:S(2)}, u32[]{:S(2)}) %collective-permute-start.12) | collective-permute-done | bytes 65568 | tf_op jit(solution)/shard_map/ppermute | solution.py:17
  396.6 2.5 collective-permute-start.15
  401.1 12.6 %collective-permute-done.15 = f32[2,4,32,128]{3,2,1,0:T(8,128)S(1)} collective-permute-done((f32[2,4,32,128]{3,2,1,0:T(8,128)S(1)}, f32[2,4,32,128]{3,2,1,0:T(8,128)S(1)}, u32[]{:S(2)}, u32[]{:S(2)}) %collective-permute-start.15) | collective-permute-done | bytes 131104 | tf_op jit(solution)/shard_map/ppermute | solution.py:17
  413.7 2.3 collective-permute-start.17
  416.1 2.5 collective-permute-start.16
  418.6 3.8 collective-permute-done.17
  422.4 2.3 collective-permute-done.16
  424.9 4.0 collective-permute-start.18
  429.2 2.1 collective-permute-start.19
  431.3 8.9 %collective-permute-done.18 = f32[2,2,2,4,32,128]{5,4,3,2,1,0:T(8,128)} collective-permute-done((f32[2,2,2,4,32,128]{5,4,3,2,1,0:T(8,128)S(1)}, f32[2,2,2,4,32,128]{5,4,3,2,1,0:T(8,128)}, u32[]{:S(2)}, u32[]{:S(2)}) %collective-permute-start.18) | collective-permute-done | bytes 524320 | tf_op jit(solution)/shard_map/ppermute | solution.py:17
  443.5 2.1 fusion.2.pair_ref
  448.9 2.6 collective-permute-done.20.other_ref
  451.6 3.2 assemble.1
  456.2 3.6 collective-permute-start.21
  463.1 6.2 %collective-permute-start.25 = (f32[1024,256]{1,0:T(8,128)S(1)}, f32[1024,256]{1,0:T(8,128)S(1)}, u32[]{:S(2)}, u32[]{:S(2)}) collective-permute-start(f32[1024,256]{1,0:T(8,128)S(1)} %slice.37), channel_id=1, source_target_pairs={{0,4},{128,132},{256,260},{384,388},{8,12},{136,140},{264,268},{39... | collective-permute-start | bytes 3145736 | tf_op jit(solution)/shard_map/ppermute | solution.py:17
  469.4 4.1 collective-permute-start.26
  475.8 8.6 %collective-permute-done.24 = f32[256,256]{1,0:T(8,128)S(1)} collective-permute-done((f32[256,256]{1,0:T(8,128)S(1)}, f32[256,256]{1,0:T(8,128)S(1)}, u32[]{:S(2)}, u32[]{:S(2)}) %collective-permute-start.24) | collective-permute-done | bytes 262176 | tf_op jit(solution)/shard_map/ppermute | solution.py:17
  487.0 2.7 collective-permute-start.29
  489.7 5.3 collective-permute-start.27
  495.0 12.6 %collective-permute-done.27 = f32[256,256]{1,0:T(8,128)S(1)} collective-permute-done((f32[256,256]{1,0:T(8,128)S(1)}, f32[256,256]{1,0:T(8,128)S(1)}, u32[]{:S(2)}, u32[]{:S(2)}) %collective-permute-start.27) | collective-permute-done | bytes 262176 | tf_op jit(solution)/shard_map/ppermute | solution.py:17
  509.3 2.3 collective-permute-start.30
  511.7 12.7 %collective-permute-done.30 = f32[256,256]{1,0:T(8,128)S(1)} collective-permute-done((f32[256,256]{1,0:T(8,128)S(1)}, f32[256,256]{1,0:T(8,128)S(1)}, u32[]{:S(2)}, u32[]{:S(2)}) %collective-permute-start.30) | collective-permute-done | bytes 262176 | tf_op jit(solution)/shard_map/ppermute | solution.py:17
  527.5 23.4 %collective-permute-start.35 = (f32[256,512]{1,0:T(8,128)S(1)}, f32[256,512]{1,0:T(8,128)S(1)}, u32[]{:S(2)}, u32[]{:S(2)}) collective-permute-start(f32[256,512]{1,0:T(8,128)S(1)} %broadcast_select_fusion.5), channel_id=1, source_target_pairs={{0,8},{16,24},{32,40},{48,56},{1,9},{17,25},{33,41},{49,57},{2,10}... | collective-permute-start | bytes 1572872 | tf_op jit(solution)/shard_map/ppermute | solution.py:17
  554.3 12.4 %inverse_factor.3 = f32[256,256]{1,0:T(8,128)} custom-call(f32[256,256]{1,0:T(8,128)} %broadcast_select_fusion.11.a_ref), custom_call_target="tpu_custom_call" | custom-call | tf_op jit(solution)/shard_map/inverse_factor/pallas_call | solution.py:89
  568.3 2.2 fusion
  571.2 3.7 subtract_select_fusion
  (123 shorter events, 64.6 us)
Async XLA Ops:
  3.4 1.3 copy-start.5
  4.7 17.9 %copy-start.3 = (f32[1,512,512]{2,1,0:T(8,128)S(1)}, f32[1,512,512]{2,1,0:T(8,128)}, u32[]{:S(2)}) copy-start(f32[1,512,512]{2,1,0:T(8,128)} %param.3) | copy-start | bytes 3145732
  4.7 234.5 %all-to-all-start = ((f32[8,128,512]{2,1,0:T(8,128)}), f32[8,128,512]{2,1,0:T(8,128)S(1)}, u32[]{:S(2)}, u32[]{:S(2)}) async-start(f32[8,128,512]{2,1,0:T(8,128)} %copy-done.5), calls=%async_computation | async-start | bytes 4194304 | tf_op jit(solution)/shard_map/all_to_all | solution.py:330
  23.4 33.1 %collective-permute-start.2 = (f32[256,512]{1,0:T(8,128)}, f32[256,512]{1,0:T(8,128)}, u32[]{:S(2)}, u32[]{:S(2)}) collective-permute-start(f32[256,512]{1,0:T(8,128)} %slice.28), channel_id=1, source_target_pairs={{0,32},{1,33},{2,34},{3,35},{4,36},{5,37},{6,38},{7,39},{64,96},{6... | collective-permute-start | bytes 1572872 | tf_op jit(solution)/shard_map/ppermute | solution.py:17
  29.7 26.8 %collective-permute-start = (f32[256,256]{1,0:T(8,128)S(1)}, f32[256,256]{1,0:T(8,128)}, u32[]{:S(2)}, u32[]{:S(2)}) collective-permute-start(f32[256,256]{1,0:T(8,128)S(1)} %slice.26), channel_id=1, source_target_pairs={{0,32},{64,96},{128,160},{192,224},{256,288},{320,352},{384,416},{... | collective-permute-start | bytes 786440 | tf_op jit(solution)/shard_map/ppermute | solution.py:17
  32.5 79.7 %collective-permute-start.1 = (f32[512,256]{1,0:T(8,128)}, f32[512,256]{1,0:T(8,128)}, u32[]{:S(2)}, u32[]{:S(2)}) collective-permute-start(f32[512,256]{1,0:T(8,128)} %slice.27), channel_id=1, source_target_pairs={{0,4},{8,12},{16,20},{24,28},{32,36},{40,44},{48,52},{56,60},{64,6... | collective-permute-start | bytes 1572872 | tf_op jit(solution)/shard_map/ppermute | solution.py:17
  56.5 63.0 %copy-start.11 = (f32[256,256]{1,0:T(8,128)}, f32[256,256]{1,0:T(8,128)S(1)}, u32[]{:S(2)}) copy-start(f32[256,256]{1,0:T(8,128)S(1)} %broadcast_select_fusion.12) | copy-start | bytes 786436
  113.1 19.8 %collective-permute-start.5 = (f32[256,512]{1,0:T(8,128)}, f32[256,512]{1,0:T(8,128)S(1)}, u32[]{:S(2)}, u32[]{:S(2)}) collective-permute-start(f32[256,512]{1,0:T(8,128)} %broadcast_select_fusion.9), channel_id=1, source_target_pairs={{0,16},{32,48},{1,17},{33,49},{2,18},{34,50},{3,19},{35,51},{4,20}... | collective-permute-start | bytes 1572872 | tf_op jit(solution)/shard_map/ppermute | solution.py:17
  116.1 15.8 %collective-permute-start.3 = (f32[256,256]{1,0:T(8,128)S(1)}, f32[256,256]{1,0:T(8,128)S(1)}, u32[]{:S(2)}, u32[]{:S(2)}) collective-permute-start(f32[256,256]{1,0:T(8,128)S(1)} %broadcast_select_fusion.12), channel_id=1, source_target_pairs={{0,16},{32,48},{64,80},{96,112},{128,144},{160,176},{192,208},{224... | collective-permute-start | bytes 786440 | tf_op jit(solution)/shard_map/ppermute | solution.py:17
  117.4 23.7 %collective-permute-start.4 = (f32[512,256]{1,0:T(8,128)}, f32[512,256]{1,0:T(8,128)}, u32[]{:S(2)}, u32[]{:S(2)}) collective-permute-start(f32[512,256]{1,0:T(8,128)} %broadcast_select_fusion.10), channel_id=1, source_target_pairs={{0,2},{4,6},{8,10},{12,14},{16,18},{20,22},{24,26},{28,30},{32,34}... | collective-permute-start | bytes 1572872 | tf_op jit(solution)/shard_map/ppermute | solution.py:17
  142.2 22.3 %collective-permute-start.8 = (f32[256,512]{1,0:T(8,128)S(1)}, f32[256,512]{1,0:T(8,128)}, u32[]{:S(2)}, u32[]{:S(2)}) collective-permute-start(f32[256,512]{1,0:T(8,128)S(1)} %broadcast_select_fusion.6), channel_id=1, source_target_pairs={{0,8},{16,24},{32,40},{48,56},{1,9},{17,25},{33,41},{49,57},{2,10}... | collective-permute-start | bytes 1572872 | tf_op jit(solution)/shard_map/ppermute | solution.py:17
  147.3 17.2 %collective-permute-start.6 = (f32[256,256]{1,0:T(8,128)S(1)}, f32[256,256]{1,0:T(8,128)}, u32[]{:S(2)}, u32[]{:S(2)}) collective-permute-start(f32[256,256]{1,0:T(8,128)S(1)} %broadcast_select_fusion.13), channel_id=1, source_target_pairs={{0,8},{16,24},{32,40},{48,56},{64,72},{80,88},{96,104},{112,120},{... | collective-permute-start | bytes 786440 | tf_op jit(solution)/shard_map/ppermute | solution.py:17
  149.3 23.6 %collective-permute-start.7 = (f32[512,256]{1,0:T(8,128)S(1)}, f32[512,256]{1,0:T(8,128)}, u32[]{:S(2)}, u32[]{:S(2)}) collective-permute-start(f32[512,256]{1,0:T(8,128)S(1)} %broadcast_select_fusion.7), channel_id=1, source_target_pairs={{0,1},{2,3},{4,5},{6,7},{8,9},{10,11},{12,13},{14,15},{16,17},{18,... | collective-permute-start | bytes 1572872 | tf_op jit(solution)/shard_map/ppermute | solution.py:17
  173.8 61.2 %copy-start.10 = (f32[256,512]{1,0:T(8,128)S(1)}, f32[256,512]{1,0:T(8,128)}, u32[]{:S(2)}) copy-start(f32[256,512]{1,0:T(8,128)} %broadcast_select_fusion.3) | copy-start | bytes 1572868
  173.8 63.4 %copy-start.9 = (f32[512,256]{1,0:T(8,128)S(1)}, f32[512,256]{1,0:T(8,128)}, u32[]{:S(2)}) copy-start(f32[512,256]{1,0:T(8,128)} %broadcast_select_fusion.4) | copy-start | bytes 1572868
  173.8 35.6 %collective-permute-start.9 = (f32[256,256]{1,0:T(8,128)S(1)}, f32[256,256]{1,0:T(8,128)S(1)}, u32[]{:S(2)}, u32[]{:S(2)}) collective-permute-start(f32[256,256]{1,0:T(8,128)S(1)} %broadcast_select_fusion.15), channel_id=1, source_target_pairs={{0,4},{8,12},{16,20},{24,28},{32,36},{40,44},{48,52},{56,60},{64,6... | collective-permute-start | bytes 786440 | tf_op jit(solution)/shard_map/ppermute | solution.py:17
  209.4 6.5 %collective-permute-start.10 = (f32[256,256]{1,0:T(8,128)S(1)}, f32[256,256]{1,0:T(8,128)S(1)}, u32[]{:S(2)}, u32[]{:S(2)}) collective-permute-start(f32[256,256]{1,0:T(8,128)S(1)} %broadcast_select_fusion.17), channel_id=1, source_target_pairs={{0,2},{4,6},{8,10},{12,14},{16,18},{20,22},{24,26},{28,30},{32,34}... | collective-permute-start | bytes 786440 | tf_op jit(solution)/shard_map/ppermute | solution.py:17
  215.9 5.8 %collective-permute-start.11 = (f32[256,256]{1,0:T(8,128)S(1)}, f32[256,256]{1,0:T(8,128)}, u32[]{:S(2)}, u32[]{:S(2)}) collective-permute-start(f32[256,256]{1,0:T(8,128)S(1)} %broadcast_select_fusion.19), channel_id=1, source_target_pairs={{0,1},{2,3},{4,5},{6,7},{8,9},{10,11},{12,13},{14,15},{16,17},{18,... | collective-permute-start | bytes 786440 | tf_op jit(solution)/shard_map/ppermute | solution.py:17
  238.5 2.5 copy-start.8
  241.0 1.3 copy-start.4
  290.3 155.3 %all-to-all-start.1 = ((f32[8,512,128]{2,1,0:T(8,128)}), f32[8,512,128]{2,1,0:T(8,128)S(1)}, u32[]{:S(2)}, u32[]{:S(2)}) async-start(f32[8,512,128]{2,1,0:T(8,128)} %bitcast.75), calls=%async_computation.1 | async-start | bytes 4194304 | tf_op jit(solution)/shard_map/all_to_all | solution.py:369
  295.5 96.3 %collective-permute-start.12 = (f32[4,32,128]{2,1,0:T(8,128)S(1)}, f32[4,32,128]{2,1,0:T(8,128)S(1)}, u32[]{:S(2)}, u32[]{:S(2)}) collective-permute-start(f32[4,32,128]{2,1,0:T(8,128)S(1)} %row_pick.1), channel_id=1, source_target_pairs={{0,4},{1,5},{2,6},{3,7},{4,0},{5,1},{6,2},{7,3},{8,12},{9,13},{10,... | collective-permute-start | bytes 196616 | tf_op jit(solution)/shard_map/ppermute | solution.py:17
  393.4 3.1 collective-permute-start.13
  396.6 17.1 %collective-permute-start.15 = (f32[2,4,32,128]{3,2,1,0:T(8,128)S(1)}, f32[2,4,32,128]{3,2,1,0:T(8,128)S(1)}, u32[]{:S(2)}, u32[]{:S(2)}) collective-permute-start(f32[2,4,32,128]{3,2,1,0:T(8,128)S(1)} %pad_maximum_fusion.5), channel_id=1, source_target_pairs={{0,8},{8,0},{16,24},{24,16},{32,40},{40,32},{48,56},{56,48},{1,9},... | collective-permute-start | bytes 393224 | tf_op jit(solution)/shard_map/ppermute | solution.py:17
  399.1 14.5 %collective-permute-start.14 = (f32[2,4,32,128]{3,2,1,0:T(8,128)S(1)}, f32[2,4,32,128]{3,2,1,0:T(8,128)S(1)}, u32[]{:S(2)}, u32[]{:S(2)}) collective-permute-start(f32[2,4,32,128]{3,2,1,0:T(8,128)S(1)} %pad_maximum_fusion.4), channel_id=1, source_target_pairs={{0,2},{1,3},{2,0},{3,1},{4,6},{5,7},{6,4},{7,5},{8,10},{9,11},{10,... | collective-permute-start | bytes 393224 | tf_op jit(solution)/shard_map/ppermute | solution.py:17
  413.7 8.6 %collective-permute-start.17 = (f32[2,2,4,32,128]{4,3,2,1,0:T(8,128)S(1)}, f32[2,2,4,32,128]{4,3,2,1,0:T(8,128)S(1)}, u32[]{:S(2)}, u32[]{:S(2)}) collective-permute-start(f32[2,2,4,32,128]{4,3,2,1,0:T(8,128)S(1)} %get-tuple-element.68), channel_id=1, source_target_pairs={{0,16},{8,24},{16,0},{24,8},{32,48},{40,56},{48,32},{56,40},{1,17}... | collective-permute-start | bytes 786440 | tf_op jit(solution)/shard_map/ppermute | solution.py:17
  416.1 8.7 %collective-permute-start.16 = (f32[2,2,4,32,128]{4,3,2,1,0:T(8,128)S(1)}, f32[2,2,4,32,128]{4,3,2,1,0:T(8,128)S(1)}, u32[]{:S(2)}, u32[]{:S(2)}) collective-permute-start(f32[2,2,4,32,128]{4,3,2,1,0:T(8,128)S(1)} %get-tuple-element.67), channel_id=1, source_target_pairs={{0,1},{1,0},{2,3},{3,2},{4,5},{5,4},{6,7},{7,6},{8,9},{9,8},{10,11... | collective-permute-start | bytes 786440 | tf_op jit(solution)/shard_map/ppermute | solution.py:17
  424.9 15.4 %collective-permute-start.18 = (f32[2,2,2,4,32,128]{5,4,3,2,1,0:T(8,128)S(1)}, f32[2,2,2,4,32,128]{5,4,3,2,1,0:T(8,128)}, u32[]{:S(2)}, u32[]{:S(2)}) collective-permute-start(f32[2,2,2,4,32,128]{5,4,3,2,1,0:T(8,128)S(1)} %pad_maximum_fusion.1), channel_id=1, source_target_pairs={{0,32},{8,40},{16,48},{24,56},{32,0},{40,8},{48,16},{56,24},{1,33}... | collective-permute-start | bytes 1572872 | tf_op jit(solution)/shard_map/ppermute | solution.py:17
  429.2 14.2 %collective-permute-start.19 = (f32[256,512]{1,0:T(8,128)S(1)}, f32[256,512]{1,0:T(8,128)S(1)}, u32[]{:S(2)}, u32[]{:S(2)}) collective-permute-start(f32[256,512]{1,0:T(8,128)S(1)} %bitcast.83), channel_id=1, source_target_pairs={{0,64},{64,0},{128,192},{192,128},{256,320},{320,256},{384,448},{4... | collective-permute-start | bytes 1572872 | tf_op jit(solution)/shard_map/ppermute | solution.py:17
  445.6 6.0 %copy-start.6 = (f32[512,512]{1,0:T(8,128)S(1)}, f32[512,512]{1,0:T(8,128)}, u32[]{:S(2)}) copy-start(f32[512,512]{1,0:T(8,128)} %fusion.2.pair_ref) | copy-start | bytes 3145732
  445.6 6.0 %copy-start.7 = (bf16[1024,512]{1,0:T(8,128)(2,1)S(1)}, bf16[1024,512]{1,0:T(8,128)(2,1)}, u32[]{:S(2)}) copy-start(bf16[1024,512]{1,0:T(8,128)(2,1)} %parent_ref.1) | copy-start | bytes 3145732
  447.0 4.6 collective-permute-start.20
  456.2 17.3 %collective-permute-start.21 = (f32[256,256]{1,0:T(8,128)S(1)}, f32[256,256]{1,0:T(8,128)S(1)}, u32[]{:S(2)}, u32[]{:S(2)}) collective-permute-start(f32[256,256]{1,0:T(8,128)S(1)} %slice.36), channel_id=1, source_target_pairs={{0,16},{128,144},{256,272},{384,400}} | collective-permute-start | bytes 786440 | tf_op jit(solution)/shard_map/ppermute | solution.py:17
  459.8 13.7 %collective-permute-start.22 = (f32[256,256]{1,0:T(8,128)S(1)}, f32[256,256]{1,0:T(8,128)S(1)}, u32[]{:S(2)}, u32[]{:S(2)}) collective-permute-start(f32[256,256]{1,0:T(8,128)S(1)} %slice.36), channel_id=1, source_target_pairs={{0,32},{128,160},{256,288},{384,416}} | collective-permute-start | bytes 786440 | tf_op jit(solution)/shard_map/ppermute | solution.py:17
  461.1 12.4 %collective-permute-start.23 = (f32[256,256]{1,0:T(8,128)S(1)}, f32[256,256]{1,0:T(8,128)}, u32[]{:S(2)}, u32[]{:S(2)}) collective-permute-start(f32[256,256]{1,0:T(8,128)S(1)} %slice.36), channel_id=1, source_target_pairs={{0,48},{128,176},{256,304},{384,432}} | collective-permute-start | bytes 786440 | tf_op jit(solution)/shard_map/ppermute | solution.py:17
  463.1 22.4 %collective-permute-start.25 = (f32[1024,256]{1,0:T(8,128)S(1)}, f32[1024,256]{1,0:T(8,128)S(1)}, u32[]{:S(2)}, u32[]{:S(2)}) collective-permute-start(f32[1024,256]{1,0:T(8,128)S(1)} %slice.37), channel_id=1, source_target_pairs={{0,4},{128,132},{256,260},{384,388},{8,12},{136,140},{264,268},{39... | collective-permute-start | bytes 3145736 | tf_op jit(solution)/shard_map/ppermute | solution.py:17
  469.4 16.1 %collective-permute-start.26 = (f32[256,512]{1,0:T(8,128)S(1)}, f32[256,512]{1,0:T(8,128)S(1)}, u32[]{:S(2)}, u32[]{:S(2)}) collective-permute-start(f32[256,512]{1,0:T(8,128)S(1)} %slice.38), channel_id=1, source_target_pairs={{0,32},{1,33},{2,34},{3,35},{4,36},{5,37},{6,38},{7,39},{64,96},{6... | collective-permute-start | bytes 1572872 | tf_op jit(solution)/shard_map/ppermute | solution.py:17
  474.5 9.9 %collective-permute-start.24 = (f32[256,256]{1,0:T(8,128)S(1)}, f32[256,256]{1,0:T(8,128)S(1)}, u32[]{:S(2)}, u32[]{:S(2)}) collective-permute-start(f32[256,256]{1,0:T(8,128)S(1)} %add_select_fusion), channel_id=1, source_target_pairs={{0,8},{16,24},{32,40},{48,56},{128,136},{144,152},{160,168},{176,1... | collective-permute-start | bytes 786440 | tf_op jit(solution)/shard_map/ppermute | solution.py:17
  485.7 22.2 %collective-permute-start.28 = (f32[1024,256]{1,0:T(8,128)S(1)}, f32[1024,256]{1,0:T(8,128)S(1)}, u32[]{:S(2)}, u32[]{:S(2)}) collective-permute-start(f32[1024,256]{1,0:T(8,128)S(1)} %broadcast_select_fusion.2), channel_id=1, source_target_pairs={{0,2},{4,6},{128,130},{132,134},{256,258},{260,262},{384,386},{388... | collective-permute-start | bytes 3145736 | tf_op jit(solution)/shard_map/ppermute | solution.py:17
  487.0 20.7 %collective-permute-start.29 = (f32[256,512]{1,0:T(8,128)S(1)}, f32[256,512]{1,0:T(8,128)S(1)}, u32[]{:S(2)}, u32[]{:S(2)}) collective-permute-start(f32[256,512]{1,0:T(8,128)S(1)} %broadcast_select_fusion.8), channel_id=1, source_target_pairs={{0,16},{32,48},{1,17},{33,49},{2,18},{34,50},{3,19},{35,51},{4,20}... | collective-permute-start | bytes 1572872 | tf_op jit(solution)/shard_map/ppermute | solution.py:17
  489.7 18.0 %collective-permute-start.27 = (f32[256,256]{1,0:T(8,128)S(1)}, f32[256,256]{1,0:T(8,128)S(1)}, u32[]{:S(2)}, u32[]{:S(2)}) collective-permute-start(f32[256,256]{1,0:T(8,128)S(1)} %broadcast_select_fusion.14), channel_id=1, source_target_pairs={{0,4},{128,132},{256,260},{384,388},{8,12},{136,140},{264,268},{39... | collective-permute-start | bytes 786440 | tf_op jit(solution)/shard_map/ppermute | solution.py:17
  508.0 16.4 %collective-permute-start.31 = (f32[1024,256]{1,0:T(8,128)S(1)}, f32[1024,256]{1,0:T(8,128)S(1)}, u32[]{:S(2)}, u32[]{:S(2)}) collective-permute-start(f32[1024,256]{1,0:T(8,128)S(1)} %broadcast_select_fusion.1), channel_id=1, source_target_pairs={{0,1},{2,3},{4,5},{6,7},{128,129},{130,131},{132,133},{134,135},{2... | collective-permute-start | bytes 3145736 | tf_op jit(solution)/shard_map/ppermute | solution.py:17
  509.3 15.0 %collective-permute-start.30 = (f32[256,256]{1,0:T(8,128)S(1)}, f32[256,256]{1,0:T(8,128)S(1)}, u32[]{:S(2)}, u32[]{:S(2)}) collective-permute-start(f32[256,256]{1,0:T(8,128)S(1)} %broadcast_select_fusion.16), channel_id=1, source_target_pairs={{0,2},{4,6},{128,130},{132,134},{256,258},{260,262},{384,386},{388... | collective-permute-start | bytes 786440 | tf_op jit(solution)/shard_map/ppermute | solution.py:17
  524.6 26.3 %collective-permute-start.33 = (f32[256,256]{1,0:T(8,128)S(1)}, f32[256,256]{1,0:T(8,128)S(1)}, u32[]{:S(2)}, u32[]{:S(2)}) collective-permute-start(f32[256,256]{1,0:T(8,128)S(1)} %broadcast_select_fusion.18), channel_id=1, source_target_pairs={{0,1},{2,3},{4,5},{6,7},{128,129},{130,131},{132,133},{134,135},{2... | collective-permute-start | bytes 786440 | tf_op jit(solution)/shard_map/ppermute | solution.py:17
  526.1 42.2 %collective-permute-start.32 = (f32[1024,256]{1,0:T(8,128)S(1)}, f32[1024,256]{1,0:T(8,128)S(1)}, u32[]{:S(2)}, u32[]{:S(2)}) collective-permute-start(f32[1024,256]{1,0:T(8,128)S(1)} %broadcast_select_fusion), channel_id=1, source_target_pairs={{0,64},{128,192},{256,320},{384,448},{1,65},{129,193},{257,321},{3... | collective-permute-start | bytes 3145736 | tf_op jit(solution)/shard_map/ppermute | solution.py:17
  527.5 39.2 %collective-permute-start.35 = (f32[256,512]{1,0:T(8,128)S(1)}, f32[256,512]{1,0:T(8,128)S(1)}, u32[]{:S(2)}, u32[]{:S(2)}) collective-permute-start(f32[256,512]{1,0:T(8,128)S(1)} %broadcast_select_fusion.5), channel_id=1, source_target_pairs={{0,8},{16,24},{32,40},{48,56},{1,9},{17,25},{33,41},{49,57},{2,10}... | collective-permute-start | bytes 1572872 | tf_op jit(solution)/shard_map/ppermute | solution.py:17
  550.9 2.6 collective-permute-start.34
  568.3 2.9 copy-start.1
  (2 other events, 2.5 us)

commit v5 on v4

--- a/solution.py
+++ b/solution.py
@@ -173,8 +173,8 @@
     lax.fori_loop(0, count, body, jnp.int32(0))
 
 
-def assemble_kernel(sizes, ids_ref, map_ref, pair_map_ref, parent_ref, own_ref, pair_ref,
-                    other_ref, landed_ref, out_ref, rank_ref, at_ref, pair_at_ref):
+def assemble_kernel(sizes, ids_ref, map_ref, pair_map_ref, parent_ref, other_ref, landed_ref,
+                    out_ref, diagonal_ref, slab_ref, top_ref, rank_ref, at_ref, pair_at_ref):
     row_span, col_span, first, col_blocks, cols, count = sizes
     half, row, col = ids_ref[0], ids_ref[1], ids_ref[2]
     out_ref[...] = parent_ref[...].astype(jnp.float32)
@@ -182,14 +182,6 @@
     row_tables(map_ref, row, row_span, count, rank_ref, at_ref)
     caps = at_ref.shape[0]
     for m in range(caps):
-        for table, product in ((at_ref, own_ref), (pair_at_ref, pair_ref)):
-            at = table[m]
-
-            @pl.when(at >= 0)
-            def _():
-                spot = (pl.ds(pl.multiple_of(at * BLK, BLK), BLK), slice(None))
-                out_ref[spot] = out_ref[spot] - product[m * BLK : (m + 1) * BLK, :]
-
         at = pair_at_ref[m]
 
         @pl.when(at >= 0)
@@ -217,66 +209,10 @@
         return carry
 
     lax.fori_loop(0, count, body, jnp.int32(0))
-
-
-def row_slots_kernel(sizes, ids_ref, map_ref, part_ref, out_ref):
-    row_span, first, row_blocks = sizes
-    row = ids_ref[1]
-    for a in range(row_blocks):
-        block = row * row_blocks + a - first
-
-        @pl.when(block >= 0)
-        def _():
-            target = map_ref[jnp.maximum(block, 0)] // row_span
-            out_ref[target] = part_ref[:, a * BLK : (a + 1) * BLK]
-
-
-def col_slots_kernel(sizes, ids_ref, map_ref, part_ref, out_ref):
-    col_span, first, col_blocks, cols = sizes
-    col = ids_ref[2]
-    for y in range(col_blocks):
-        block = col * col_blocks + y - first
-
-        @pl.when(block >= 0)
-        def _():
-            target = (map_ref[jnp.maximum(block, 0)] // col_span) % cols
-            out_ref[target] = part_ref[:, y * BLK : (y + 1) * BLK]
-
-
-def row_pick_kernel(sizes, ids_ref, map_ref, got_ref, out_ref, rank_ref, at_ref):
-    row_span, first, row_blocks, count = sizes
-    row_tables(map_ref, ids_ref[1], row_span, count, rank_ref, at_ref)
-    out_ref[...] = jnp.zeros_like(out_ref)
-
-    def body(k, carry):
-        rank = rank_ref[k]
-
-        @pl.when(rank >= 0)
-        def _():
-            out_ref[jnp.minimum(rank, out_ref.shape[0] - 1)] = got_ref[(k + first) // row_blocks]
-
-        return carry
-
-    lax.fori_loop(0, count, body, jnp.int32(0))
-
-
-def col_pick_kernel(sizes, ids_ref, map_ref, got_ref, own_ref, other_ref):
-    col_span, first, col_blocks, cols, count = sizes
-    half, col = ids_ref[0], ids_ref[2]
-    own_ref[...] = jnp.zeros_like(own_ref)
-    other_ref[...] = jnp.zeros_like(other_ref)
-
-    def body(k, carry):
-        owner = map_ref[k] // col_span
-        for target, wanted in ((own_ref, half), (other_ref, 1 - half)):
-
-            @pl.when((owner % cols == col) & (owner // cols == wanted))
-            def _():
-                target[map_ref[k] % col_span] = got_ref[(k + first) // col_blocks]
-
-        return carry
-
-    lax.fori_loop(0, count, body, jnp.int32(0))
+    width = diagonal_ref.shape[0]
+    diagonal_ref[...] = out_ref[:width, :width]
+    slab_ref[...] = out_ref[:, :width]
+    top_ref[...] = out_ref[:width, :]
 
 
 def kernel_call(body, name, outs, n_smem, n_vmem, scratch=()):
@@ -317,46 +253,68 @@
     cap = -(-count // row_count)
     swap = [(i, i ^ 1) for i in range(leaf_count)]
 
-    def only(cell, got, value, targets):
-        index = lax.axis_index(cell)
+    def only(axis, got, value, targets):
+        index = lax.axis_index(axis)
         hit = functools.reduce(jnp.logical_or, [index == t for t in targets])
         return jnp.where(hit, got, value)
+
+    def after(value, earlier):
+        return lax.optimization_barrier((value, earlier))[0]
+
+    grid = row_count * col_count
+    zhi = [(r, r + 1) for r in range(0, row_count, 2)]
+    fan = list(range(2, row_count, 2))
+
+    def panel_parts(diagonal, slab, top, leaves, paired):
+        def down(value, pairs):
+            moves = [
+                (l * grid + r * col_count, l * grid + q * col_count)
+                for l in leaves for r, q in pairs
+            ]
+            return send(value, ("leaf", "row", "col"), moves)
+
+        def along(value, pairs):
+            moves = [(l * col_count + r, l * col_count + q) for l in leaves for r, q in pairs]
+            got = send(value, ("leaf", "col"), moves)
+            return only("col", got, value, [q for _, q in pairs])
+
+        def over(value, pairs):
+            return only("row", send(value, "row", pairs), value, [q for _, q in pairs])
+
+        first_hop = functools.reduce(jnp.add, [down(diagonal, [(0, q)]) for q in fan])
+        d1 = only("row", first_hop, diagonal, fan)
+        slab1 = along(slab, HALVING[0])
+        top1 = over(top, HALVING[0])
+        d2 = only("row", down(d1, zhi), d1, [q for _, q in zhi])
+        d3 = along(d2, HALVING[0])
+        slab2 = along(after(slab1, d2), HALVING[1])
+        top2 = over(after(top1, d2), HALVING[1])
+        d4 = along(d3, HALVING[1])
+        slab3 = along(after(slab2, d3), HALVING[2])
+        top3 = over(after(top2, d3), HALVING[2])
+        d5 = along(d4, HALVING[2])
+        if paired:
+            across = [(l, l + 1) for l in leaves]
+            d5 = jnp.where(half_id == 0, d5, send(d5, "leaf", across))
+            slab3 = jnp.where(half_id == 0, slab3, send(slab3, "leaf", across))
+        return d5, slab3, top3
+
+    diagonal, slab, top = panel_parts(
+        child_block[:width, :width], child_block[:, :width], child_block[:width],
+        list(range(leaf_count)), False,
+    )
+    inverse = inverse_factor(diagonal)
+    rows_factor = lax.dot_general(slab, inverse, (((1,), (1,)), ((), ())), precision=HIGHEST)
+    cols_factor = jnp.dot(inverse, top, precision=HIGHEST)
+    contribution = child_block - jnp.dot(rows_factor, cols_factor, precision=HIGHEST)
+    out_width = width // col_count
+    child_out = lax.dynamic_slice_in_dim(rows_factor, col_id * out_width, out_width, 1).T
 
     strips = kernel_call(
         functools.partial(strips_kernel, (row_span, first, row_blocks)),
         "strips", (row_count, BLK, child_cols), 2, 1,
-    )(ids, own_map, child_block)
-    strips, child_block = lax.optimization_barrier((strips, child_block))
+    )(ids, own_map, contribution)
     got = lax.all_to_all(strips, "row", 0, 0, tiled=True)
-
-    def by_rows(pairs):
-        return [(r * col_count, q * col_count) for r, q in pairs]
-
-    diagonal, slab, top = child_block[:width, :width], child_block[:, :width], child_block[:width]
-    for pairs in HALVING:
-        targets = [t for _, t in pairs]
-        diagonal = only("row", send(diagonal, ("row", "col"), by_rows(pairs)), diagonal, targets)
-        slab = only("col", send(slab, "col", pairs), slab, targets)
-        top = only("row", send(top, "row", pairs), top, targets)
-        diagonal, slab, top = lax.optimization_barrier((diagonal, slab, top))
-    for pairs in HALVING:
-        diagonal = only("col", send(diagonal, "col", pairs), diagonal, [t for _, t in pairs])
-    inverse = inverse_factor(diagonal)
-    cols_factor = jnp.dot(inverse, top, precision=HIGHEST)
-    out_width = width // col_count
-    share = lax.dynamic_slice_in_dim(inverse, col_id * out_width, out_width, 0)
-    child_out = lax.dot_general(share, slab, (((1,), (1,)), ((), ())), precision=HIGHEST)
-    piece = (out_width, BLK)
-    row_slots = kernel_call(
-        functools.partial(row_slots_kernel, (row_span, first, row_blocks)),
-        "row_slots", (row_count,) + piece, 2, 1,
-    )(ids, own_map, child_out)
-    col_share = lax.dynamic_slice_in_dim(cols_factor, row_id * out_width, out_width, 0)
-    col_slots = kernel_call(
-        functools.partial(col_slots_kernel, (col_span, first, col_blocks, col_count)),
-        "col_slots", (col_count,) + piece, 2, 1,
-    )(ids, own_map, col_share)
-    got, row_slots, col_slots = lax.optimization_barrier((got, row_slots, col_slots))
     tables = [pltpu.SMEM((count,), jnp.int32), pltpu.SMEM((cap,), jnp.int32)]
     tiles = kernel_call(
         functools.partial(
@@ -365,107 +323,31 @@
         ),
         "tiles", (col_count, cap, BLK, BLK), 2, 1, tables,
     )(ids, own_map, got)
-    tiles, row_slots, col_slots = lax.optimization_barrier((tiles, row_slots, col_slots))
     landed = lax.all_to_all(
         tiles.reshape(col_count, cap * BLK, BLK), "col", 0, 0, tiled=True
     ).reshape(tiles.shape)
-
-    row_got = lax.all_to_all(row_slots, "row", 0, 0, tiled=True)
-    col_slots, row_got = lax.optimization_barrier((col_slots, row_got))
-    col_got = lax.all_to_all(col_slots, "col", 0, 0, tiled=True)
-    row_panel = kernel_call(
-        functools.partial(row_pick_kernel, (row_span, first, row_blocks, count)),
-        "row_pick", (cap,) + piece, 2, 1, tables,
-    )(ids, own_map, row_got)
-    own_cols, other_cols = kernel_call(
-        functools.partial(col_pick_kernel, (col_span, first, col_blocks, col_count, count)),
-        "col_pick", [(col_span,) + piece] * 2, 2, 1,
-    )(ids, own_map, col_got)
-
-    def doubled(value, axis, bit):
-        got = send(value, axis, [(i, i ^ (1 << bit)) for i in range(lax.axis_size(axis))])
-        upper = (lax.axis_index(axis) >> bit) & 1
-        low = jnp.where(upper == 0, value, got)
-        high = jnp.where(upper == 0, got, value)
-        return jnp.stack([low, high])
-
-    row_panel = doubled(row_panel, "col", 2)
-    col_panels = jnp.stack([own_cols, send(other_cols, "leaf", swap)])
-    row_panel, col_panels = lax.optimization_barrier((row_panel, col_panels))
-    row_panel = doubled(row_panel, "col", 1)
-    col_panels = doubled(col_panels, "row", 0)
-    row_panel, col_panels = lax.optimization_barrier((row_panel, col_panels))
-    row_panel = doubled(row_panel, "col", 0)
-    col_panels = doubled(col_panels, "row", 1)
-    row_panel, col_panels = lax.optimization_barrier((row_panel, col_panels))
-    row_panel = jnp.transpose(row_panel, (2, 1, 0, 4, 3, 5)).reshape(width, cap * BLK)
-    pair_row_panel = send(row_panel, "leaf", swap)
-    col_panels = doubled(col_panels, "row", 2)
-    col_panels = jnp.transpose(col_panels, (3, 0, 1, 2, 5, 4, 6))
-    col_panels = col_panels.reshape(2, width, col_span * BLK)
-
-    def product(rows, cols):
-        return lax.dot_general(rows, cols, (((0,), (0,)), ((), ())), precision=HIGHEST)
-
-    own_product = product(row_panel, col_panels[0])
-    pair_product = product(pair_row_panel, col_panels[1])
-    landed, own_product, pair_product = lax.optimization_barrier(
-        (landed, own_product, pair_product)
-    )
     other = kernel_call(
         functools.partial(other_kernel, (col_span, first, col_blocks, col_count, count)),
         "other", (col_span, cap, BLK, BLK), 2, 1,
     )(ids, own_map, landed)
     other = send(other, "leaf", swap)
-    assembled = kernel_call(
+
+    parent_order = parent_rows * row_count
+    parent_width = parent_cols // 2
+    assembled, diagonal, slab, top = kernel_call(
         functools.partial(
             assemble_kernel, (row_span, col_span, first, col_blocks, col_count, count)
         ),
-        "assemble", parent_front.shape, 3, 5,
-        tables + [pltpu.SMEM((cap,), jnp.int32)],
-    )(ids, own_map, partner_map, parent_front, own_product, pair_product, other, landed)
-
-    parent_order = parent_rows * row_count
-    parent_width = parent_cols // 2
-    even = range(0, leaf_count, 2)
-    grid = row_count * col_count
-    across = [(l, l + 1) for l in even]
-    diagonal = assembled[:parent_width, :parent_width]
-    slab, top = assembled[:, :parent_width], assembled[:parent_width]
-    diagonal, slab, top = lax.optimization_barrier((diagonal, slab, top))
-
-    def spread_rows(value, pairs):
-        moves = [
-            (l * grid + r * col_count, l * grid + q * col_count) for l in even for r, q in pairs
-        ]
-        return send(value, ("leaf", "row", "col"), moves)
-
-    def spread_cols(value, pairs):
-        moves = [(l * col_count + r, l * col_count + q) for l in even for r, q in pairs]
-        return only("col", send(value, ("leaf", "col"), moves), value, [q for _, q in pairs])
-
-    def spread_top(value, pairs):
-        return only("row", send(value, "row", pairs), value, [q for _, q in pairs])
-
-    fan = [spread_rows(diagonal, [(0, q)]) for q in (2, 4, 6)]
-    diagonal = only("row", functools.reduce(jnp.add, fan), diagonal, (2, 4, 6))
-    slab = spread_cols(slab, HALVING[0])
-    (diagonal,) = lax.optimization_barrier([diagonal])
-    zhi = [(0, 1), (2, 3), (4, 5), (6, 7)]
-    diagonal = only("row", spread_rows(diagonal, zhi), diagonal, (1, 3, 5, 7))
-    top = spread_top(top, HALVING[0])
-    diagonal, slab, top = lax.optimization_barrier((diagonal, slab, top))
-    diagonal = spread_cols(diagonal, HALVING[0])
-    slab = spread_cols(slab, HALVING[1])
-    top = spread_top(top, HALVING[1])
-    diagonal, slab, top = lax.optimization_barrier((diagonal, slab, top))
-    diagonal = spread_cols(diagonal, HALVING[1])
-    slab = spread_cols(slab, HALVING[2])
-    top = spread_top(top, HALVING[2])
-    diagonal, slab = lax.optimization_barrier((diagonal, slab))
-    diagonal = spread_cols(diagonal, HALVING[2])
-    diagonal = jnp.where(half_id == 0, diagonal, send(diagonal, "leaf", across))
-    slab = jnp.where(half_id == 0, slab, send(slab, "leaf", across))
+        "assemble",
+        [
+            parent_front.shape, (parent_width, parent_width),
+            (parent_rows, parent_width), (parent_width, parent_cols),
+        ],
+        3, 3, tables + [pltpu.SMEM((cap,), jnp.int32)],
+    )(ids, own_map, partner_map, parent_front, other, landed)
+    diagonal, slab, top = panel_parts(
+        diagonal, slab, top, list(range(0, leaf_count, 2)), True
+    )
     inverse = inverse_factor(diagonal)
     rows_factor = lax.dot_general(slab, inverse, (((1,), (1,)), ((), ())), precision=HIGHEST)
     cols_factor = jnp.dot(inverse, top, precision=HIGHEST)

time: 585 us -> 458 us (0.78)
  waiting for transfers between devices: 284 us -> 59.3 us
  blocking collectives: 48 us -> 235 us
  starting transfers between devices: 170 us -> 98.8 us
    ppermute x36 -> x29, waiting for transfers between devices: 284 us -> 59.3 us  [send(): return lax.ppermute(value, axes, pairs)]
    all_to_all x2, blocking collectives: 48 us -> 235 us  [the longest x1 191 us: shards(): lax.all_to_all(tiles.reshape(col_count, cap * BLK, BLK), 'col', 0, 0, til...]
    ppermute x36 -> x29, starting transfers between devices: 148 us -> 98.8 us  [send(): return lax.ppermute(value, axes, pairs)]
    all_to_all x2 -> x0, starting transfers between devices: 21.5 us -> none  [the longest x1 17.9 us: shards(): got = lax.all_to_all(strips, 'row', 0, 0, tiled=True)]
  transfers between devices with their start and end apart: 38 -> 29, of which waited for: 21 -> 12; matrix products, arithmetic and copies ran while one was open for 4% -> 3% of each run, Pallas kernels for 5% -> 5%
where the time goes in v5:
time: 458 us; the launch traced here: 452 us
  blocking collectives  235 us (51%)
  starting transfers between devices  98.8 us (22%)
  waiting for transfers between devices  59.3 us (13%)
  Pallas kernels  32.1 us (7%)
  matrix products  10.1 us (2%)
  other arithmetic  9.47 us (2%)
  local copies, waits for them, and re-layouts  5.88 us (1%)
    all_to_all x1, blocking collectives, shards(): lax.all_to_all(tiles.reshape(col_count, cap * BLK, BLK), 'col', 0, 0, til...  191 us
    ppermute x29, starting transfers between devices, send(): return lax.ppermute(value, axes, pairs)  98.8 us
    ppermute x29, waiting for transfers between devices, send(): return lax.ppermute(value, axes, pairs)  59.3 us
    all_to_all x1, blocking collectives, shards(): got = lax.all_to_all(strips, 'row', 0, 0, tiled=True)  44.4 us
    pallas_call x2, Pallas kernels, inverse_factor(): pl.pallas_call(inverse_factor_kernel, out_shape=jax.ShapeDtypeStruct(bloc...  24.9 us
  transfers between devices with their start and end apart: 29, of which 12 were waited for; matrix products, arithmetic and copies ran while one was open for 3% of the time, Pallas kernels for 5%

profile of v5, /device:TPU:6, one launch (start us, length us, event | category | flops | bytes accessed | tf_op | source)
XLA Modules:
  0.0 452.0 jit_solution(14498868414787209914)
XLA Ops:
  1.7 4.9 %collective-permute-start.3 = (f32[256,256]{1,0:T(8,128)S(1)}, f32[256,256]{1,0:T(8,128)S(1)}, u32[]{:S(2)}, u32[]{:S(2)}) collective-permute-start(f32[256,256]{1,0:T(8,128)S(1)} %slice.17), channel_id=1, source_target_pairs={{0,48},{64,112},{128,176},{192,240},{256,304},{320,368},{384,432},... | collective-permute-start | bytes 786440 | tf_op jit(solution)/shard_map/ppermute | solution.py:17
  6.6 1.3 collective-permute-start.1
  10.4 3.6 collective-permute-start
  14.6 4.5 collective-permute-done.2
  20.1 5.8 %collective-permute-start.4 = (f32[256,256]{1,0:T(8,128)S(1)}, f32[256,256]{1,0:T(8,128)S(1)}, u32[]{:S(2)}, u32[]{:S(2)}) collective-permute-start(f32[256,256]{1,0:T(8,128)S(1)} %add_select_fusion.1), channel_id=1, source_target_pairs={{0,8},{16,24},{32,40},{48,56},{64,72},{80,88},{96,104},{112,120},{... | collective-permute-start | bytes 786440 | tf_op jit(solution)/shard_map/ppermute | solution.py:17
  26.8 5.1 %collective-permute-start.10 = (f32[256,512]{1,0:T(8,128)}, f32[256,512]{1,0:T(8,128)S(1)}, u32[]{:S(2)}, u32[]{:S(2)}) collective-permute-start(f32[256,512]{1,0:T(8,128)} %slice_bitcast_fusion), channel_id=1, source_target_pairs={{0,32},{1,33},{2,34},{3,35},{4,36},{5,37},{6,38},{7,39},{64,96},{6... | collective-permute-start | bytes 1572872 | tf_op jit(solution)/shard_map/ppermute | solution.py:17
  33.4 2.1 collective-permute-start.5
  35.5 4.5 %collective-permute-done.6 = f32[256,256]{1,0:T(8,128)S(1)} collective-permute-done((f32[256,256]{1,0:T(8,128)S(1)}, f32[256,256]{1,0:T(8,128)S(1)}, u32[]{:S(2)}, u32[]{:S(2)}) %collective-permute-start.6) | collective-permute-done | bytes 262176 | tf_op jit(solution)/shard_map/ppermute | solution.py:17
  40.1 1.3 collective-permute-start.8
  41.4 1.4 collective-permute-done.10
  42.9 1.4 collective-permute-start.11
  45.1 10.1 %collective-permute-done.8 = f32[256,256]{1,0:T(8,128)S(1)} collective-permute-done((f32[256,256]{1,0:T(8,128)S(1)}, f32[256,256]{1,0:T(8,128)S(1)}, u32[]{:S(2)}, u32[]{:S(2)}) %collective-permute-start.8) | collective-permute-done | bytes 262176 | tf_op jit(solution)/shard_map/ppermute | solution.py:17
  55.2 2.0 collective-permute-start.9
  57.3 2.1 collective-permute-start.7
  59.5 12.3 %collective-permute-start.12 = (f32[256,512]{1,0:T(8,128)S(1)}, f32[256,512]{1,0:T(8,128)S(1)}, u32[]{:S(2)}, u32[]{:S(2)}) collective-permute-start(f32[256,512]{1,0:T(8,128)S(1)} %broadcast_select_fusion.6), channel_id=1, source_target_pairs={{0,8},{16,24},{32,40},{48,56},{1,9},{17,25},{33,41},{49,57},{2,10}... | collective-permute-start | bytes 1572872 | tf_op jit(solution)/shard_map/ppermute | solution.py:17
  72.6 12.4 %inverse_factor.2 = f32[256,256]{1,0:T(8,128)} custom-call(f32[256,256]{1,0:T(8,128)} %broadcast_select_fusion.13.a_ref), custom_call_target="tpu_custom_call" | custom-call | tf_op jit(solution)/shard_map/inverse_factor/pallas_call | solution.py:89
  85.1 1.6 fusion.6
  86.7 1.8 fusion.4
  90.2 44.4 %all_to_all.10.got_ref = f32[8,128,512]{2,1,0:T(8,128)S(1)} all-to-all(f32[8,128,512]{2,1,0:T(8,128)S(1)} %strips.1), channel_id=1, replica_groups=mesh['leaf'=8,'row'=8,'col'=8] {'row'}, dimensions={0} | all-to-all | bytes 4194304 | tf_op jit(solution)/shard_map/all_to_all | solution.py:317
  134.6 1.8 tiles.1
  136.4 190.9 %all_to_all.11 = f32[8,512,128]{2,1,0:T(8,128)S(1)} all-to-all(f32[8,512,128]{2,1,0:T(8,128)S(1)} %bitcast.31), channel_id=1, replica_groups=mesh['leaf'=8,'row'=8,'col'=8] {'col'}, dimensions={0} | all-to-all | bytes 4194304 | tf_op jit(solution)/shard_map/all_to_all | solution.py:326
  327.4 1.4 other.1
  328.8 1.9 collective-permute-start.13
  330.7 2.6 collective-permute-done.13.other_ref
  333.4 3.3 assemble.1
  336.7 1.9 collective-permute-start.14
  338.6 2.8 collective-permute-start.17
  345.2 2.9 collective-permute-done.15
  348.1 5.6 %collective-permute-done.16 = f32[256,256]{1,0:T(8,128)S(1)} collective-permute-done((f32[256,256]{1,0:T(8,128)S(1)}, f32[256,256]{1,0:T(8,128)S(1)}, u32[]{:S(2)}, u32[]{:S(2)}) %collective-permute-start.16) | collective-permute-done | bytes 262176 | tf_op jit(solution)/shard_map/ppermute | solution.py:17
  355.1 3.9 collective-permute-done.18
  359.2 1.4 collective-permute-start.19
  361.8 5.9 %collective-permute-start.26 = (f32[256,512]{1,0:T(8,128)S(1)}, f32[256,512]{1,0:T(8,128)S(1)}, u32[]{:S(2)}, u32[]{:S(2)}) collective-permute-start(f32[256,512]{1,0:T(8,128)S(1)} %get-tuple-element.24), channel_id=1, source_target_pairs={{0,32},{1,33},{2,34},{3,35},{4,36},{5,37},{6,38},{7,39},{64,96},{6... | collective-permute-start | bytes 1572872 | tf_op jit(solution)/shard_map/ppermute | solution.py:17
  367.8 13.4 %collective-permute-done.20 = f32[256,256]{1,0:T(8,128)S(1)} collective-permute-done((f32[256,256]{1,0:T(8,128)S(1)}, f32[256,256]{1,0:T(8,128)S(1)}, u32[]{:S(2)}, u32[]{:S(2)}) %collective-permute-start.20) | collective-permute-done | bytes 262176 | tf_op jit(solution)/shard_map/ppermute | solution.py:17
  381.4 2.3 collective-permute-start.21
  384.5 2.1 collective-permute-start.27
  386.6 2.7 collective-permute-start.23
  389.3 8.4 %collective-permute-done.23 = f32[256,256]{1,0:T(8,128)} collective-permute-done((f32[256,256]{1,0:T(8,128)S(1)}, f32[256,256]{1,0:T(8,128)}, u32[]{:S(2)}, u32[]{:S(2)}) %collective-permute-start.23) | collective-permute-done | bytes 262176 | tf_op jit(solution)/shard_map/ppermute | solution.py:17
  399.1 1.9 broadcast_select_fusion.5
  401.1 22.4 %collective-permute-start.28 = (f32[256,512]{1,0:T(8,128)}, f32[256,512]{1,0:T(8,128)}, u32[]{:S(2)}, u32[]{:S(2)}) collective-permute-start(f32[256,512]{1,0:T(8,128)} %broadcast_select_fusion.5), channel_id=1, source_target_pairs={{0,8},{16,24},{32,40},{48,56},{1,9},{17,25},{33,41},{49,57},{2,10}... | collective-permute-start | bytes 1572872 | tf_op jit(solution)/shard_map/ppermute | solution.py:17
  423.5 1.4 broadcast_select_fusion.2
  424.9 2.3 collective-permute-start.22
  427.2 2.0 collective-permute-start.25
  429.2 1.5 dynamic-slice_bitcast_fusion.1
  431.4 12.4 %inverse_factor.3 = f32[256,256]{1,0:T(8,128)} custom-call(f32[256,256]{1,0:T(8,128)} %broadcast_select_fusion.9.a_ref), custom_call_target="tpu_custom_call" | custom-call | tf_op jit(solution)/shard_map/inverse_factor/pallas_call | solution.py:89
  443.9 1.7 fusion.2
  445.6 2.1 fusion
  448.4 1.9 fusion.14
  450.2 1.8 subtract_select_fusion
  (62 shorter events, 21.5 us)
Async XLA Ops:
  0.6 25.4 %copy-start.1 = (f32[1,512,512]{2,1,0:T(8,128)S(1)}, f32[1,512,512]{2,1,0:T(8,128)}, u32[]{:S(2)}) copy-start(f32[1,512,512]{2,1,0:T(8,128)} %param.3) | copy-start | bytes 3145732
  1.7 12.3 %collective-permute-start.3 = (f32[256,256]{1,0:T(8,128)S(1)}, f32[256,256]{1,0:T(8,128)S(1)}, u32[]{:S(2)}, u32[]{:S(2)}) collective-permute-start(f32[256,256]{1,0:T(8,128)S(1)} %slice.17), channel_id=1, source_target_pairs={{0,48},{64,112},{128,176},{192,240},{256,304},{320,368},{384,432},... | collective-permute-start | bytes 786440 | tf_op jit(solution)/shard_map/ppermute | solution.py:17
  6.6 8.0 %collective-permute-start.1 = (f32[256,256]{1,0:T(8,128)S(1)}, f32[256,256]{1,0:T(8,128)S(1)}, u32[]{:S(2)}, u32[]{:S(2)}) collective-permute-start(f32[256,256]{1,0:T(8,128)S(1)} %slice.17), channel_id=1, source_target_pairs={{0,16},{64,80},{128,144},{192,208},{256,272},{320,336},{384,400},{... | collective-permute-start | bytes 786440 | tf_op jit(solution)/shard_map/ppermute | solution.py:17
  8.0 11.1 %collective-permute-start.2 = (f32[256,256]{1,0:T(8,128)S(1)}, f32[256,256]{1,0:T(8,128)S(1)}, u32[]{:S(2)}, u32[]{:S(2)}) collective-permute-start(f32[256,256]{1,0:T(8,128)S(1)} %slice.17), channel_id=1, source_target_pairs={{0,32},{64,96},{128,160},{192,224},{256,288},{320,352},{384,416},{... | collective-permute-start | bytes 786440 | tf_op jit(solution)/shard_map/ppermute | solution.py:17
  10.4 23.0 %collective-permute-start = (f32[512,256]{1,0:T(8,128)S(1)}, f32[512,256]{1,0:T(8,128)S(1)}, u32[]{:S(2)}, u32[]{:S(2)}) collective-permute-start(f32[512,256]{1,0:T(8,128)S(1)} %slice.16), channel_id=1, source_target_pairs={{0,4},{64,68},{128,132},{192,196},{256,260},{320,324},{384,388},{4... | collective-permute-start | bytes 1572872 | tf_op jit(solution)/shard_map/ppermute | solution.py:17
  20.1 11.9 %collective-permute-start.4 = (f32[256,256]{1,0:T(8,128)S(1)}, f32[256,256]{1,0:T(8,128)S(1)}, u32[]{:S(2)}, u32[]{:S(2)}) collective-permute-start(f32[256,256]{1,0:T(8,128)S(1)} %add_select_fusion.1), channel_id=1, source_target_pairs={{0,8},{16,24},{32,40},{48,56},{64,72},{80,88},{96,104},{112,120},{... | collective-permute-start | bytes 786440 | tf_op jit(solution)/shard_map/ppermute | solution.py:17
  26.8 16.0 %collective-permute-start.10 = (f32[256,512]{1,0:T(8,128)}, f32[256,512]{1,0:T(8,128)S(1)}, u32[]{:S(2)}, u32[]{:S(2)}) collective-permute-start(f32[256,512]{1,0:T(8,128)} %slice_bitcast_fusion), channel_id=1, source_target_pairs={{0,32},{1,33},{2,34},{3,35},{4,36},{5,37},{6,38},{7,39},{64,96},{6... | collective-permute-start | bytes 1572872 | tf_op jit(solution)/shard_map/ppermute | solution.py:17
  32.0 8.0 %collective-permute-start.6 = (f32[256,256]{1,0:T(8,128)S(1)}, f32[256,256]{1,0:T(8,128)S(1)}, u32[]{:S(2)}, u32[]{:S(2)}) collective-permute-start(f32[256,256]{1,0:T(8,128)S(1)} %broadcast_select_fusion.17), channel_id=1, source_target_pairs={{0,4},{64,68},{128,132},{192,196},{256,260},{320,324},{384,388},{4... | collective-permute-start | bytes 786440 | tf_op jit(solution)/shard_map/ppermute | solution.py:17
  33.4 23.8 %collective-permute-start.5 = (f32[512,256]{1,0:T(8,128)S(1)}, f32[512,256]{1,0:T(8,128)}, u32[]{:S(2)}, u32[]{:S(2)}) collective-permute-start(f32[512,256]{1,0:T(8,128)S(1)} %broadcast_select_fusion.7), channel_id=1, source_target_pairs={{0,2},{4,6},{64,66},{68,70},{128,130},{132,134},{192,194},{196,198... | collective-permute-start | bytes 1572872 | tf_op jit(solution)/shard_map/ppermute | solution.py:17
  40.1 15.1 %collective-permute-start.8 = (f32[256,256]{1,0:T(8,128)S(1)}, f32[256,256]{1,0:T(8,128)S(1)}, u32[]{:S(2)}, u32[]{:S(2)}) collective-permute-start(f32[256,256]{1,0:T(8,128)S(1)} %broadcast_select_fusion.15), channel_id=1, source_target_pairs={{0,2},{4,6},{64,66},{68,70},{128,130},{132,134},{192,194},{196,198... | collective-permute-start | bytes 786440 | tf_op jit(solution)/shard_map/ppermute | solution.py:17
  42.9 16.5 %collective-permute-start.11 = (f32[256,512]{1,0:T(8,128)S(1)}, f32[256,512]{1,0:T(8,128)S(1)}, u32[]{:S(2)}, u32[]{:S(2)}) collective-permute-start(f32[256,512]{1,0:T(8,128)S(1)} %broadcast_select_fusion.4), channel_id=1, source_target_pairs={{0,16},{32,48},{1,17},{33,49},{2,18},{34,50},{3,19},{35,51},{4,20}... | collective-permute-start | bytes 1572872 | tf_op jit(solution)/shard_map/ppermute | solution.py:17
  55.2 16.7 %collective-permute-start.9 = (f32[256,256]{1,0:T(8,128)S(1)}, f32[256,256]{1,0:T(8,128)}, u32[]{:S(2)}, u32[]{:S(2)}) collective-permute-start(f32[256,256]{1,0:T(8,128)S(1)} %broadcast_select_fusion.11), channel_id=1, source_target_pairs={{0,1},{2,3},{4,5},{6,7},{64,65},{66,67},{68,69},{70,71},{128,129},... | collective-permute-start | bytes 786440 | tf_op jit(solution)/shard_map/ppermute | solution.py:17
  57.3 27.8 %collective-permute-start.7 = (f32[512,256]{1,0:T(8,128)S(1)}, f32[512,256]{1,0:T(8,128)}, u32[]{:S(2)}, u32[]{:S(2)}) collective-permute-start(f32[512,256]{1,0:T(8,128)S(1)} %broadcast_select_fusion.8), channel_id=1, source_target_pairs={{0,1},{2,3},{4,5},{6,7},{64,65},{66,67},{68,69},{70,71},{128,129},... | collective-permute-start | bytes 1572872 | tf_op jit(solution)/shard_map/ppermute | solution.py:17
  59.5 27.3 %collective-permute-start.12 = (f32[256,512]{1,0:T(8,128)S(1)}, f32[256,512]{1,0:T(8,128)S(1)}, u32[]{:S(2)}, u32[]{:S(2)}) collective-permute-start(f32[256,512]{1,0:T(8,128)S(1)} %broadcast_select_fusion.6), channel_id=1, source_target_pairs={{0,8},{16,24},{32,40},{48,56},{1,9},{17,25},{33,41},{49,57},{2,10}... | collective-permute-start | bytes 1572872 | tf_op jit(solution)/shard_map/ppermute | solution.py:17
  86.7 2.8 copy-start.3
  327.4 6.0 %copy-start = (bf16[1024,512]{1,0:T(8,128)(2,1)S(1)}, bf16[1024,512]{1,0:T(8,128)(2,1)}, u32[]{:S(2)}) copy-start(bf16[1024,512]{1,0:T(8,128)(2,1)} %parent_ref.1) | copy-start | bytes 3145732
  328.8 4.6 %collective-permute-start.13 = (f32[4,4,128,128]{3,2,1,0:T(8,128)S(1)}, f32[4,4,128,128]{3,2,1,0:T(8,128)S(1)}, u32[]{:S(2)}, u32[]{:S(2)}) collective-permute-start(f32[4,4,128,128]{3,2,1,0:T(8,128)S(1)} %other.1), channel_id=1, source_target_pairs={{0,64},{64,0},{128,192},{192,128},{256,320},{320,256},{384,448},{4... | collective-permute-start | bytes 3145736 | tf_op jit(solution)/shard_map/ppermute | solution.py:17
  336.7 22.3 %collective-permute-start.14 = (f32[1024,256]{1,0:T(8,128)S(1)}, f32[1024,256]{1,0:T(8,128)S(1)}, u32[]{:S(2)}, u32[]{:S(2)}) collective-permute-start(f32[1024,256]{1,0:T(8,128)S(1)} %get-tuple-element.19), channel_id=1, source_target_pairs={{0,4},{128,132},{256,260},{384,388},{8,12},{136,140},{264,268},{39... | collective-permute-start | bytes 3145736 | tf_op jit(solution)/shard_map/ppermute | solution.py:17
  338.6 6.6 %collective-permute-start.17 = (f32[256,256]{1,0:T(8,128)S(1)}, f32[256,256]{1,0:T(8,128)S(1)}, u32[]{:S(2)}, u32[]{:S(2)}) collective-permute-start(f32[256,256]{1,0:T(8,128)S(1)} %get-tuple-element.20), channel_id=1, source_target_pairs={{0,48},{128,176},{256,304},{384,432}} | collective-permute-start | bytes 786440 | tf_op jit(solution)/shard_map/ppermute | solution.py:17
  341.4 6.7 %collective-permute-start.15 = (f32[256,256]{1,0:T(8,128)S(1)}, f32[256,256]{1,0:T(8,128)S(1)}, u32[]{:S(2)}, u32[]{:S(2)}) collective-permute-start(f32[256,256]{1,0:T(8,128)S(1)} %get-tuple-element.20), channel_id=1, source_target_pairs={{0,16},{128,144},{256,272},{384,400}} | collective-permute-start | bytes 786440 | tf_op jit(solution)/shard_map/ppermute | solution.py:17
  342.7 11.0 %collective-permute-start.16 = (f32[256,256]{1,0:T(8,128)S(1)}, f32[256,256]{1,0:T(8,128)S(1)}, u32[]{:S(2)}, u32[]{:S(2)}) collective-permute-start(f32[256,256]{1,0:T(8,128)S(1)} %get-tuple-element.20), channel_id=1, source_target_pairs={{0,32},{128,160},{256,288},{384,416}} | collective-permute-start | bytes 786440 | tf_op jit(solution)/shard_map/ppermute | solution.py:17
  353.8 5.2 %collective-permute-start.18 = (f32[256,256]{1,0:T(8,128)S(1)}, f32[256,256]{1,0:T(8,128)S(1)}, u32[]{:S(2)}, u32[]{:S(2)}) collective-permute-start(f32[256,256]{1,0:T(8,128)S(1)} %add_select_fusion), channel_id=1, source_target_pairs={{0,8},{16,24},{32,40},{48,56},{128,136},{144,152},{160,168},{176,1... | collective-permute-start | bytes 786440 | tf_op jit(solution)/shard_map/ppermute | solution.py:17
  359.2 22.1 %collective-permute-start.19 = (f32[1024,256]{1,0:T(8,128)S(1)}, f32[1024,256]{1,0:T(8,128)S(1)}, u32[]{:S(2)}, u32[]{:S(2)}) collective-permute-start(f32[1024,256]{1,0:T(8,128)S(1)} %broadcast_select_fusion), channel_id=1, source_target_pairs={{0,2},{4,6},{128,130},{132,134},{256,258},{260,262},{384,386},{388... | collective-permute-start | bytes 3145736 | tf_op jit(solution)/shard_map/ppermute | solution.py:17
  360.5 20.7 %collective-permute-start.20 = (f32[256,256]{1,0:T(8,128)S(1)}, f32[256,256]{1,0:T(8,128)S(1)}, u32[]{:S(2)}, u32[]{:S(2)}) collective-permute-start(f32[256,256]{1,0:T(8,128)S(1)} %broadcast_select_fusion.16), channel_id=1, source_target_pairs={{0,4},{128,132},{256,260},{384,388},{8,12},{136,140},{264,268},{39... | collective-permute-start | bytes 786440 | tf_op jit(solution)/shard_map/ppermute | solution.py:17
  361.8 21.8 %collective-permute-start.26 = (f32[256,512]{1,0:T(8,128)S(1)}, f32[256,512]{1,0:T(8,128)S(1)}, u32[]{:S(2)}, u32[]{:S(2)}) collective-permute-start(f32[256,512]{1,0:T(8,128)S(1)} %get-tuple-element.24), channel_id=1, source_target_pairs={{0,32},{1,33},{2,34},{3,35},{4,36},{5,37},{6,38},{7,39},{64,96},{6... | collective-permute-start | bytes 1572872 | tf_op jit(solution)/shard_map/ppermute | solution.py:17
  381.4 42.1 %copy-start.2 = (f32[1024,256]{1,0:T(8,128)}, f32[1024,256]{1,0:T(8,128)S(1)}, u32[]{:S(2)}) copy-start(f32[1024,256]{1,0:T(8,128)S(1)} %broadcast_select_fusion.1) | copy-start | bytes 3145732
  381.4 42.1 %collective-permute-start.21 = (f32[1024,256]{1,0:T(8,128)S(1)}, f32[1024,256]{1,0:T(8,128)}, u32[]{:S(2)}, u32[]{:S(2)}) collective-permute-start(f32[1024,256]{1,0:T(8,128)S(1)} %broadcast_select_fusion.1), channel_id=1, source_target_pairs={{0,1},{2,3},{4,5},{6,7},{128,129},{130,131},{132,133},{134,135},{2... | collective-permute-start | bytes 3145736 | tf_op jit(solution)/shard_map/ppermute | solution.py:17
  384.5 14.6 %collective-permute-start.27 = (f32[256,512]{1,0:T(8,128)}, f32[256,512]{1,0:T(8,128)}, u32[]{:S(2)}, u32[]{:S(2)}) collective-permute-start(f32[256,512]{1,0:T(8,128)} %broadcast_select_fusion.3), channel_id=1, source_target_pairs={{0,16},{32,48},{1,17},{33,49},{2,18},{34,50},{3,19},{35,51},{4,20}... | collective-permute-start | bytes 1572872 | tf_op jit(solution)/shard_map/ppermute | solution.py:17
  386.6 11.2 %collective-permute-start.23 = (f32[256,256]{1,0:T(8,128)S(1)}, f32[256,256]{1,0:T(8,128)}, u32[]{:S(2)}, u32[]{:S(2)}) collective-permute-start(f32[256,256]{1,0:T(8,128)S(1)} %broadcast_select_fusion.14), channel_id=1, source_target_pairs={{0,2},{4,6},{128,130},{132,134},{256,258},{260,262},{384,386},{388... | collective-permute-start | bytes 786440 | tf_op jit(solution)/shard_map/ppermute | solution.py:17
  397.8 29.3 %collective-permute-start.24 = (f32[256,256]{1,0:T(8,128)S(1)}, f32[256,256]{1,0:T(8,128)S(1)}, u32[]{:S(2)}, u32[]{:S(2)}) collective-permute-start(f32[256,256]{1,0:T(8,128)S(1)} %broadcast_select_fusion.10), channel_id=1, source_target_pairs={{0,1},{2,3},{4,5},{6,7},{128,129},{130,131},{132,133},{134,135},{2... | collective-permute-start | bytes 786440 | tf_op jit(solution)/shard_map/ppermute | solution.py:17
  401.1 42.8 %collective-permute-start.28 = (f32[256,512]{1,0:T(8,128)}, f32[256,512]{1,0:T(8,128)}, u32[]{:S(2)}, u32[]{:S(2)}) collective-permute-start(f32[256,512]{1,0:T(8,128)} %broadcast_select_fusion.5), channel_id=1, source_target_pairs={{0,8},{16,24},{32,40},{48,56},{1,9},{17,25},{33,41},{49,57},{2,10}... | collective-permute-start | bytes 1572872 | tf_op jit(solution)/shard_map/ppermute | solution.py:17
  424.9 20.7 %collective-permute-start.22 = (f32[1024,256]{1,0:T(8,128)S(1)}, f32[1024,256]{1,0:T(8,128)}, u32[]{:S(2)}, u32[]{:S(2)}) collective-permute-start(f32[1024,256]{1,0:T(8,128)S(1)} %broadcast_select_fusion.2), channel_id=1, source_target_pairs={{0,64},{128,192},{256,320},{384,448},{1,65},{129,193},{257,321},{3... | collective-permute-start | bytes 3145736 | tf_op jit(solution)/shard_map/ppermute | solution.py:17
  427.2 3.5 collective-permute-start.25
